TPU v7x, 32 devices: a whole 2x2x4 slice. The times are simulated.
32 devices in a mesh: chan: 8 (over y, x, core), filt: 4 (over z).
Axes of the slice: x: 2, y: 2, z: 4, core: 2. Of those that a mesh axis runs over, the one named last changes fastest.
Arguments:
- activations: bfloat16 [2592, 2048], P(None, ('chan', 'filt')), may hold values from -6 to 6
- act_tangent: bfloat16 [2592, 2048], P(None, ('chan', 'filt')), may hold values from -6 to 6
- kernel: bfloat16 [9, 2048, 2048], P(None, 'chan', 'filt'), may hold values from -0.046875 to 0.046875
- kernel_tangent: bfloat16 [9, 2048, 2048], P(None, 'chan', 'filt'), may hold values from -0.046875 to 0.046875
- slope: bfloat16 [2592, 2048], P('chan', 'filt'), may hold values from 0.19921875 to 1.09375
- curvature: bfloat16 [2592, 2048], P('chan', 'filt'), may hold values from 0.29882812 to 3
Outputs:
- input_cotangent: bfloat16 [2592, 2048], P('filt', 'chan')
- kernel_product: float32 [9, 2048, 2048], P(None, 'chan', 'filt')
All inputs are finite; a program needn't handle non-finite values.
Results may differ from a plain program's by a relative error of at most 0.0047.
Values may be sent and summed in bfloat16 or wider, within the bound.
No kernel may reach another device: no remote copies, remote signals or barrier semaphores. Data moves between devices by JAX's collectives and lax.ppermute only.
A program may use at most 192 MiB of HBM per device.

v0:
```python
import functools

import jax
import jax.numpy as jnp
from jax import lax
from jax.experimental import pallas as pl
from jax.experimental.pallas import tpu as pltpu
from jax.sharding import PartitionSpec as P


HH = 12
WW = 12
LANES = 128
STRIPS = 4
DEEP = HH // STRIPS
PAIR = 2
EIGHT = PAIR * STRIPS
PIECE = WW * EIGHT
GROUP = DEEP * PIECE

PARAMS = pltpu.CompilerParams(vmem_limit_bytes=28 << 20)


def windows(flat, flip):
    width = flat.shape[-1]
    image = flat.reshape(-1, HH, WW, width)
    padded = jnp.pad(image, ((0, 0), (1, 1), (1, 1), (0, 0)))
    result = []
    for row_tap in range(3):
        for col_tap in range(3):
            top = 2 - row_tap if flip else row_tap
            left = 2 - col_tap if flip else col_tap
            result.append(padded[:, top : top + HH, left : left + WW, :].reshape(-1, width))
    return result


def weigh(slope, curvature, tangent):
    slope_f = slope.astype(jnp.float32)
    return (slope_f * slope_f * curvature.astype(jnp.float32) * tangent).astype(jnp.bfloat16)


def any_device(activations, act_tangent, kernel, kernel_tangent, slope, curvature):
    acts_block, tans_block = (
        lax.all_gather(activations, "filt", axis=1, tiled=True),
        lax.all_gather(act_tangent, "filt", axis=1, tiled=True),
    )
    acts = windows(acts_block, False)
    tans = windows(tans_block, False)
    pixel_count = acts_block.shape[0]
    partial_value = jnp.zeros((pixel_count, kernel.shape[2]), jnp.float32)
    for tap in range(9):
        partial_value = partial_value + jnp.dot(
            tans[tap], kernel[tap], preferred_element_type=jnp.float32
        )
        partial_value = partial_value + jnp.dot(
            acts[tap], kernel_tangent[tap], preferred_element_type=jnp.float32
        )
    total = lax.psum(partial_value, "chan")
    slope_all, curve_all = (
        lax.all_gather(slope, "chan", axis=0, tiled=True),
        lax.all_gather(curvature, "chan", axis=0, tiled=True),
    )
    weighted = weigh(slope_all, curve_all, total)
    backs = windows(weighted, True)
    cot_part = jnp.zeros((pixel_count, kernel.shape[1]), jnp.float32)
    grads = []
    for tap in range(9):
        cot_part = cot_part + lax.dot_general(
            backs[tap], kernel[tap], (((1,), (1,)), ((), ())), preferred_element_type=jnp.float32
        )
        grads.append(
            lax.dot_general(
                acts[tap], weighted, (((0,), (0,)), ((), ())), preferred_element_type=jnp.float32
            )
        )
    kernel_product = jnp.stack(grads) / jnp.sqrt(jnp.float32(pixel_count))
    cotangent = lax.psum_scatter(cot_part, "filt", scatter_dimension=0, tiled=True).astype(
        jnp.bfloat16
    )
    return (cotangent, kernel_product)


def pieces_of(groups):
    for g, images in enumerate(groups):
        for strip in range(EIGHT):
            image, part = images[strip // STRIPS], strip % STRIPS
            for deep in range(DEEP):
                source = (image * HH + part * DEEP + deep) * WW
                yield g, strip, deep, source, (deep * len(groups) + g) * PIECE + strip


def sort_into(chunks, flat, sorted_, outs, cols):
    for groups, out in zip(chunks, outs):
        for _, _, _, source, target in pieces_of(groups):
            sorted_[pl.ds(target, WW, stride=EIGHT), :] = flat[pl.ds(source, WW), :]
        out[:, cols] = sorted_[pl.ds(0, out.shape[0]), :].astype(out.dtype)


def sort_kernel(chunks, x_ref, *refs):
    outs, (flat, sorted_) = refs[: len(chunks)], refs[len(chunks) :]
    blocks, each = x_ref.shape[0], x_ref.shape[1] // 2
    rows = flat.shape[0] // blocks
    for kind in range(2):
        for n in range(blocks):
            block = x_ref[n, kind * each : (kind + 1) * each, :].astype(jnp.float32)
            flat[n * rows : (n + 1) * rows, :] = block[:rows]
        sort_into(chunks, flat, sorted_, outs, pl.ds(kind * LANES, LANES))


def mix_kernel(chunks, a_ref, t_ref, *refs):
    outs, (flat, sorted_) = refs[: len(chunks)], refs[len(chunks) :]
    both = jnp.concatenate(
        [a_ref[...].astype(jnp.float32), t_ref[...].astype(jnp.float32)], axis=0
    )
    flat[...] = both.T
    sort_into(chunks, flat, sorted_, outs, pl.ds(0, LANES))


def sort_call(kernel, chunks, given, pixels, width):
    rows = [len(groups) * GROUP for groups in chunks]
    return pl.pallas_call(
        functools.partial(kernel, chunks),
        out_shape=[jax.ShapeDtypeStruct((r, width), given[0].dtype) for r in rows],
        scratch_shapes=[
            pltpu.VMEM((pixels, LANES), jnp.float32),
            pltpu.VMEM((max(rows), LANES), jnp.float32),
        ],
        compiler_params=PARAMS,
    )(*given)


def copy_all(copies):
    for copy in copies:
        copy.start()
    for copy in copies:
        copy.wait()


def build(x_ref, views, groups):
    width = x_ref.shape[1]
    strip = lax.broadcasted_iota(jnp.int32, (PIECE, width), 0) % STRIPS

    def put(at, block):
        at = pl.multiple_of(at, PIECE)
        none = jnp.zeros((EIGHT, width), jnp.float32)
        views[1, pl.ds(at, PIECE), :] = block.astype(jnp.bfloat16)
        before = jnp.concatenate([none, block[: PIECE - EIGHT]], axis=0)
        views[0, pl.ds(at, PIECE), :] = before.astype(jnp.bfloat16)
        after = jnp.concatenate([block[EIGHT:], none], axis=0)
        views[2, pl.ds(at, PIECE), :] = after.astype(jnp.bfloat16)

    def load(at):
        return x_ref[pl.ds(pl.multiple_of(at, PIECE), PIECE), :].astype(jnp.float32)

    def turn(block, by):
        return pltpu.roll(block.reshape(WW, EIGHT, width), by, 1).reshape(PIECE, width)

    @pl.loop(0, DEEP * groups)
    def _(n):
        put((groups + n) * PIECE, load(n * PIECE))

    @pl.loop(0, groups)
    def _(g):
        above = turn(load(((DEEP - 1) * groups + g) * PIECE), 1)
        put(g * PIECE, jnp.where(strip == 0, 0.0, above))
        below = turn(load(g * PIECE), EIGHT - 1)
        put(((DEEP + 1) * groups + g) * PIECE, jnp.where(strip == STRIPS - 1, 0.0, below))


def tap_rows(views, groups, row, col):
    start = row * (groups * PIECE)
    if not isinstance(row, int):
        start = pl.multiple_of(start, PIECE)
    return views[col, pl.ds(start, groups * GROUP), :]


def views_shape(groups, width):
    return pltpu.VMEM((3, (DEEP + 2) * groups * PIECE, width), jnp.bfloat16)


HALF, CHIP, PLACE, SHARDS = 0, 1, 2, 3


def tangent_kernel(groups, sources, slots, more, last, meta, *refs):
    count = len(slots)
    given = 1 + max(n for order in sources for n in order)
    shards = refs[:given]
    v_ref, w_ref = refs[given : given + 2]
    before = refs[given + 2] if more else None
    refs = refs[given + 2 + more :]
    if last:
        send_ref, keep_ref, xt_ref, x, xt, views, sem, *refs = refs
        acc, *refs = refs
    else:
        acc, xt_ref, x, xt, views, sem, *refs = refs
    away = pltpu.make_async_copy(xt, xt_ref, sem.at[count + 2])
    own = v_ref.shape[1] // len(sources)
    step = pl.program_id(0)

    @pl.when(step == 0)
    def _():
        fetch = []
        if count == 1:
            at = pl.ds(pl.multiple_of(meta[SHARDS + slots[0]] * own, own), own)
            for n, ref in enumerate((v_ref, w_ref)):
                to = refs[0].at[:, pl.ds(n * own, own), :]
                fetch.append(pltpu.make_async_copy(ref.at[:, at, :], to, sem.at[count + n]))
        for copy in fetch:
            copy.start()
        for z, order in enumerate(sources):

            @pl.when(meta[PLACE] == z)
            def _():
                copy_all(
                    [
                        pltpu.make_async_copy(
                            shards[n],
                            x.at[:, pl.ds(i * LANES, LANES)],
                            sem.at[i],
                        )
                        for i, n in enumerate(order)
                    ]
                )

        build(x, views, groups)
        for i in range(count):
            turned = x[:, i * LANES : (i + 1) * LANES].astype(jnp.float32).T
            xt[i * own : (i + 1) * own, :] = turned[:own].astype(jnp.bfloat16)
        away.start()
        for copy in fetch:
            copy.wait()

    if count == 1:
        lhs = [tap_rows(views, groups, row, col) for row in range(3) for col in range(3)]
        rhs = refs[0][...].reshape(9 * LANES, acc.shape[1])
    else:
        lhs, rhs = [], []
        for col in range(3):
            lhs.append(tap_rows(views, groups, step, col))
            for slot in slots:
                at = pl.ds(pl.multiple_of(meta[SHARDS + slot] * own, own), own)
                rhs += [v_ref[col, at, :], w_ref[col, at, :]]
        rhs = jnp.concatenate(rhs, axis=0)
    value = jnp.dot(jnp.concatenate(lhs, axis=1), rhs, preferred_element_type=jnp.float32)
    pl.when(step == pl.num_programs(0) - 1)(away.wait)
    if count == 1:
        acc[...] = before[...] + value if more else value
    elif more:
        acc[...] = value + jnp.where(step == 0, before[...], acc[...])
    else:
        acc[...] = jnp.where(step == 0, value, acc[...] + value)
    if last:
        pl.when(step == pl.num_programs(0) - 1)(
            functools.partial(halves, meta, acc, send_ref, keep_ref)
        )


def halves(meta, acc, send_ref, keep_ref):
    half, n = meta[HALF], acc.shape[0] // 2
    mine = pl.ds(pl.multiple_of(half * n, n), n)
    other = pl.ds(pl.multiple_of((1 - half) * n, n), n)
    send_ref[...] = acc[other, :].astype(jnp.bfloat16)
    keep_ref[...] = acc[mine, :]


def tangent(meta, shards, sources, slots, v, w, groups, before, last):
    more = before is not None
    rows = groups * GROUP
    channels, filters = w.shape[1:]
    count = len(slots)
    own = channels // len(sources)
    whole_block = pl.BlockSpec(memory_space=pl.ANY)
    row_block = pl.BlockSpec((3, channels, filters), lambda t, m: (t, 0, 0))

    def whole(*shape):
        return pl.BlockSpec(shape, lambda t, m: (0,) * len(shape))

    if last:
        outs = [(rows // 2, filters, jnp.bfloat16), (rows // 2, filters, jnp.float32)]
    else:
        outs = [(rows, filters, jnp.float32)]
    return pl.pallas_call(
        functools.partial(tangent_kernel, groups, sources, slots, more, last),
        grid_spec=pltpu.PrefetchScalarGridSpec(
            num_scalar_prefetch=1,
            grid=(1 if count == 1 else 3,),
            in_specs=[whole_block] * len(shards)
            + [whole_block if count == 1 else row_block] * 2
            + ([whole(rows, filters)] if more else []),
            out_specs=[whole(*o[:2]) for o in outs] + [pl.BlockSpec(memory_space=pltpu.HBM)],
            scratch_shapes=[
                pltpu.VMEM((rows, count * LANES), jnp.bfloat16),
                pltpu.VMEM((count * own, rows), jnp.bfloat16),
                views_shape(groups, count * LANES),
                pltpu.SemaphoreType.DMA((count + 3,)),
            ]
            + ([pltpu.VMEM((rows, filters), jnp.float32)] if last else [])
            + ([pltpu.VMEM((9, LANES, filters), jnp.bfloat16)] if count == 1 else []),
        ),
        out_shape=[jax.ShapeDtypeStruct(o[:2], o[2]) for o in outs]
        + [pltpu.HBM((count * own, rows), jnp.bfloat16)],
        cost_estimate=pl.CostEstimate(
            flops=18 * rows * count * LANES * filters,
            bytes_accessed=4 * w.size,
            transcendentals=0,
        ),
        name="tangent",
        compiler_params=PARAMS,
    )(meta, *shards, v, w, *([before] if more else []))


def split_kernel(meta, keep_ref, got_ref, mine_ref, *parts):
    for m in range(1 + len(parts)):
        at = pl.multiple_of((meta[CHIP] ^ m) * LANES, LANES)
        total = keep_ref[:, pl.ds(at, LANES)] + got_ref[:, pl.ds(at, LANES)].astype(jnp.float32)
        if m:
            parts[m - 1][...] = total.astype(jnp.bfloat16)
        else:
            mine_ref[...] = total


def split(meta, keep, got):
    rows, filters = keep.shape
    block = pl.BlockSpec((rows, filters), lambda t, m: (0, 0))
    out = pl.BlockSpec((rows, LANES), lambda t, m: (0, 0))
    kinds = [jnp.float32] + [jnp.bfloat16] * (filters // LANES - 1)
    return pl.pallas_call(
        split_kernel,
        grid_spec=pltpu.PrefetchScalarGridSpec(
            num_scalar_prefetch=1, grid=(1,), in_specs=[block] * 2, out_specs=[out] * len(kinds)
        ),
        out_shape=[jax.ShapeDtypeStruct((rows, LANES), kind) for kind in kinds],
        cost_estimate=pl.CostEstimate(
            flops=rows * filters, bytes_accessed=8 * keep.size, transcendentals=0
        ),
        name="split",
        compiler_params=PARAMS,
    )(meta, keep, got)


def gather_parts(meta, parts, x, sem):
    blocks, rows = len(parts) // 2, x.shape[0] // 2
    copies = []
    for n, part in enumerate(parts):
        half = meta[HALF] if n < blocks else 1 - meta[HALF]
        at = pl.multiple_of(half * rows, rows)
        lane = pl.multiple_of((meta[CHIP] ^ (n % blocks)) * LANES, LANES)
        to = x.at[pl.ds(at, rows), pl.ds(lane, LANES)]
        copies.append(pltpu.make_async_copy(part, to, sem.at[n]))
    copy_all(copies)


def cotangent_kernel(groups, places, meta, *refs):
    w_parts, (k_ref, out_ref, rows_ref, x, views, sem, acc, flat) = refs[:-8], refs[-8:]
    step = pl.program_id(0)
    keep = pltpu.make_async_copy(x, rows_ref, sem.at[len(w_parts)])

    @pl.when(step == 0)
    def _():
        gather_parts(meta, w_parts, x, sem)
        keep.start()
        build(x, views, len(groups))

    value = lax.dot_general(
        jnp.concatenate(
            [tap_rows(views, len(groups), 2 - step, 2 - col) for col in range(3)], axis=1
        ),
        jnp.concatenate([k_ref[col] for col in range(3)], axis=1),
        (((1,), (1,)), ((), ())),
        preferred_element_type=jnp.float32,
    )
    for n in range(acc.shape[0]):
        column = value[:, n * LANES : (n + 1) * LANES]
        acc[n] = jnp.where(step == 0, column, acc[n] + column)

    @pl.when(step == 2)
    def _():
        keep.wait()
        for n in range(acc.shape[0]):
            for g, strip, deep, _, row in pieces_of(groups):
                target = places(g, strip) + deep * WW
                flat[pl.ds(target, WW), :] = acc[n, pl.ds(row, WW, stride=EIGHT), :]
            out_ref[:, n * LANES : (n + 1) * LANES] = flat[...].astype(jnp.bfloat16)


def cotangent_part(meta, w_parts, groups, kernel, places):
    channels, filters = kernel.shape[1:]
    rows = 2 * w_parts[0].shape[0]
    return pl.pallas_call(
        functools.partial(cotangent_kernel, groups, places),
        grid_spec=pltpu.PrefetchScalarGridSpec(
            num_scalar_prefetch=1,
            grid=(3,),
            in_specs=[pl.BlockSpec(memory_space=pl.ANY)] * len(w_parts)
            + [pl.BlockSpec((3, channels, filters), lambda t, m: (t, 0, 0))],
            out_specs=[
                pl.BlockSpec((rows, channels), lambda t, m: (0, 0)),
                pl.BlockSpec(memory_space=pltpu.HBM),
            ],
            scratch_shapes=[
                pltpu.VMEM((rows, filters), jnp.bfloat16),
                views_shape(len(groups), filters),
                pltpu.SemaphoreType.DMA((len(w_parts) + 1,)),
                pltpu.VMEM((channels // LANES, rows, LANES), jnp.float32),
                pltpu.VMEM((rows, LANES), jnp.float32),
            ],
        ),
        out_shape=[
            jax.ShapeDtypeStruct((rows, channels), jnp.bfloat16),
            pltpu.HBM((rows, filters), jnp.bfloat16),
        ],
        cost_estimate=pl.CostEstimate(
            flops=18 * rows * channels * filters,
            bytes_accessed=18 * channels * filters,
            transcendentals=0,
        ),
        name="cotangent",
        compiler_params=PARAMS,
    )(meta, *w_parts, kernel)


def product_kernel(own, counts, sizes, scale, meta, *refs):
    chunks = len(counts)
    scratch = refs[-2 * chunks :]
    given, out_ref = refs[: -1 - 2 * chunks], refs[-1 - 2 * chunks]
    ends = [sum(sizes[: n + 1]) for n in range(chunks)]
    tap = pl.program_id(0)

    @pl.when(tap == 0)
    def _():
        for n, count in enumerate(counts):
            w_ref, *xts = given[ends[n] - sizes[n] : ends[n]]
            views, xt = scratch[2 * n : 2 * n + 2]
            build(w_ref, views, count)
            slot = 0
            for ref in xts:
                for row in range(0, ref.shape[0], own):
                    at = pl.multiple_of(meta[SHARDS + slot] * own, own)
                    xt[pl.ds(at, own), :] = ref[pl.ds(row, own), :]
                    slot += 1

    value = None
    for n, count in enumerate(counts):
        views, xt = scratch[2 * n : 2 * n + 2]
        term = jnp.dot(
            xt[...], tap_rows(views, count, 2 - tap // 3, 2 - lax.rem(tap, 3)), preferred_element_type=jnp.float32
        )
        value = term if value is None else value + term
    out_ref[0] = value * scale


def product_of(meta, chunks, counts, scale, channels, own):
    given = [array for chunk in chunks for array in chunk]
    total = sum(chunk[0].shape[0] for chunk in chunks)
    filters = chunks[0][0].shape[1]
    scratch = []
    for (w, *_), count in zip(chunks, counts):
        scratch += [views_shape(count, filters), pltpu.VMEM((channels, w.shape[0]), jnp.bfloat16)]
    return pl.pallas_call(
        functools.partial(product_kernel, own, counts, [len(chunk) for chunk in chunks], scale),
        grid_spec=pltpu.PrefetchScalarGridSpec(
            num_scalar_prefetch=1,
            grid=(9,),
            in_specs=[pl.BlockSpec(array.shape, lambda t, m: (0, 0)) for array in given],
            out_specs=pl.BlockSpec((1, channels, filters), lambda t, m: (t, 0, 0)),
            scratch_shapes=scratch,
        ),
        out_shape=jax.ShapeDtypeStruct((9, channels, filters), jnp.float32),
        cost_estimate=pl.CostEstimate(
            flops=18 * total * channels * filters,
            bytes_accessed=36 * channels * filters,
            transcendentals=0,
        ),
        name="product",
        compiler_params=PARAMS,
    )(meta, *given)


def pack_kernel(s_ref, c_ref, out_ref):
    rows = s_ref.shape[0]
    each = out_ref.shape[1] // 2
    for n in range(out_ref.shape[0]):
        cols = pl.ds(n // 2 * LANES, LANES)
        for kind, ref in enumerate((s_ref, c_ref)):
            out_ref[n, kind * each : kind * each + rows, :] = ref[:, cols]
            rest = jnp.zeros((each - rows, LANES), out_ref.dtype)
            out_ref[n, kind * each + rows : (kind + 1) * each, :] = rest


def pack(slope, curvature):
    rows, filters = slope.shape
    each = -(-rows // 16) * 16
    return pl.pallas_call(
        pack_kernel,
        out_shape=jax.ShapeDtypeStruct((2 * filters // LANES, 2 * each, LANES), slope.dtype),
        name="pack",
        compiler_params=PARAMS,
    )(slope, curvature)


def block_program(activations, act_tangent, kernel, kernel_tangent, slope, curvature):
    z, me = lax.axis_index("filt"), lax.axis_index("chan")
    depth, across = lax.axis_size("filt"), lax.axis_size("chan")
    half, chips = lax.rem(me, 2), across // 2
    pixels, own = activations.shape
    channels = kernel.shape[1]

    first, second, middle = [], [], []
    per = 2 * (pixels // (HH * WW)) // depth
    for a in range(0, depth, 2):
        at = a // 2 * per
        first += [(at, at + 1), (at + per - 2, at + per - 1)]
        second += [(at + 2, at + 3), (at + per - 4, at + per - 3)]
        middle.append(at + 4)
    second.append(tuple(middle))
    chunks = [second, first]

    orders, owners = [], []
    for place in range(depth):
        order, owner = [(0, 0)], [place]
        for step in range(1, depth):
            for link in range(2):
                shard = place + step if place % 2 == link else place - step
                if 0 <= shard < depth:
                    order.append((step, link))
                    owner.append(shard)
        orders.append(order)
        owners.append(owner)
    table = [
        [n % 2, n // 2, place] + owners[place]
        for place in range(depth)
        for n in range(across)
    ]
    meta = lax.dynamic_index_in_dim(
        jnp.asarray(table, jnp.int32), z * across + me, 0, keepdims=False
    )

    mixed = sort_call(mix_kernel, chunks, [activations.T, act_tangent.T], pixels, 2 * own)

    packed = pack(slope, curvature)
    packed = lax.all_to_all(packed, "chan", 0, 0, tiled=True)
    factors = sort_call(sort_kernel, chunks, [packed], pixels, 2 * LANES)

    def gathered(x):
        got = {(0, 0): x}
        last = [x, x]
        for step in range(1, depth):
            now = [None, None]
            for link in range(2):
                pairs = []
                for i in range(link, depth - 1, 2):
                    pairs += [(i, i + 1)] * (i >= step - 1) + [(i + 1, i)] * (i + 1 <= depth - step)
                if pairs:
                    now[link] = lax.ppermute(last[1 - link], "filt", pairs)
                    got[step, link] = now[link]
            last = now
        return got

    def swap(x, bit):
        return lax.ppermute(x, "chan", [(i, i ^ bit) for i in range(across)])

    def some(slots, c):
        names = sorted({order[slot] for order in orders for slot in slots})
        sources = [[names.index(order[slot]) for slot in slots] for order in orders]
        return [got[c][name] for name in names], sources

    def tangents(c):
        stages = [[0, 1], [2], [3]] if c == 0 else [[0, 1], [2, 3]]
        before, xts = None, []
        for n, slots in enumerate(stages):
            shards, sources = some(slots, c)
            *sums, xt = tangent(
                meta,
                shards,
                sources,
                slots,
                kernel_tangent,
                kernel,
                len(chunks[c]),
                before,
                n == len(stages) - 1,
            )
            before = sums[0]
            xts.append(xt)
        return sums, xts

    def exchange(send, keep):
        got = swap(send, 1)
        mine, *parts = split(meta, keep, got)
        for m, part in enumerate(parts):
            mine = mine + swap(part, 2 * (m + 1)).astype(jnp.float32)
        return mine

    def weighted(mine, factor):
        rows = mine.shape[0]
        factor = lax.dynamic_slice_in_dim(factor, half * rows, rows, axis=0)
        w = weigh(factor[:, :LANES], factor[:, LANES:], mine)
        parts = [w] + [swap(w, 2 * m) for m in range(1, chips)]
        return parts + [swap(part, 1) for part in parts]

    strip_rows = GROUP // EIGHT
    share = len(second) * GROUP // depth

    def place_first(g, strip):
        return g * GROUP + strip * strip_rows

    def place_second(g, strip):
        if g < depth:
            return g * share + strip * strip_rows
        place, rest = divmod(strip, EIGHT // depth)
        return place * share + GROUP + rest * strip_rows

    def spread(part):
        part = lax.all_to_all(
            part.reshape(depth, -1, channels), "filt", 0, 0, tiled=True
        ).astype(jnp.float32)
        total = part[0]
        for j in range(1, depth):
            total = total + part[j]
        return total.astype(jnp.bfloat16)

    got = [gathered(x) for x in mixed]
    sums, xts = zip(*[tangents(c) for c in range(2)])
    mine = [exchange(*sums[c]) for c in range(2)]
    w = [weighted(mine[c], factors[c]) for c in range(2)]
    cots, whole = [], []
    for c, place in enumerate((place_second, place_first)):
        part, rows = cotangent_part(meta, w[c], chunks[c], kernel, place)
        cots.append(spread(part))
        whole.append(rows)
    scale = float(1.0 / (float(pixels) ** 0.5))
    product = product_of(
        meta,
        [(whole[c], *xts[c]) for c in range(2)],
        [len(groups) for groups in chunks],
        scale,
        channels,
        own,
    )
    inner, outer = cots
    main, edge = inner[:GROUP], inner[GROUP:]
    result = jnp.where(
        lax.rem(z, 2) == 0,
        jnp.concatenate([outer, main, edge], axis=0),
        jnp.concatenate([edge, main, outer], axis=0),
    )
    return (result, product)


def block_device(*args):
    return block_program(*args)


def fits(mesh, pixels, channels, filters):
    depth, across = mesh.shape["filt"], mesh.shape["chan"]
    images = pixels // (HH * WW)
    return (
        depth == 2 * PAIR
        and 2 * images == 9 * depth
        and across == 8
        and 2 * channels == LANES * across * depth
        and filters == LANES * (across // 2) * depth
    )


def solution(mesh):
    in_specs = (
        P(None, ("chan", "filt")),
        P(None, ("chan", "filt")),
        P(None, "chan", "filt"),
        P(None, "chan", "filt"),
        P("chan", "filt"),
        P("chan", "filt"),
    )

    def program(*args):
        pixels, channels = args[0].shape
        body = block_device if fits(mesh, pixels, channels, args[2].shape[2]) else any_device
        return jax.shard_map(
            body,
            mesh=mesh,
            in_specs=in_specs,
            out_specs=(P("filt", "chan"), P(None, "chan", "filt")),
            check_vma=False,
        )(*args)

    return program
```

profile of v0, /device:TPU:0, one launch (start us, length us, event | category | flops | bytes accessed | tf_op | source)
XLA Modules:
  0.0 162.3 jit_solution(1778186128332882476)
XLA Ops:
  3.8 3.1 %collective-permute-start.2 = (bf16[1152,128]{1,0:T(8,128)(2,1)}, bf16[1152,128]{1,0:T(8,128)(2,1)}, u32[]{:S(2)}, u32[]{:S(2)}) collective-permute-start(bf16[1152,128]{1,0:T(8,128)(2,1)} %get-tuple-element.31.refs_0_), channel_id=1, source_target_pairs={{0,1},{1,0},{2,3},{3,2},{4,5},{5,4},{6,7},{7,6},{8,9},{9,8},{10,11... | collective-permute-start | bytes 884744 | tf_op jit(solution)/shard_map/ppermute | solution.py:554
  8.2 6.8 %collective-permute-done.2.refs_1_ = bf16[1152,128]{1,0:T(8,128)(2,1)} collective-permute-done((bf16[1152,128]{1,0:T(8,128)(2,1)}, bf16[1152,128]{1,0:T(8,128)(2,1)}, u32[]{:S(2)}, u32[]{:S(2)}) %collective-permute-start.2) | collective-permute-done | bytes 294944 | tf_op jit(solution)/shard_map/ppermute | solution.py:554
  17.0 5.0 %collective-permute-done.16.refs_1_ = bf16[1440,128]{1,0:T(8,128)(2,1)} collective-permute-done((bf16[1440,128]{1,0:T(8,128)(2,1)S(1)}, bf16[1440,128]{1,0:T(8,128)(2,1)}, u32[]{:S(2)}, u32[]{:S(2)}) %collective-permute-start.16) | collective-permute-done | bytes 368672 | tf_op jit(solution)/shard_map/ppermute | solution.py:554
  26.0 4.4 %all-to-all-start = ((bf16[8,672,128]{2,1,0:T(8,128)(2,1)}), bf16[8,672,128]{2,1,0:T(8,128)(2,1)}, u32[]{:S(2)}, u32[]{:S(2)}) async-start(bf16[8,672,128]{2,1,0:T(8,128)(2,1)} %copy-done.4), calls=%async_computation | async-start | bytes 2752512 | tf_op jit(solution)/shard_map/all_to_all | solution.py:541
  33.7 1.7 %copy-done.1 = bf16[9,256,512]{2,1,0:T(8,128)(2,1)S(1)} copy-done((bf16[9,256,512]{2,1,0:T(8,128)(2,1)S(1)}, bf16[9,256,512]{2,1,0:T(8,128)(2,1)}, u32[]{:S(2)}) %copy-start.1) | copy-done | bytes 2359320
  35.4 6.3 %tangent.5 = (f32[1152,512]{1,0:T(8,128)S(1)}, bf16[128,1152]{1,0:T(8,128)(2,1)}) custom-call(s32[7]{0:T(128)S(1)} %fusion.3.meta, bf16[1152,128]{1,0:T(8,128)(2,1)} %get-tuple-element.31.refs_0_, bf16[1152,128]{1,0:T(8,128)(2,1)} %collective-permute-done.2.refs_1_, bf16[9,256,512]{2,1,0:T(8,128)(2,1)S(1)} %copy-done, bf16[9,256,512]{2,1,0:T(8,128)(2,1)S(1)} %copy-done.1), custom_call_target="tpu_custom_call" | custom-call | flops 2717908992 | bytes 4718592 | tf_op jit(solution)/shard_map/tangent/pallas_call | solution.py:282
  44.3 6.3 %collective-permute-done.4.refs_3_ = bf16[1152,128]{1,0:T(8,128)(2,1)S(1)} collective-permute-done((bf16[1152,128]{1,0:T(8,128)(2,1)}, bf16[1152,128]{1,0:T(8,128)(2,1)S(1)}, u32[]{:S(2)}, u32[]{:S(2)}) %collective-permute-start.4) | collective-permute-done | bytes 294944 | tf_op jit(solution)/shard_map/ppermute | solution.py:554
  50.6 5.6 %tangent.6 = (bf16[576,512]{1,0:T(8,128)(2,1)S(1)}, f32[576,512]{1,0:T(8,128)S(1)}, bf16[128,1152]{1,0:T(8,128)(2,1)}) custom-call(s32[7]{0:T(128)S(1)} %fusion.3.meta, bf16[1152,128]{1,0:T(8,128)(2,1)} %collective-permute-done.refs_0_, bf16[1152,128]{1,0:T(8,128)(2,1)S(1)} %collective-permute-done.1.refs_1_, ...), custom_call_target="tpu_custom_call" | custom-call | flops 2717908992 | bytes 4718592 | tf_op jit(solution)/shard_map/tangent/pallas_call | solution.py:282
  56.3 7.4 %tangent.7 = (f32[1440,512]{1,0:T(8,128)S(1)}, bf16[128,1440]{1,0:T(8,128)(2,1)}) custom-call(s32[7]{0:T(128)S(1)} %fusion.3.meta, bf16[1440,128]{1,0:T(8,128)(2,1)S(1)} %get-tuple-element.41.refs_0_, bf16[1440,128]{1,0:T(8,128)(2,1)} %collective-permute-done.16.refs_1_, bf16[9,256,512]{2,1,0:T(8,128)(2,1)S(1)} %copy-done, bf16[9,256,512]{2,1,0:T(8,128)(2,1)S(1)} %copy-done.2), custom_call_target="tpu_custom_call" | custom-call | flops 3397386240 | bytes 4718592 | tf_op jit(solution)/shard_map/tangent/pallas_call | solution.py:282
  63.6 3.7 %tangent.8 = (f32[1440,512]{1,0:T(8,128)S(1)}, bf16[64,1440]{1,0:T(8,128)(2,1)}) custom-call(s32[7]{0:T(128)S(1)} %fusion.3.meta, bf16[1440,128]{1,0:T(8,128)(2,1)S(1)} %collective-permute-done.19.refs_0_, bf16[1440,128]{1,0:T(8,128)(2,1)S(1)} %collective-permute-done.20.refs_1_, bf16[9,256,512]{2,1,0:T(8,128)(2,1)S(1)} %copy-done, ...), custom_call_target="tpu_custom_call" | custom-call | flops 1698693120 | bytes 4718592 | tf_op jit(solution)/shard_map/tangent/pallas_call | solution.py:282
  67.4 5.0 %tangent.9 = (bf16[720,512]{1,0:T(8,128)(2,1)}, f32[720,512]{1,0:T(8,128)S(1)}, bf16[64,1440]{1,0:T(8,128)(2,1)}) custom-call(s32[7]{0:T(128)S(1)} %fusion.3.meta, bf16[1440,128]{1,0:T(8,128)(2,1)S(1)} %collective-permute-done.17.refs_0_, bf16[1440,128]{1,0:T(8,128)(2,1)S(1)} %collective-permute-done.18.refs_1_, bf16[9,256,512]{2,1,0:T(8,128)(2,1)S(1)} %copy-done, ...), custom_call_target="tpu_custom_call" | custom-call | flops 1698693120 | bytes 4718592 | tf_op jit(solution)/shard_map/tangent/pallas_call | solution.py:282
  74.8 2.9 %collective-permute-start.8 = (bf16[576,128]{1,0:T(8,128)(2,1)S(1)}, bf16[576,128]{1,0:T(8,128)(2,1)S(1)}, u32[]{:S(2)}, u32[]{:S(2)}) collective-permute-start(bf16[576,128]{1,0:T(8,128)(2,1)S(1)} %get-tuple-element.38), channel_id=1, source_target_pairs={{0,24},{4,28},{8,16},{12,20},{16,8},{20,12},{24,0},{28,4},{1,25},{... | collective-permute-start | bytes 442376 | tf_op jit(solution)/shard_map/ppermute | solution.py:560
  78.3 2.2 %shard_map.86 = (bf16[1440,256]{1,0:T(8,128)(2,1)S(1)}, bf16[1152,256]{1,0:T(8,128)(2,1)S(1)}) custom-call(bf16[8,672,128]{2,1,0:T(8,128)(2,1)} %all-to-all-done.x_ref), custom_call_target="tpu_custom_call" | custom-call | tf_op jit(solution)/shard_map/pallas_call | solution.py:121
  80.5 1.7 %collective-permute-done.8 = bf16[576,128]{1,0:T(8,128)(2,1)S(1)} collective-permute-done((bf16[576,128]{1,0:T(8,128)(2,1)S(1)}, bf16[576,128]{1,0:T(8,128)(2,1)S(1)}, u32[]{:S(2)}, u32[]{:S(2)}) %collective-permute-start.8) | collective-permute-done | bytes 147488 | tf_op jit(solution)/shard_map/ppermute | solution.py:560
  82.2 2.6 %collective-permute-done.7 = bf16[576,128]{1,0:T(8,128)(2,1)S(1)} collective-permute-done((bf16[576,128]{1,0:T(8,128)(2,1)S(1)}, bf16[576,128]{1,0:T(8,128)(2,1)S(1)}, u32[]{:S(2)}, u32[]{:S(2)}) %collective-permute-start.7) | collective-permute-done | bytes 147488 | tf_op jit(solution)/shard_map/ppermute | solution.py:560
  85.8 1.9 %multiply_convert_fusion.1.refs_0_ = bf16[576,128]{1,0:T(8,128)(2,1)} fusion(bf16[576,128]{1,0:T(8,128)(2,1)S(1)} %collective-permute-done.8, bf16[576,128]{1,0:T(8,128)(2,1)} %copy-done.19, f32[576,128]{1,0:T(8,128)S(1)} %get-tuple-element.35, bf16[576,128]{1,0:T(8,128)(2,1)} %copy-done.20, bf16[1152,256]{1,0:T(8,128)(2,1)S(1)} %get-tuple-element.30, ...), kind=kLoop, calls=%fused_computation.10 | loop fusion | flops 884736 | bytes 1179656 | tf_op jit(solution)/shard_map/convert_element_type | solution.py:39
  87.7 1.5 collective-permute-start.9
  91.2 2.9 %collective-permute-done.9.refs_1_ = bf16[576,128]{1,0:T(8,128)(2,1)} collective-permute-done((bf16[576,128]{1,0:T(8,128)(2,1)}, bf16[576,128]{1,0:T(8,128)(2,1)}, u32[]{:S(2)}, u32[]{:S(2)}) %collective-permute-start.9) | collective-permute-done | bytes 147488 | tf_op jit(solution)/shard_map/ppermute | solution.py:560
  94.1 4.0 %collective-permute-done.10.refs_2_ = bf16[576,128]{1,0:T(8,128)(2,1)} collective-permute-done((bf16[576,128]{1,0:T(8,128)(2,1)}, bf16[576,128]{1,0:T(8,128)(2,1)}, u32[]{:S(2)}, u32[]{:S(2)}) %collective-permute-start.10) | collective-permute-done | bytes 147488 | tf_op jit(solution)/shard_map/ppermute | solution.py:560
  100.1 1.5 split.3
  101.6 1.5 collective-permute-start.24
  103.4 1.7 %collective-permute-start.22 = (bf16[720,128]{1,0:T(8,128)(2,1)}, bf16[720,128]{1,0:T(8,128)(2,1)}, u32[]{:S(2)}, u32[]{:S(2)}) collective-permute-start(bf16[720,128]{1,0:T(8,128)(2,1)} %get-tuple-element.47), channel_id=1, source_target_pairs={{0,8},{4,12},{8,0},{12,4},{16,24},{20,28},{24,16},{28,20},{1,9},{5... | collective-permute-start | bytes 552968 | tf_op jit(solution)/shard_map/ppermute | solution.py:560
  105.1 7.1 %cotangent.2 = (bf16[1152,256]{1,0:T(8,128)(2,1)}, bf16[1152,512]{1,0:T(8,128)(2,1)}) custom-call(s32[7]{0:T(128)S(1)} %fusion.3.meta, bf16[576,128]{1,0:T(8,128)(2,1)} %multiply_convert_fusion.1.refs_0_, bf16[576,128]{1,0:T(8,128)(2,1)} %collective-permute-done.9.refs_1_, bf16[576,128]{1,0:T(8,128)(2,1)} %collective-permute-done.10.refs_2_, ...), custom_call_target="tpu_custom_call" | custom-call | flops 2717908992 | bytes 2359296 | tf_op jit(solution)/shard_map/cotangent/pallas_call | solution.py:389
  112.2 4.2 %all-to-all-start.1 = ((bf16[4,288,256]{2,1,0:T(8,128)(2,1)}), bf16[4,288,256]{2,1,0:T(8,128)(2,1)}, u32[]{:S(2)}, u32[]{:S(2)}) async-start(bf16[4,288,256]{2,1,0:T(8,128)(2,1)} %bitcast.3), calls=%async_computation.1 | async-start | bytes 1179648 | tf_op jit(solution)/shard_map/all_to_all | solution.py:614
  118.3 1.7 %collective-permute-start.26 = (bf16[720,128]{1,0:T(8,128)(2,1)S(1)}, bf16[720,128]{1,0:T(8,128)(2,1)S(1)}, u32[]{:S(2)}, u32[]{:S(2)}) collective-permute-start(bf16[720,128]{1,0:T(8,128)(2,1)S(1)} %multiply_convert_fusion.refs_0_), channel_id=1, source_target_pairs={{0,16},{4,20},{8,24},{12,28},{16,0},{20,4},{24,8},{28,12},{1,17},{... | collective-permute-start | bytes 552968 | tf_op jit(solution)/shard_map/ppermute | solution.py:560
  120.0 1.4 collective-permute-start.27
  121.4 4.0 %collective-permute-done.25.refs_1_ = bf16[720,128]{1,0:T(8,128)(2,1)S(1)} collective-permute-done((bf16[720,128]{1,0:T(8,128)(2,1)S(1)}, bf16[720,128]{1,0:T(8,128)(2,1)S(1)}, u32[]{:S(2)}, u32[]{:S(2)}) %collective-permute-start.25) | collective-permute-done | bytes 184352 | tf_op jit(solution)/shard_map/ppermute | solution.py:560
  125.4 2.3 %collective-permute-done.26.refs_2_ = bf16[720,128]{1,0:T(8,128)(2,1)S(1)} collective-permute-done((bf16[720,128]{1,0:T(8,128)(2,1)S(1)}, bf16[720,128]{1,0:T(8,128)(2,1)S(1)}, u32[]{:S(2)}, u32[]{:S(2)}) %collective-permute-start.26) | collective-permute-done | bytes 184352 | tf_op jit(solution)/shard_map/ppermute | solution.py:560
  129.4 7.0 %cotangent.3 = (bf16[1440,256]{1,0:T(8,128)(2,1)}, bf16[1440,512]{1,0:T(8,128)(2,1)}) custom-call(s32[7]{0:T(128)S(1)} %fusion.3.meta, bf16[720,128]{1,0:T(8,128)(2,1)S(1)} %multiply_convert_fusion.refs_0_, bf16[720,128]{1,0:T(8,128)(2,1)S(1)} %collective-permute-done.25.refs_1_, bf16[720,128]{1,0:T(8,128)(2,1)S(1)} %collective-permute-done.26.refs_2_, ...), custom_call_target="tpu_custom_call" | custom-call | flops 3397386240 | bytes 2359296 | tf_op jit(solution)/shard_map/cotangent/pallas_call | solution.py:389
  136.5 5.2 %all-to-all-start.2 = ((bf16[4,360,256]{2,1,0:T(8,128)(2,1)}), bf16[4,360,256]{2,1,0:T(8,128)(2,1)S(1)}, u32[]{:S(2)}, u32[]{:S(2)}) async-start(bf16[4,360,256]{2,1,0:T(8,128)(2,1)} %bitcast.5), calls=%async_computation.2 | async-start | bytes 1474560 | tf_op jit(solution)/shard_map/all_to_all | solution.py:614
  144.3 11.2 %product.1 = f32[9,256,512]{2,1,0:T(8,128)} custom-call(s32[7]{0:T(128)S(1)} %fusion.3.meta, bf16[1440,512]{1,0:T(8,128)(2,1)S(1)} %copy-done.16, bf16[128,1440]{1,0:T(8,128)(2,1)S(1)} %copy-done.18, bf16[64,1440]{1,0:T(8,128)(2,1)S(1)} %copy-done.12, bf16[64,1440]{1,0:T(8,128)(2,1)S(1)} %copy-done.13, bf16[1152,512]{1,0:T(8,128)(2,1)S(1)} %copy-done.15, ...), custom_call_target="tpu_custom_call" | custom-call | flops 6115295232 | bytes 4718592 | tf_op jit(solution)/shard_map/product/pallas_call | solution.py:459
  156.8 4.3 %all-to-all-done.2 = bf16[4,360,256]{2,1,0:T(8,128)(2,1)S(1)} async-done(((bf16[4,360,256]{2,1,0:T(8,128)(2,1)}), bf16[4,360,256]{2,1,0:T(8,128)(2,1)S(1)}, u32[]{:S(2)}, u32[]{:S(2)}) %all-to-all-start.2) | async-done | bytes 737312 | tf_op jit(solution)/shard_map/all_to_all | solution.py:614
  (104 shorter events, 33.2 us)
Async XLA Ops:
  3.8 11.2 %collective-permute-start.2 = (bf16[1152,128]{1,0:T(8,128)(2,1)}, bf16[1152,128]{1,0:T(8,128)(2,1)}, u32[]{:S(2)}, u32[]{:S(2)}) collective-permute-start(bf16[1152,128]{1,0:T(8,128)(2,1)} %get-tuple-element.31.refs_0_), channel_id=1, source_target_pairs={{0,1},{1,0},{2,3},{3,2},{4,5},{5,4},{6,7},{7,6},{8,9},{9,8},{10,11... | collective-permute-start | bytes 884744 | tf_op jit(solution)/shard_map/ppermute | solution.py:554
  6.8 15.2 %collective-permute-start.16 = (bf16[1440,128]{1,0:T(8,128)(2,1)S(1)}, bf16[1440,128]{1,0:T(8,128)(2,1)}, u32[]{:S(2)}, u32[]{:S(2)}) collective-permute-start(bf16[1440,128]{1,0:T(8,128)(2,1)S(1)} %get-tuple-element.41.refs_0_), channel_id=1, source_target_pairs={{0,1},{1,0},{2,3},{3,2},{4,5},{5,4},{6,7},{7,6},{8,9},{9,8},{10,11... | collective-permute-start | bytes 1105928 | tf_op jit(solution)/shard_map/ppermute | solution.py:554
  6.8 23.6 %collective-permute-start = (bf16[1152,128]{1,0:T(8,128)(2,1)}, bf16[1152,128]{1,0:T(8,128)(2,1)}, u32[]{:S(2)}, u32[]{:S(2)}) collective-permute-start(bf16[1152,128]{1,0:T(8,128)(2,1)} %get-tuple-element.31.refs_0_), channel_id=1, source_target_pairs={{1,2},{2,1},{5,6},{6,5},{9,10},{10,9},{13,14},{14,13},{17,18},{18,... | collective-permute-start | bytes 884744 | tf_op jit(solution)/shard_map/ppermute | solution.py:554
  15.0 16.7 %collective-permute-start.3 = (bf16[1152,128]{1,0:T(8,128)(2,1)}, bf16[1152,128]{1,0:T(8,128)(2,1)}, u32[]{:S(2)}, u32[]{:S(2)}) collective-permute-start(bf16[1152,128]{1,0:T(8,128)(2,1)} %collective-permute-done.2.refs_1_), channel_id=1, source_target_pairs={{1,2},{2,1},{5,6},{6,5},{9,10},{10,9},{13,14},{14,13},{17,18},{18,... | collective-permute-start | bytes 884744 | tf_op jit(solution)/shard_map/ppermute | solution.py:554
  16.4 25.3 %collective-permute-start.19 = (bf16[1440,128]{1,0:T(8,128)(2,1)S(1)}, bf16[1440,128]{1,0:T(8,128)(2,1)S(1)}, u32[]{:S(2)}, u32[]{:S(2)}) collective-permute-start(bf16[1440,128]{1,0:T(8,128)(2,1)S(1)} %get-tuple-element.41.refs_0_), channel_id=1, source_target_pairs={{1,2},{2,1},{5,6},{6,5},{9,10},{10,9},{13,14},{14,13},{17,18},{18,... | collective-permute-start | bytes 1105928 | tf_op jit(solution)/shard_map/ppermute | solution.py:554
  22.0 21.0 %collective-permute-start.17 = (bf16[1440,128]{1,0:T(8,128)(2,1)}, bf16[1440,128]{1,0:T(8,128)(2,1)S(1)}, u32[]{:S(2)}, u32[]{:S(2)}) collective-permute-start(bf16[1440,128]{1,0:T(8,128)(2,1)} %collective-permute-done.16.refs_1_), channel_id=1, source_target_pairs={{1,2},{2,1},{5,6},{6,5},{9,10},{10,9},{13,14},{14,13},{17,18},{18,... | collective-permute-start | bytes 1105928 | tf_op jit(solution)/shard_map/ppermute | solution.py:554
  26.0 52.4 %all-to-all-start = ((bf16[8,672,128]{2,1,0:T(8,128)(2,1)}), bf16[8,672,128]{2,1,0:T(8,128)(2,1)}, u32[]{:S(2)}, u32[]{:S(2)}) async-start(bf16[8,672,128]{2,1,0:T(8,128)(2,1)} %copy-done.4), calls=%async_computation | async-start | bytes 2752512 | tf_op jit(solution)/shard_map/all_to_all | solution.py:541
  30.4 13.9 %collective-permute-start.1 = (bf16[1152,128]{1,0:T(8,128)(2,1)}, bf16[1152,128]{1,0:T(8,128)(2,1)S(1)}, u32[]{:S(2)}, u32[]{:S(2)}) collective-permute-start(bf16[1152,128]{1,0:T(8,128)(2,1)} %collective-permute-done.refs_0_), channel_id=1, source_target_pairs={{1,0},{2,3},{5,4},{6,7},{9,8},{10,11},{13,12},{14,15},{17,16},{18,... | collective-permute-start | bytes 884744 | tf_op jit(solution)/shard_map/ppermute | solution.py:554
  31.7 18.9 %collective-permute-start.4 = (bf16[1152,128]{1,0:T(8,128)(2,1)}, bf16[1152,128]{1,0:T(8,128)(2,1)S(1)}, u32[]{:S(2)}, u32[]{:S(2)}) collective-permute-start(bf16[1152,128]{1,0:T(8,128)(2,1)} %collective-permute-done.3.refs_2_), channel_id=1, source_target_pairs={{1,0},{2,3},{5,4},{6,7},{9,8},{10,11},{13,12},{14,15},{17,16},{18,... | collective-permute-start | bytes 884744 | tf_op jit(solution)/shard_map/ppermute | solution.py:554
  41.7 21.9 %collective-permute-start.20 = (bf16[1440,128]{1,0:T(8,128)(2,1)S(1)}, bf16[1440,128]{1,0:T(8,128)(2,1)S(1)}, u32[]{:S(2)}, u32[]{:S(2)}) collective-permute-start(bf16[1440,128]{1,0:T(8,128)(2,1)S(1)} %collective-permute-done.19.refs_0_), channel_id=1, source_target_pairs={{1,0},{2,3},{5,4},{6,7},{9,8},{10,11},{13,12},{14,15},{17,16},{18,... | collective-permute-start | bytes 1105928 | tf_op jit(solution)/shard_map/ppermute | solution.py:554
  43.0 24.4 %collective-permute-start.18 = (bf16[1440,128]{1,0:T(8,128)(2,1)S(1)}, bf16[1440,128]{1,0:T(8,128)(2,1)S(1)}, u32[]{:S(2)}, u32[]{:S(2)}) collective-permute-start(bf16[1440,128]{1,0:T(8,128)(2,1)S(1)} %collective-permute-done.17.refs_0_), channel_id=1, source_target_pairs={{1,0},{2,3},{5,4},{6,7},{9,8},{10,11},{13,12},{14,15},{17,16},{18,... | collective-permute-start | bytes 1105928 | tf_op jit(solution)/shard_map/ppermute | solution.py:554
  56.2 17.8 %collective-permute-start.5 = (bf16[576,512]{1,0:T(8,128)(2,1)S(1)}, bf16[576,512]{1,0:T(8,128)(2,1)S(1)}, u32[]{:S(2)}, u32[]{:S(2)}) collective-permute-start(bf16[576,512]{1,0:T(8,128)(2,1)S(1)} %get-tuple-element.34), channel_id=1, source_target_pairs={{0,4},{4,0},{8,12},{12,8},{16,20},{20,16},{24,28},{28,24},{1,5},{5... | collective-permute-start | bytes 1769480 | tf_op jit(solution)/shard_map/ppermute | solution.py:560
  73.5 25.2 %collective-permute-start.21 = (bf16[720,512]{1,0:T(8,128)(2,1)}, bf16[720,512]{1,0:T(8,128)(2,1)S(1)}, u32[]{:S(2)}, u32[]{:S(2)}) collective-permute-start(bf16[720,512]{1,0:T(8,128)(2,1)} %get-tuple-element.45), channel_id=1, source_target_pairs={{0,4},{4,0},{8,12},{12,8},{16,20},{20,16},{24,28},{28,24},{1,5},{5... | collective-permute-start | bytes 2211848 | tf_op jit(solution)/shard_map/ppermute | solution.py:560
  74.8 7.4 %collective-permute-start.8 = (bf16[576,128]{1,0:T(8,128)(2,1)S(1)}, bf16[576,128]{1,0:T(8,128)(2,1)S(1)}, u32[]{:S(2)}, u32[]{:S(2)}) collective-permute-start(bf16[576,128]{1,0:T(8,128)(2,1)S(1)} %get-tuple-element.38), channel_id=1, source_target_pairs={{0,24},{4,28},{8,16},{12,20},{16,8},{20,12},{24,0},{28,4},{1,25},{... | collective-permute-start | bytes 442376 | tf_op jit(solution)/shard_map/ppermute | solution.py:560
  77.7 7.2 %collective-permute-start.7 = (bf16[576,128]{1,0:T(8,128)(2,1)S(1)}, bf16[576,128]{1,0:T(8,128)(2,1)S(1)}, u32[]{:S(2)}, u32[]{:S(2)}) collective-permute-start(bf16[576,128]{1,0:T(8,128)(2,1)S(1)} %get-tuple-element.37), channel_id=1, source_target_pairs={{0,16},{4,20},{8,24},{12,28},{16,0},{20,4},{24,8},{28,12},{1,17},{... | collective-permute-start | bytes 442376 | tf_op jit(solution)/shard_map/ppermute | solution.py:560
  78.2 7.0 %collective-permute-start.6 = (bf16[576,128]{1,0:T(8,128)(2,1)S(1)}, bf16[576,128]{1,0:T(8,128)(2,1)S(1)}, u32[]{:S(2)}, u32[]{:S(2)}) collective-permute-start(bf16[576,128]{1,0:T(8,128)(2,1)S(1)} %get-tuple-element.36), channel_id=1, source_target_pairs={{0,8},{4,12},{8,0},{12,4},{16,24},{20,28},{24,16},{28,20},{1,9},{5... | collective-permute-start | bytes 442376 | tf_op jit(solution)/shard_map/ppermute | solution.py:560
  87.7 6.4 %collective-permute-start.9 = (bf16[576,128]{1,0:T(8,128)(2,1)}, bf16[576,128]{1,0:T(8,128)(2,1)}, u32[]{:S(2)}, u32[]{:S(2)}) collective-permute-start(bf16[576,128]{1,0:T(8,128)(2,1)} %multiply_convert_fusion.1.refs_0_), channel_id=1, source_target_pairs={{0,8},{4,12},{8,0},{12,4},{16,24},{20,28},{24,16},{28,20},{1,9},{5... | collective-permute-start | bytes 442376 | tf_op jit(solution)/shard_map/ppermute | solution.py:560
  89.2 8.9 %collective-permute-start.10 = (bf16[576,128]{1,0:T(8,128)(2,1)}, bf16[576,128]{1,0:T(8,128)(2,1)}, u32[]{:S(2)}, u32[]{:S(2)}) collective-permute-start(bf16[576,128]{1,0:T(8,128)(2,1)} %multiply_convert_fusion.1.refs_0_), channel_id=1, source_target_pairs={{0,16},{4,20},{8,24},{12,28},{16,0},{20,4},{24,8},{28,12},{1,17},{... | collective-permute-start | bytes 442376 | tf_op jit(solution)/shard_map/ppermute | solution.py:560
  89.9 8.3 %collective-permute-start.11 = (bf16[576,128]{1,0:T(8,128)(2,1)}, bf16[576,128]{1,0:T(8,128)(2,1)}, u32[]{:S(2)}, u32[]{:S(2)}) collective-permute-start(bf16[576,128]{1,0:T(8,128)(2,1)} %multiply_convert_fusion.1.refs_0_), channel_id=1, source_target_pairs={{0,24},{4,28},{8,16},{12,20},{16,8},{20,12},{24,0},{28,4},{1,25},{... | collective-permute-start | bytes 442376 | tf_op jit(solution)/shard_map/ppermute | solution.py:560
  91.2 11.8 %collective-permute-start.12 = (bf16[576,128]{1,0:T(8,128)(2,1)}, bf16[576,128]{1,0:T(8,128)(2,1)}, u32[]{:S(2)}, u32[]{:S(2)}) collective-permute-start(bf16[576,128]{1,0:T(8,128)(2,1)} %multiply_convert_fusion.1.refs_0_), channel_id=1, source_target_pairs={{0,4},{4,0},{8,12},{12,8},{16,20},{20,16},{24,28},{28,24},{1,5},{5... | collective-permute-start | bytes 442376 | tf_op jit(solution)/shard_map/ppermute | solution.py:560
  94.1 9.3 %collective-permute-start.13 = (bf16[576,128]{1,0:T(8,128)(2,1)}, bf16[576,128]{1,0:T(8,128)(2,1)}, u32[]{:S(2)}, u32[]{:S(2)}) collective-permute-start(bf16[576,128]{1,0:T(8,128)(2,1)} %collective-permute-done.9.refs_1_), channel_id=1, source_target_pairs={{0,4},{4,0},{8,12},{12,8},{16,20},{20,16},{24,28},{28,24},{1,5},{5... | collective-permute-start | bytes 442376 | tf_op jit(solution)/shard_map/ppermute | solution.py:560
  98.2 6.9 %collective-permute-start.14 = (bf16[576,128]{1,0:T(8,128)(2,1)}, bf16[576,128]{1,0:T(8,128)(2,1)}, u32[]{:S(2)}, u32[]{:S(2)}) collective-permute-start(bf16[576,128]{1,0:T(8,128)(2,1)} %collective-permute-done.10.refs_2_), channel_id=1, source_target_pairs={{0,4},{4,0},{8,12},{12,8},{16,20},{20,16},{24,28},{28,24},{1,5},{5... | collective-permute-start | bytes 442376 | tf_op jit(solution)/shard_map/ppermute | solution.py:560
  98.2 6.9 %collective-permute-start.15 = (bf16[576,128]{1,0:T(8,128)(2,1)}, bf16[576,128]{1,0:T(8,128)(2,1)}, u32[]{:S(2)}, u32[]{:S(2)}) collective-permute-start(bf16[576,128]{1,0:T(8,128)(2,1)} %collective-permute-done.11.refs_3_), channel_id=1, source_target_pairs={{0,4},{4,0},{8,12},{12,8},{16,20},{20,16},{24,28},{28,24},{1,5},{5... | collective-permute-start | bytes 442376 | tf_op jit(solution)/shard_map/ppermute | solution.py:560
  101.6 14.8 %collective-permute-start.24 = (bf16[720,128]{1,0:T(8,128)(2,1)}, bf16[720,128]{1,0:T(8,128)(2,1)}, u32[]{:S(2)}, u32[]{:S(2)}) collective-permute-start(bf16[720,128]{1,0:T(8,128)(2,1)} %get-tuple-element.49), channel_id=1, source_target_pairs={{0,24},{4,28},{8,16},{12,20},{16,8},{20,12},{24,0},{28,4},{1,25},{... | collective-permute-start | bytes 552968 | tf_op jit(solution)/shard_map/ppermute | solution.py:560
  103.1 13.4 %collective-permute-start.23 = (bf16[720,128]{1,0:T(8,128)(2,1)}, bf16[720,128]{1,0:T(8,128)(2,1)}, u32[]{:S(2)}, u32[]{:S(2)}) collective-permute-start(bf16[720,128]{1,0:T(8,128)(2,1)} %get-tuple-element.48), channel_id=1, source_target_pairs={{0,16},{4,20},{8,24},{12,28},{16,0},{20,4},{24,8},{28,12},{1,17},{... | collective-permute-start | bytes 552968 | tf_op jit(solution)/shard_map/ppermute | solution.py:560
  103.4 13.1 %collective-permute-start.22 = (bf16[720,128]{1,0:T(8,128)(2,1)}, bf16[720,128]{1,0:T(8,128)(2,1)}, u32[]{:S(2)}, u32[]{:S(2)}) collective-permute-start(bf16[720,128]{1,0:T(8,128)(2,1)} %get-tuple-element.47), channel_id=1, source_target_pairs={{0,8},{4,12},{8,0},{12,4},{16,24},{20,28},{24,16},{28,20},{1,9},{5... | collective-permute-start | bytes 552968 | tf_op jit(solution)/shard_map/ppermute | solution.py:560
  112.2 24.3 %all-to-all-start.1 = ((bf16[4,288,256]{2,1,0:T(8,128)(2,1)}), bf16[4,288,256]{2,1,0:T(8,128)(2,1)}, u32[]{:S(2)}, u32[]{:S(2)}) async-start(bf16[4,288,256]{2,1,0:T(8,128)(2,1)} %bitcast.3), calls=%async_computation.1 | async-start | bytes 1179648 | tf_op jit(solution)/shard_map/all_to_all | solution.py:614
  117.9 7.6 %collective-permute-start.25 = (bf16[720,128]{1,0:T(8,128)(2,1)S(1)}, bf16[720,128]{1,0:T(8,128)(2,1)S(1)}, u32[]{:S(2)}, u32[]{:S(2)}) collective-permute-start(bf16[720,128]{1,0:T(8,128)(2,1)S(1)} %multiply_convert_fusion.refs_0_), channel_id=1, source_target_pairs={{0,8},{4,12},{8,0},{12,4},{16,24},{20,28},{24,16},{28,20},{1,9},{5... | collective-permute-start | bytes 552968 | tf_op jit(solution)/shard_map/ppermute | solution.py:560
  118.3 9.5 %collective-permute-start.26 = (bf16[720,128]{1,0:T(8,128)(2,1)S(1)}, bf16[720,128]{1,0:T(8,128)(2,1)S(1)}, u32[]{:S(2)}, u32[]{:S(2)}) collective-permute-start(bf16[720,128]{1,0:T(8,128)(2,1)S(1)} %multiply_convert_fusion.refs_0_), channel_id=1, source_target_pairs={{0,16},{4,20},{8,24},{12,28},{16,0},{20,4},{24,8},{28,12},{1,17},{... | collective-permute-start | bytes 552968 | tf_op jit(solution)/shard_map/ppermute | solution.py:560
  120.0 7.8 %collective-permute-start.27 = (bf16[720,128]{1,0:T(8,128)(2,1)S(1)}, bf16[720,128]{1,0:T(8,128)(2,1)S(1)}, u32[]{:S(2)}, u32[]{:S(2)}) collective-permute-start(bf16[720,128]{1,0:T(8,128)(2,1)S(1)} %multiply_convert_fusion.refs_0_), channel_id=1, source_target_pairs={{0,24},{4,28},{8,16},{12,20},{16,8},{20,12},{24,0},{28,4},{1,25},{... | collective-permute-start | bytes 552968 | tf_op jit(solution)/shard_map/ppermute | solution.py:560
  121.4 6.9 %collective-permute-start.28 = (bf16[720,128]{1,0:T(8,128)(2,1)S(1)}, bf16[720,128]{1,0:T(8,128)(2,1)S(1)}, u32[]{:S(2)}, u32[]{:S(2)}) collective-permute-start(bf16[720,128]{1,0:T(8,128)(2,1)S(1)} %multiply_convert_fusion.refs_0_), channel_id=1, source_target_pairs={{0,4},{4,0},{8,12},{12,8},{16,20},{20,16},{24,28},{28,24},{1,5},{5... | collective-permute-start | bytes 552968 | tf_op jit(solution)/shard_map/ppermute | solution.py:560
  136.5 24.6 %all-to-all-start.2 = ((bf16[4,360,256]{2,1,0:T(8,128)(2,1)}), bf16[4,360,256]{2,1,0:T(8,128)(2,1)S(1)}, u32[]{:S(2)}, u32[]{:S(2)}) async-start(bf16[4,360,256]{2,1,0:T(8,128)(2,1)} %bitcast.5), calls=%async_computation.2 | async-start | bytes 1474560 | tf_op jit(solution)/shard_map/all_to_all | solution.py:614
  (24 other events, 85.0 us)
where the time goes:
time: 163 us; the launch traced here: 162 us
  Pallas kernels  59.1 us (36%)
  starting transfers between devices  41.7 us (26%)
  waiting for transfers between devices  41.5 us (25%)
  local copies, waits for them, and re-layouts  13.2 us (8%)
  other arithmetic  5.68 us (3%)
    pallas_call x5, Pallas kernels, tangent(): pl.pallas_call(functools.partial(tangent_kernel, groups, sources, slots,...  28 us
    ppermute x22, waiting for transfers between devices, swap(): return lax.ppermute(x, 'chan', [(i, i ^ bit) for i in range(across)])  19.1 us
    ppermute x10, waiting for transfers between devices, gathered(): now[link] = lax.ppermute(last[1 - link], 'filt', pairs)  18.1 us
    ppermute x22, starting transfers between devices, swap(): return lax.ppermute(x, 'chan', [(i, i ^ bit) for i in range(across)])  15.7 us
    pallas_call x2, Pallas kernels, cotangent_part(): pl.pallas_call(functools.partial(cotangent_kernel, groups, places), grid_...  14.1 us
    unnamed x42, local copies, waits for them, and re-layouts  12.5 us
    ppermute x10, starting transfers between devices, gathered(): now[link] = lax.ppermute(last[1 - link], 'filt', pairs)  12.3 us
    pallas_call x1, Pallas kernels, product_of(): pl.pallas_call(functools.partial(product_kernel, own, counts, [len(chunk)...  11.2 us
  transfers between devices with their start and end apart: 35, of which 13 were waited for; matrix products, arithmetic and copies ran while one was open for 3% of the time, Pallas kernels for 36%

commit v1 on v0

--- a/solution.py
+++ b/solution.py
@@ -18,6 +18,7 @@
 PIECE = WW * EIGHT
 GROUP = DEEP * PIECE
 
+INNER = 1
 PARAMS = pltpu.CompilerParams(vmem_limit_bytes=28 << 20)
 
 
@@ -275,10 +276,16 @@
     def whole(*shape):
         return pl.BlockSpec(shape, lambda t, m: (0,) * len(shape))
 
+    hbm = pl.BlockSpec(memory_space=pltpu.HBM)
     if last:
-        outs = [(rows // 2, filters, jnp.bfloat16), (rows // 2, filters, jnp.float32)]
+        out_specs = [whole(rows // 2, filters)] * 2
+        outs = [
+            jax.ShapeDtypeStruct((rows // 2, filters), jnp.bfloat16),
+            jax.ShapeDtypeStruct((rows // 2, filters), jnp.float32),
+        ]
     else:
-        outs = [(rows, filters, jnp.float32)]
+        out_specs = [whole(rows, filters)]
+        outs = [jax.ShapeDtypeStruct((rows, filters), jnp.float32)]
     return pl.pallas_call(
         functools.partial(tangent_kernel, groups, sources, slots, more, last),
         grid_spec=pltpu.PrefetchScalarGridSpec(
@@ -287,7 +294,7 @@
             in_specs=[whole_block] * len(shards)
             + [whole_block if count == 1 else row_block] * 2
             + ([whole(rows, filters)] if more else []),
-            out_specs=[whole(*o[:2]) for o in outs] + [pl.BlockSpec(memory_space=pltpu.HBM)],
+            out_specs=out_specs + [hbm],
             scratch_shapes=[
                 pltpu.VMEM((rows, count * LANES), jnp.bfloat16),
                 pltpu.VMEM((count * own, rows), jnp.bfloat16),
@@ -297,8 +304,7 @@
             + ([pltpu.VMEM((rows, filters), jnp.float32)] if last else [])
             + ([pltpu.VMEM((9, LANES, filters), jnp.bfloat16)] if count == 1 else []),
         ),
-        out_shape=[jax.ShapeDtypeStruct(o[:2], o[2]) for o in outs]
-        + [pltpu.HBM((count * own, rows), jnp.bfloat16)],
+        out_shape=outs + [pltpu.HBM((count * own, rows), jnp.bfloat16)],
         cost_estimate=pl.CostEstimate(
             flops=18 * rows * count * LANES * filters,
             bytes_accessed=4 * w.size,
@@ -350,8 +356,10 @@
     copy_all(copies)
 
 
-def cotangent_kernel(groups, places, meta, *refs):
-    w_parts, (k_ref, out_ref, rows_ref, x, views, sem, acc, flat) = refs[:-8], refs[-8:]
+def cotangent_kernel(groups, places, parts, meta, *refs):
+    outs = refs[-6 - parts : -6]
+    w_parts, k_ref = refs[: -7 - parts], refs[-7 - parts]
+    rows_ref, x, views, sem, acc, flat = refs[-6:]
     step = pl.program_id(0)
     keep = pltpu.make_async_copy(x, rows_ref, sem.at[len(w_parts)])
 
@@ -378,25 +386,27 @@
         keep.wait()
         for n in range(acc.shape[0]):
             for g, strip, deep, _, row in pieces_of(groups):
-                target = places(g, strip) + deep * WW
+                target = places[g, strip] + deep * WW
                 flat[pl.ds(target, WW), :] = acc[n, pl.ds(row, WW, stride=EIGHT), :]
-            out_ref[:, n * LANES : (n + 1) * LANES] = flat[...].astype(jnp.bfloat16)
-
-
-def cotangent_part(meta, w_parts, groups, kernel, places):
+            share = flat.shape[0] // parts
+            for m, out in enumerate(outs):
+                at = pl.multiple_of((meta[PLACE] ^ m) * share, share)
+                cols = pl.ds(n * LANES, LANES)
+                out[:, cols] = flat[pl.ds(at, share), :].astype(out.dtype)
+
+
+def cotangent_part(meta, w_parts, groups, kernel, places, parts):
     channels, filters = kernel.shape[1:]
     rows = 2 * w_parts[0].shape[0]
     return pl.pallas_call(
-        functools.partial(cotangent_kernel, groups, places),
+        functools.partial(cotangent_kernel, groups, places, parts),
         grid_spec=pltpu.PrefetchScalarGridSpec(
             num_scalar_prefetch=1,
             grid=(3,),
             in_specs=[pl.BlockSpec(memory_space=pl.ANY)] * len(w_parts)
             + [pl.BlockSpec((3, channels, filters), lambda t, m: (t, 0, 0))],
-            out_specs=[
-                pl.BlockSpec((rows, channels), lambda t, m: (0, 0)),
-                pl.BlockSpec(memory_space=pltpu.HBM),
-            ],
+            out_specs=[pl.BlockSpec((rows // parts, channels), lambda t, m: (0, 0))] * parts
+            + [pl.BlockSpec(memory_space=pltpu.HBM)],
             scratch_shapes=[
                 pltpu.VMEM((rows, filters), jnp.bfloat16),
                 views_shape(len(groups), filters),
@@ -406,9 +416,10 @@
             ],
         ),
         out_shape=[
-            jax.ShapeDtypeStruct((rows, channels), jnp.bfloat16),
-            pltpu.HBM((rows, filters), jnp.bfloat16),
-        ],
+            jax.ShapeDtypeStruct((rows // parts, channels), jnp.bfloat16 if m else jnp.float32)
+            for m in range(parts)
+        ]
+        + [pltpu.HBM((rows, filters), jnp.bfloat16)],
         cost_estimate=pl.CostEstimate(
             flops=18 * rows * channels * filters,
             bytes_accessed=18 * channels * filters,
@@ -505,15 +516,11 @@
     pixels, own = activations.shape
     channels = kernel.shape[1]
 
-    first, second, middle = [], [], []
     per = 2 * (pixels // (HH * WW)) // depth
-    for a in range(0, depth, 2):
-        at = a // 2 * per
-        first += [(at, at + 1), (at + per - 2, at + per - 1)]
-        second += [(at + 2, at + 3), (at + per - 4, at + per - 3)]
-        middle.append(at + 4)
-    second.append(tuple(middle))
-    chunks = [second, first]
+    outer, inner = [], []
+    for image in range(per * depth // 2):
+        (inner if abs(image % per - per // 2) <= INNER else outer).append(image)
+    chunks = [list(zip(images[::PAIR], images[1::PAIR])) for images in (outer, inner)]
 
     orders, owners = [], []
     for place in range(depth):
@@ -596,27 +603,23 @@
         factor = lax.dynamic_slice_in_dim(factor, half * rows, rows, axis=0)
         w = weigh(factor[:, :LANES], factor[:, LANES:], mine)
         parts = [w] + [swap(w, 2 * m) for m in range(1, chips)]
-        return parts + [swap(part, 1) for part in parts]
-
-    strip_rows = GROUP // EIGHT
-    share = len(second) * GROUP // depth
-
-    def place_first(g, strip):
-        return g * GROUP + strip * strip_rows
-
-    def place_second(g, strip):
-        if g < depth:
-            return g * share + strip * strip_rows
-        place, rest = divmod(strip, EIGHT // depth)
-        return place * share + GROUP + rest * strip_rows
-
-    def spread(part):
-        part = lax.all_to_all(
-            part.reshape(depth, -1, channels), "filt", 0, 0, tiled=True
-        ).astype(jnp.float32)
-        total = part[0]
-        for j in range(1, depth):
-            total = total + part[j]
+        parts += [swap(part, 1) for part in parts]
+        return [pltpu.with_memory_space_constraint(part, pltpu.HBM) for part in parts]
+
+    def places_of(groups):
+        strip_rows = GROUP // EIGHT
+        sources = {}
+        for g, images in enumerate(groups):
+            for strip in range(EIGHT):
+                row = images[strip // STRIPS] * HH * WW + strip % STRIPS * strip_rows
+                sources[row] = (g, strip)
+        return {sources[row]: n * strip_rows for n, row in enumerate(sorted(sources))}
+
+    def spread(own_part, parts):
+        total = own_part
+        for m, part in enumerate(parts):
+            part = lax.ppermute(part, "filt", [(i, i ^ (m + 1)) for i in range(depth)])
+            total = total + part.astype(jnp.float32)
         return total.astype(jnp.bfloat16)
 
     got = [gathered(x) for x in mixed]
@@ -624,9 +627,9 @@
     mine = [exchange(*sums[c]) for c in range(2)]
     w = [weighted(mine[c], factors[c]) for c in range(2)]
     cots, whole = [], []
-    for c, place in enumerate((place_second, place_first)):
-        part, rows = cotangent_part(meta, w[c], chunks[c], kernel, place)
-        cots.append(spread(part))
+    for c, place in enumerate([places_of(groups) for groups in chunks]):
+        own_part, *parts, rows = cotangent_part(meta, w[c], chunks[c], kernel, place, depth)
+        cots.append(spread(own_part, parts))
         whole.append(rows)
     scale = float(1.0 / (float(pixels) ** 0.5))
     product = product_of(
@@ -637,12 +640,8 @@
         channels,
         own,
     )
-    inner, outer = cots
-    main, edge = inner[:GROUP], inner[GROUP:]
     result = jnp.where(
-        lax.rem(z, 2) == 0,
-        jnp.concatenate([outer, main, edge], axis=0),
-        jnp.concatenate([edge, main, outer], axis=0),
+        lax.rem(z, 2) == 0, jnp.concatenate(cots, axis=0), jnp.concatenate(cots[::-1], axis=0)
     )
     return (result, product)
 

time: 163 us -> 164 us (level)
  waiting for transfers between devices: 41.5 us -> 46.1 us
  starting transfers between devices: 41.7 us -> 38.7 us
  other arithmetic: 5.68 us -> 3.35 us
    all_to_all x2 -> x0, starting transfers between devices: 9.33 us -> none  [spread(): lax.all_to_all(part.reshape(depth, -1, channels), 'filt', 0, 0, tiled=True)]
    ppermute x0 -> x6, waiting for transfers between devices: none -> 8.7 us  [spread(): part = lax.ppermute(part, 'filt', [(i, i ^ m + 1) for i in range(depth)])]
    ppermute x0 -> x6, starting transfers between devices: none -> 7.83 us  [spread(): part = lax.ppermute(part, 'filt', [(i, i ^ m + 1) for i in range(depth)])]
    ppermute x10, waiting for transfers between devices: 18.1 us -> 24.6 us  [gathered(): now[link] = lax.ppermute(last[1 - link], 'filt', pairs)]
    ppermute x22, waiting for transfers between devices: 19.1 us -> 12.9 us  [swap(): return lax.ppermute(x, 'chan', [(i, i ^ bit) for i in range(across)])]
    all_to_all x2 -> x0, waiting for transfers between devices: 4.35 us -> none  [spread(): lax.all_to_all(part.reshape(depth, -1, channels), 'filt', 0, 0, tiled=True)]
    unnamed x42 -> x60, local copies, waits for them, and re-layouts: 12.5 us -> 13.3 us
  transfers between devices with their start and end apart: 35 -> 39, of which waited for: 13 -> 15; matrix products, arithmetic and copies ran while one was open for 3% -> 1% of each run, Pallas kernels for 36% -> 31%
where the time goes in v1:
time: 164 us; the launch traced here: 163 us
  Pallas kernels  59.4 us (36%)
  waiting for transfers between devices  46.1 us (28%)
  starting transfers between devices  38.7 us (24%)
  local copies, waits for them, and re-layouts  14 us (9%)
  other arithmetic  3.35 us (2%)
    pallas_call x5, Pallas kernels, tangent(): pl.pallas_call(functools.partial(tangent_kernel, groups, sources, slots,...  27.9 us
    ppermute x10, waiting for transfers between devices, gathered(): now[link] = lax.ppermute(last[1 - link], 'filt', pairs)  24.6 us
    ppermute x22, starting transfers between devices, swap(): return lax.ppermute(x, 'chan', [(i, i ^ bit) for i in range(across)])  15.5 us
    pallas_call x2, Pallas kernels, cotangent_part(): pl.pallas_call(functools.partial(cotangent_kernel, groups, places, parts)...  13.5 us
    unnamed x60, local copies, waits for them, and re-layouts  13.3 us
    ppermute x22, waiting for transfers between devices, swap(): return lax.ppermute(x, 'chan', [(i, i ^ bit) for i in range(across)])  12.9 us
    pallas_call x1, Pallas kernels, product_of(): pl.pallas_call(functools.partial(product_kernel, own, counts, [len(chunk)...  11.2 us
    ppermute x10, starting transfers between devices, gathered(): now[link] = lax.ppermute(last[1 - link], 'filt', pairs)  11.1 us
  transfers between devices with their start and end apart: 39, of which 15 were waited for; matrix products, arithmetic and copies ran while one was open for 1% of the time, Pallas kernels for 31%

profile of v1, /device:TPU:0, one launch (start us, length us, event | category | flops | bytes accessed | tf_op | source)
XLA Modules:
  0.0 162.6 jit_solution(2280576165955473649)
XLA Ops:
  3.9 3.1 %collective-permute-start = (bf16[1728,128]{1,0:T(8,128)(2,1)}, bf16[1728,128]{1,0:T(8,128)(2,1)}, u32[]{:S(2)}, u32[]{:S(2)}) collective-permute-start(bf16[1728,128]{1,0:T(8,128)(2,1)} %get-tuple-element.37.refs_0_), channel_id=1, source_target_pairs={{0,1},{1,0},{2,3},{3,2},{4,5},{5,4},{6,7},{7,6},{8,9},{9,8},{10,11... | collective-permute-start | bytes 1327112 | tf_op jit(solution)/shard_map/ppermute | solution.py:561
  7.8 10.5 %collective-permute-done.refs_1_ = bf16[1728,128]{1,0:T(8,128)(2,1)} collective-permute-done((bf16[1728,128]{1,0:T(8,128)(2,1)}, bf16[1728,128]{1,0:T(8,128)(2,1)}, u32[]{:S(2)}, u32[]{:S(2)}) %collective-permute-start) | collective-permute-done | bytes 442400 | tf_op jit(solution)/shard_map/ppermute | solution.py:561
  22.9 4.3 %all-to-all-start = ((bf16[8,672,128]{2,1,0:T(8,128)(2,1)}), bf16[8,672,128]{2,1,0:T(8,128)(2,1)}, u32[]{:S(2)}, u32[]{:S(2)}) async-start(bf16[8,672,128]{2,1,0:T(8,128)(2,1)} %copy-done.3), calls=%async_computation | async-start | bytes 2752512 | tf_op jit(solution)/shard_map/all_to_all | solution.py:548
  29.9 1.7 %copy-done.1 = bf16[9,256,512]{2,1,0:T(8,128)(2,1)S(1)} copy-done((bf16[9,256,512]{2,1,0:T(8,128)(2,1)S(1)}, bf16[9,256,512]{2,1,0:T(8,128)(2,1)}, u32[]{:S(2)}) %copy-start.1) | copy-done | bytes 2359320
  31.5 5.2 %tangent.8 = (f32[864,512]{1,0:T(8,128)S(1)}, bf16[128,864]{1,0:T(8,128)(2,1)}) custom-call(s32[7]{0:T(128)S(1)} %fusion.meta, bf16[864,128]{1,0:T(8,128)(2,1)} %get-tuple-element.51.refs_0_, bf16[864,128]{1,0:T(8,128)(2,1)} %collective-permute-done.21.refs_1_, bf16[9,256,512]{2,1,0:T(8,128)(2,1)S(1)} %copy-done, bf16[9,256,512]{2,1,0:T(8,128)(2,1)S(1)} %copy-done.1), custom_call_target="tpu_custom_call" | custom-call | flops 2038431744 | bytes 4718592 | tf_op jit(solution)/shard_map/tangent/pallas_call | solution.py:289
  40.6 8.6 %tangent.5 = (f32[1728,512]{1,0:T(8,128)S(1)}, bf16[128,1728]{1,0:T(8,128)(2,1)}) custom-call(s32[7]{0:T(128)S(1)} %fusion.meta, bf16[1728,128]{1,0:T(8,128)(2,1)} %get-tuple-element.37.refs_0_, bf16[1728,128]{1,0:T(8,128)(2,1)} %collective-permute-done.refs_1_, bf16[9,256,512]{2,1,0:T(8,128)(2,1)S(1)} %copy-done, bf16[9,256,512]{2,1,0:T(8,128)(2,1)S(1)} %copy-done.1), custom_call_target="tpu_custom_call" | custom-call | flops 4076863488 | bytes 4718592 | tf_op jit(solution)/shard_map/tangent/pallas_call | solution.py:289
  49.2 13.9 %collective-permute-done.23.refs_3_ = bf16[864,128]{1,0:T(8,128)(2,1)S(1)} collective-permute-done((bf16[864,128]{1,0:T(8,128)(2,1)S(1)}, bf16[864,128]{1,0:T(8,128)(2,1)S(1)}, u32[]{:S(2)}, u32[]{:S(2)}) %collective-permute-start.23) | collective-permute-done | bytes 221216 | tf_op jit(solution)/shard_map/ppermute | solution.py:561
  63.1 4.2 %tangent.9 = (bf16[432,512]{1,0:T(8,128)(2,1)S(1)}, f32[432,512]{1,0:T(8,128)S(1)}, bf16[128,864]{1,0:T(8,128)(2,1)}) custom-call(s32[7]{0:T(128)S(1)} %fusion.meta, bf16[864,128]{1,0:T(8,128)(2,1)S(1)} %collective-permute-done.19.refs_0_, bf16[864,128]{1,0:T(8,128)(2,1)S(1)} %collective-permute-done.20.refs_1_, ...), custom_call_target="tpu_custom_call" | custom-call | flops 2038431744 | bytes 4718592 | tf_op jit(solution)/shard_map/tangent/pallas_call | solution.py:289
  67.4 4.4 %tangent.6 = (f32[1728,512]{1,0:T(8,128)S(1)}, bf16[64,1728]{1,0:T(8,128)(2,1)}) custom-call(s32[7]{0:T(128)S(1)} %fusion.meta, bf16[1728,128]{1,0:T(8,128)(2,1)S(1)} %collective-permute-done.3.refs_0_, bf16[1728,128]{1,0:T(8,128)(2,1)S(1)} %collective-permute-done.4.refs_1_, bf16[9,256,512]{2,1,0:T(8,128)(2,1)S(1)} %copy-done, ...), custom_call_target="tpu_custom_call" | custom-call | flops 2038431744 | bytes 4718592 | tf_op jit(solution)/shard_map/tangent/pallas_call | solution.py:289
  71.9 5.6 %tangent.7 = (bf16[864,512]{1,0:T(8,128)(2,1)}, f32[864,512]{1,0:T(8,128)S(1)}, bf16[64,1728]{1,0:T(8,128)(2,1)}) custom-call(s32[7]{0:T(128)S(1)} %fusion.meta, bf16[1728,128]{1,0:T(8,128)(2,1)S(1)} %collective-permute-done.1.refs_0_, bf16[1728,128]{1,0:T(8,128)(2,1)S(1)} %collective-permute-done.2.refs_1_, bf16[9,256,512]{2,1,0:T(8,128)(2,1)S(1)} %copy-done, ...), custom_call_target="tpu_custom_call" | custom-call | flops 2038431744 | bytes 4718592 | tf_op jit(solution)/shard_map/tangent/pallas_call | solution.py:289
  80.4 1.9 %collective-permute-start.25 = (bf16[432,128]{1,0:T(8,128)(2,1)}, bf16[432,128]{1,0:T(8,128)(2,1)}, u32[]{:S(2)}, u32[]{:S(2)}) collective-permute-start(bf16[432,128]{1,0:T(8,128)(2,1)} %get-tuple-element.56), channel_id=1, source_target_pairs={{0,8},{4,12},{8,0},{12,4},{16,24},{20,28},{24,16},{28,20},{1,9},{5... | collective-permute-start | bytes 331784 | tf_op jit(solution)/shard_map/ppermute | solution.py:567
  82.3 1.5 collective-permute-start.26
  83.9 2.3 %shard_map.86 = (bf16[1728,256]{1,0:T(8,128)(2,1)S(1)}, bf16[864,256]{1,0:T(8,128)(2,1)S(1)}) custom-call(bf16[8,672,128]{2,1,0:T(8,128)(2,1)} %all-to-all-done.x_ref), custom_call_target="tpu_custom_call" | custom-call | tf_op jit(solution)/shard_map/pallas_call | solution.py:122
  86.3 2.4 %collective-permute-done.26 = bf16[432,128]{1,0:T(8,128)(2,1)} collective-permute-done((bf16[432,128]{1,0:T(8,128)(2,1)}, bf16[432,128]{1,0:T(8,128)(2,1)}, u32[]{:S(2)}, u32[]{:S(2)}) %collective-permute-start.26) | collective-permute-done | bytes 110624 | tf_op jit(solution)/shard_map/ppermute | solution.py:567
  92.9 1.5 collective-permute-start.30
  94.4 2.2 %collective-permute-done.28.refs_1_ = bf16[432,128]{1,0:T(8,128)(2,1)S(1)} collective-permute-done((bf16[432,128]{1,0:T(8,128)(2,1)S(1)}, bf16[432,128]{1,0:T(8,128)(2,1)S(1)}, u32[]{:S(2)}, u32[]{:S(2)}) %collective-permute-start.28) | collective-permute-done | bytes 110624 | tf_op jit(solution)/shard_map/ppermute | solution.py:567
  98.7 1.5 copy-done.5
  100.2 1.6 split.2
  102.6 1.5 collective-permute-start.6
  105.3 1.4 collective-permute-start.8
  106.7 5.2 %cotangent.3 = (f32[216,256]{1,0:T(8,128)S(1)}, bf16[216,256]{1,0:T(8,128)(2,1)S(1)}, bf16[216,256]{1,0:T(8,128)(2,1)S(1)}, bf16[216,256]{1,0:T(8,128)(2,1)S(1)}, bf16[864,512]{1,0:T(8,128)(2,1)}) custom-call(s32[7]{0:T(128)S(1)} %fusion.meta, bf16[432,128]{1,0:T(8,128)(2,1)} %copy-done.22, bf16[432,128]{1,0:T(8,128)(2,1)} %copy-done.27, ...), custom_call_target="tpu_custom_call" | custom-call | flops 2038431744 | bytes 2359296 | tf_op jit(solution)/shard_map/cotangent/pallas_call | solution.py:401
  112.0 4.7 %collective-permute-done.7 = bf16[864,128]{1,0:T(8,128)(2,1)} collective-permute-done((bf16[864,128]{1,0:T(8,128)(2,1)}, bf16[864,128]{1,0:T(8,128)(2,1)}, u32[]{:S(2)}, u32[]{:S(2)}) %collective-permute-start.7) | collective-permute-done | bytes 221216 | tf_op jit(solution)/shard_map/ppermute | solution.py:567
  119.9 1.6 collective-permute-start.11
  121.5 1.9 %collective-permute-start.36 = (bf16[216,256]{1,0:T(8,128)(2,1)S(1)}, bf16[216,256]{1,0:T(8,128)(2,1)S(1)}, u32[]{:S(2)}, u32[]{:S(2)}) collective-permute-start(bf16[216,256]{1,0:T(8,128)(2,1)S(1)} %get-tuple-element.61), channel_id=1, source_target_pairs={{0,2},{1,3},{2,0},{3,1},{4,6},{5,7},{6,4},{7,5},{8,10},{9,11},{10,... | collective-permute-start | bytes 331784 | tf_op jit(solution)/shard_map/ppermute | solution.py:621
  123.4 1.9 %collective-permute-done.35 = bf16[216,256]{1,0:T(8,128)(2,1)S(1)} collective-permute-done((bf16[216,256]{1,0:T(8,128)(2,1)S(1)}, bf16[216,256]{1,0:T(8,128)(2,1)S(1)}, u32[]{:S(2)}, u32[]{:S(2)}) %collective-permute-start.35) | collective-permute-done | bytes 110624 | tf_op jit(solution)/shard_map/ppermute | solution.py:621
  125.3 1.5 collective-permute-start.37
  126.7 3.3 %collective-permute-done.36 = bf16[216,256]{1,0:T(8,128)(2,1)S(1)} collective-permute-done((bf16[216,256]{1,0:T(8,128)(2,1)S(1)}, bf16[216,256]{1,0:T(8,128)(2,1)S(1)}, u32[]{:S(2)}, u32[]{:S(2)}) %collective-permute-start.36) | collective-permute-done | bytes 110624 | tf_op jit(solution)/shard_map/ppermute | solution.py:621
  133.6 8.3 %cotangent.2 = (f32[432,256]{1,0:T(8,128)S(1)}, bf16[432,256]{1,0:T(8,128)(2,1)S(1)}, bf16[432,256]{1,0:T(8,128)(2,1)S(1)}, bf16[432,256]{1,0:T(8,128)(2,1)S(1)}, bf16[1728,512]{1,0:T(8,128)(2,1)}) custom-call(s32[7]{0:T(128)S(1)} %fusion.meta, bf16[864,128]{1,0:T(8,128)(2,1)} %copy-done.21, bf16[864,128]{1,0:T(8,128)(2,1)} %collective-permute-done.9.refs_1_, ...), custom_call_target="tpu_custom_call" | custom-call | flops 4076863488 | bytes 2359296 | tf_op jit(solution)/shard_map/cotangent/pallas_call | solution.py:401
  144.4 2.0 %collective-permute-start.18 = (bf16[432,256]{1,0:T(8,128)(2,1)S(1)}, bf16[432,256]{1,0:T(8,128)(2,1)S(1)}, u32[]{:S(2)}, u32[]{:S(2)}) collective-permute-start(bf16[432,256]{1,0:T(8,128)(2,1)S(1)} %get-tuple-element.49), channel_id=1, source_target_pairs={{0,3},{1,2},{2,1},{3,0},{4,7},{5,6},{6,5},{7,4},{8,11},{9,10},{10,... | collective-permute-start | bytes 663560 | tf_op jit(solution)/shard_map/ppermute | solution.py:621
  146.4 1.5 copy-done.19
  147.8 11.2 %product.1 = f32[9,256,512]{2,1,0:T(8,128)} custom-call(s32[7]{0:T(128)S(1)} %fusion.meta, bf16[1728,512]{1,0:T(8,128)(2,1)S(1)} %copy-done.19, bf16[128,1728]{1,0:T(8,128)(2,1)S(1)} %copy-done.20, bf16[64,1728]{1,0:T(8,128)(2,1)S(1)} %copy-done.14, bf16[64,1728]{1,0:T(8,128)(2,1)S(1)} %copy-done.15, bf16[864,512]{1,0:T(8,128)(2,1)S(1)} %copy-done.17, ...), custom_call_target="tpu_custom_call" | custom-call | flops 6115295232 | bytes 4718592 | tf_op jit(solution)/shard_map/product/pallas_call | solution.py:470
  159.0 2.6 %collective-permute-done.17 = bf16[432,256]{1,0:T(8,128)(2,1)S(1)} collective-permute-done((bf16[432,256]{1,0:T(8,128)(2,1)S(1)}, bf16[432,256]{1,0:T(8,128)(2,1)S(1)}, u32[]{:S(2)}, u32[]{:S(2)}) %collective-permute-start.17) | collective-permute-done | bytes 221216 | tf_op jit(solution)/shard_map/ppermute | solution.py:621
  (125 shorter events, 37.0 us)
Async XLA Ops:
  3.9 14.4 %collective-permute-start = (bf16[1728,128]{1,0:T(8,128)(2,1)}, bf16[1728,128]{1,0:T(8,128)(2,1)}, u32[]{:S(2)}, u32[]{:S(2)}) collective-permute-start(bf16[1728,128]{1,0:T(8,128)(2,1)} %get-tuple-element.37.refs_0_), channel_id=1, source_target_pairs={{0,1},{1,0},{2,3},{3,2},{4,5},{5,4},{6,7},{7,6},{8,9},{9,8},{10,11... | collective-permute-start | bytes 1327112 | tf_op jit(solution)/shard_map/ppermute | solution.py:561
  6.9 20.2 %collective-permute-start.21 = (bf16[864,128]{1,0:T(8,128)(2,1)}, bf16[864,128]{1,0:T(8,128)(2,1)}, u32[]{:S(2)}, u32[]{:S(2)}) collective-permute-start(bf16[864,128]{1,0:T(8,128)(2,1)} %get-tuple-element.51.refs_0_), channel_id=1, source_target_pairs={{0,1},{1,0},{2,3},{3,2},{4,5},{5,4},{6,7},{7,6},{8,9},{9,8},{10,11... | collective-permute-start | bytes 663560 | tf_op jit(solution)/shard_map/ppermute | solution.py:561
  7.0 29.7 %collective-permute-start.3 = (bf16[1728,128]{1,0:T(8,128)(2,1)}, bf16[1728,128]{1,0:T(8,128)(2,1)S(1)}, u32[]{:S(2)}, u32[]{:S(2)}) collective-permute-start(bf16[1728,128]{1,0:T(8,128)(2,1)} %get-tuple-element.37.refs_0_), channel_id=1, source_target_pairs={{1,2},{2,1},{5,6},{6,5},{9,10},{10,9},{13,14},{14,13},{17,18},{18,... | collective-permute-start | bytes 1327112 | tf_op jit(solution)/shard_map/ppermute | solution.py:561
  18.3 21.0 %collective-permute-start.1 = (bf16[1728,128]{1,0:T(8,128)(2,1)}, bf16[1728,128]{1,0:T(8,128)(2,1)S(1)}, u32[]{:S(2)}, u32[]{:S(2)}) collective-permute-start(bf16[1728,128]{1,0:T(8,128)(2,1)} %collective-permute-done.refs_1_), channel_id=1, source_target_pairs={{1,2},{2,1},{5,6},{6,5},{9,10},{10,9},{13,14},{14,13},{17,18},{18,... | collective-permute-start | bytes 1327112 | tf_op jit(solution)/shard_map/ppermute | solution.py:561
  18.9 9.6 %collective-permute-start.19 = (bf16[864,128]{1,0:T(8,128)(2,1)}, bf16[864,128]{1,0:T(8,128)(2,1)S(1)}, u32[]{:S(2)}, u32[]{:S(2)}) collective-permute-start(bf16[864,128]{1,0:T(8,128)(2,1)} %get-tuple-element.51.refs_0_), channel_id=1, source_target_pairs={{1,2},{2,1},{5,6},{6,5},{9,10},{10,9},{13,14},{14,13},{17,18},{18,... | collective-permute-start | bytes 663560 | tf_op jit(solution)/shard_map/ppermute | solution.py:561
  22.9 61.1 %all-to-all-start = ((bf16[8,672,128]{2,1,0:T(8,128)(2,1)}), bf16[8,672,128]{2,1,0:T(8,128)(2,1)}, u32[]{:S(2)}, u32[]{:S(2)}) async-start(bf16[8,672,128]{2,1,0:T(8,128)(2,1)} %copy-done.3), calls=%async_computation | async-start | bytes 2752512 | tf_op jit(solution)/shard_map/all_to_all | solution.py:548
  27.2 10.8 %collective-permute-start.22 = (bf16[864,128]{1,0:T(8,128)(2,1)}, bf16[864,128]{1,0:T(8,128)(2,1)S(1)}, u32[]{:S(2)}, u32[]{:S(2)}) collective-permute-start(bf16[864,128]{1,0:T(8,128)(2,1)} %collective-permute-done.21.refs_1_), channel_id=1, source_target_pairs={{1,2},{2,1},{5,6},{6,5},{9,10},{10,9},{13,14},{14,13},{17,18},{18,... | collective-permute-start | bytes 663560 | tf_op jit(solution)/shard_map/ppermute | solution.py:561
  28.6 20.6 %collective-permute-start.20 = (bf16[864,128]{1,0:T(8,128)(2,1)S(1)}, bf16[864,128]{1,0:T(8,128)(2,1)S(1)}, u32[]{:S(2)}, u32[]{:S(2)}) collective-permute-start(bf16[864,128]{1,0:T(8,128)(2,1)S(1)} %collective-permute-done.19.refs_0_), channel_id=1, source_target_pairs={{1,0},{2,3},{5,4},{6,7},{9,8},{10,11},{13,12},{14,15},{17,16},{18,... | collective-permute-start | bytes 663560 | tf_op jit(solution)/shard_map/ppermute | solution.py:561
  36.7 30.7 %collective-permute-start.4 = (bf16[1728,128]{1,0:T(8,128)(2,1)S(1)}, bf16[1728,128]{1,0:T(8,128)(2,1)S(1)}, u32[]{:S(2)}, u32[]{:S(2)}) collective-permute-start(bf16[1728,128]{1,0:T(8,128)(2,1)S(1)} %collective-permute-done.3.refs_0_), channel_id=1, source_target_pairs={{1,0},{2,3},{5,4},{6,7},{9,8},{10,11},{13,12},{14,15},{17,16},{18,... | collective-permute-start | bytes 1327112 | tf_op jit(solution)/shard_map/ppermute | solution.py:561
  38.0 25.1 %collective-permute-start.23 = (bf16[864,128]{1,0:T(8,128)(2,1)S(1)}, bf16[864,128]{1,0:T(8,128)(2,1)S(1)}, u32[]{:S(2)}, u32[]{:S(2)}) collective-permute-start(bf16[864,128]{1,0:T(8,128)(2,1)S(1)} %collective-permute-done.22.refs_2_), channel_id=1, source_target_pairs={{1,0},{2,3},{5,4},{6,7},{9,8},{10,11},{13,12},{14,15},{17,16},{18,... | collective-permute-start | bytes 663560 | tf_op jit(solution)/shard_map/ppermute | solution.py:561
  39.3 32.6 %collective-permute-start.2 = (bf16[1728,128]{1,0:T(8,128)(2,1)S(1)}, bf16[1728,128]{1,0:T(8,128)(2,1)S(1)}, u32[]{:S(2)}, u32[]{:S(2)}) collective-permute-start(bf16[1728,128]{1,0:T(8,128)(2,1)S(1)} %collective-permute-done.1.refs_0_), channel_id=1, source_target_pairs={{1,0},{2,3},{5,4},{6,7},{9,8},{10,11},{13,12},{14,15},{17,16},{18,... | collective-permute-start | bytes 1327112 | tf_op jit(solution)/shard_map/ppermute | solution.py:561
  67.3 11.8 %collective-permute-start.24 = (bf16[432,512]{1,0:T(8,128)(2,1)S(1)}, bf16[432,512]{1,0:T(8,128)(2,1)S(1)}, u32[]{:S(2)}, u32[]{:S(2)}) collective-permute-start(bf16[432,512]{1,0:T(8,128)(2,1)S(1)} %get-tuple-element.54), channel_id=1, source_target_pairs={{0,4},{4,0},{8,12},{12,8},{16,20},{20,16},{24,28},{28,24},{1,5},{5... | collective-permute-start | bytes 1327112 | tf_op jit(solution)/shard_map/ppermute | solution.py:567
  78.8 19.9 %collective-permute-start.5 = (bf16[864,512]{1,0:T(8,128)(2,1)}, bf16[864,512]{1,0:T(8,128)(2,1)S(1)}, u32[]{:S(2)}, u32[]{:S(2)}) collective-permute-start(bf16[864,512]{1,0:T(8,128)(2,1)} %get-tuple-element.41), channel_id=1, source_target_pairs={{0,4},{4,0},{8,12},{12,8},{16,20},{20,16},{24,28},{28,24},{1,5},{5... | collective-permute-start | bytes 2654216 | tf_op jit(solution)/shard_map/ppermute | solution.py:567
  80.4 5.9 %collective-permute-start.25 = (bf16[432,128]{1,0:T(8,128)(2,1)}, bf16[432,128]{1,0:T(8,128)(2,1)}, u32[]{:S(2)}, u32[]{:S(2)}) collective-permute-start(bf16[432,128]{1,0:T(8,128)(2,1)} %get-tuple-element.56), channel_id=1, source_target_pairs={{0,8},{4,12},{8,0},{12,4},{16,24},{20,28},{24,16},{28,20},{1,9},{5... | collective-permute-start | bytes 331784 | tf_op jit(solution)/shard_map/ppermute | solution.py:567
  82.3 6.4 %collective-permute-start.26 = (bf16[432,128]{1,0:T(8,128)(2,1)}, bf16[432,128]{1,0:T(8,128)(2,1)}, u32[]{:S(2)}, u32[]{:S(2)}) collective-permute-start(bf16[432,128]{1,0:T(8,128)(2,1)} %get-tuple-element.57), channel_id=1, source_target_pairs={{0,16},{4,20},{8,24},{12,28},{16,0},{20,4},{24,8},{28,12},{1,17},{... | collective-permute-start | bytes 331784 | tf_op jit(solution)/shard_map/ppermute | solution.py:567
  83.8 6.0 %collective-permute-start.27 = (bf16[432,128]{1,0:T(8,128)(2,1)}, bf16[432,128]{1,0:T(8,128)(2,1)}, u32[]{:S(2)}, u32[]{:S(2)}) collective-permute-start(bf16[432,128]{1,0:T(8,128)(2,1)} %get-tuple-element.58), channel_id=1, source_target_pairs={{0,24},{4,28},{8,16},{12,20},{16,8},{20,12},{24,0},{28,4},{1,25},{... | collective-permute-start | bytes 331784 | tf_op jit(solution)/shard_map/ppermute | solution.py:567
  92.9 5.8 %collective-permute-start.30 = (bf16[432,128]{1,0:T(8,128)(2,1)S(1)}, bf16[432,128]{1,0:T(8,128)(2,1)}, u32[]{:S(2)}, u32[]{:S(2)}) collective-permute-start(bf16[432,128]{1,0:T(8,128)(2,1)S(1)} %multiply_convert_fusion.1.refs_0_), channel_id=1, source_target_pairs={{0,24},{4,28},{8,16},{12,20},{16,8},{20,12},{24,0},{28,4},{1,25},{... | collective-permute-start | bytes 331784 | tf_op jit(solution)/shard_map/ppermute | solution.py:567
  94.4 9.6 %collective-permute-start.31 = (bf16[432,128]{1,0:T(8,128)(2,1)S(1)}, bf16[432,128]{1,0:T(8,128)(2,1)S(1)}, u32[]{:S(2)}, u32[]{:S(2)}) collective-permute-start(bf16[432,128]{1,0:T(8,128)(2,1)S(1)} %multiply_convert_fusion.1.refs_0_), channel_id=1, source_target_pairs={{0,4},{4,0},{8,12},{12,8},{16,20},{20,16},{24,28},{28,24},{1,5},{5... | collective-permute-start | bytes 331784 | tf_op jit(solution)/shard_map/ppermute | solution.py:567
  96.6 8.0 %collective-permute-start.32 = (bf16[432,128]{1,0:T(8,128)(2,1)S(1)}, bf16[432,128]{1,0:T(8,128)(2,1)S(1)}, u32[]{:S(2)}, u32[]{:S(2)}) collective-permute-start(bf16[432,128]{1,0:T(8,128)(2,1)S(1)} %collective-permute-done.28.refs_1_), channel_id=1, source_target_pairs={{0,4},{4,0},{8,12},{12,8},{16,20},{20,16},{24,28},{28,24},{1,5},{5... | collective-permute-start | bytes 331784 | tf_op jit(solution)/shard_map/ppermute | solution.py:567
  97.4 9.4 %collective-permute-start.33 = (bf16[432,128]{1,0:T(8,128)(2,1)}, bf16[432,128]{1,0:T(8,128)(2,1)}, u32[]{:S(2)}, u32[]{:S(2)}) collective-permute-start(bf16[432,128]{1,0:T(8,128)(2,1)} %collective-permute-done.29.refs_2_), channel_id=1, source_target_pairs={{0,4},{4,0},{8,12},{12,8},{16,20},{20,16},{24,28},{28,24},{1,5},{5... | collective-permute-start | bytes 331784 | tf_op jit(solution)/shard_map/ppermute | solution.py:567
  98.7 8.0 %collective-permute-start.34 = (bf16[432,128]{1,0:T(8,128)(2,1)}, bf16[432,128]{1,0:T(8,128)(2,1)}, u32[]{:S(2)}, u32[]{:S(2)}) collective-permute-start(bf16[432,128]{1,0:T(8,128)(2,1)} %collective-permute-done.30.refs_3_), channel_id=1, source_target_pairs={{0,4},{4,0},{8,12},{12,8},{16,20},{20,16},{24,28},{28,24},{1,5},{5... | collective-permute-start | bytes 331784 | tf_op jit(solution)/shard_map/ppermute | solution.py:567
  102.6 9.4 %collective-permute-start.6 = (bf16[864,128]{1,0:T(8,128)(2,1)}, bf16[864,128]{1,0:T(8,128)(2,1)S(1)}, u32[]{:S(2)}, u32[]{:S(2)}) collective-permute-start(bf16[864,128]{1,0:T(8,128)(2,1)} %get-tuple-element.43), channel_id=1, source_target_pairs={{0,8},{4,12},{8,0},{12,4},{16,24},{20,28},{24,16},{28,20},{1,9},{5... | collective-permute-start | bytes 663560 | tf_op jit(solution)/shard_map/ppermute | solution.py:567
  104.0 12.6 %collective-permute-start.7 = (bf16[864,128]{1,0:T(8,128)(2,1)}, bf16[864,128]{1,0:T(8,128)(2,1)}, u32[]{:S(2)}, u32[]{:S(2)}) collective-permute-start(bf16[864,128]{1,0:T(8,128)(2,1)} %get-tuple-element.44), channel_id=1, source_target_pairs={{0,16},{4,20},{8,24},{12,28},{16,0},{20,4},{24,8},{28,12},{1,17},{... | collective-permute-start | bytes 663560 | tf_op jit(solution)/shard_map/ppermute | solution.py:567
  105.3 11.4 %collective-permute-start.8 = (bf16[864,128]{1,0:T(8,128)(2,1)S(1)}, bf16[864,128]{1,0:T(8,128)(2,1)}, u32[]{:S(2)}, u32[]{:S(2)}) collective-permute-start(bf16[864,128]{1,0:T(8,128)(2,1)S(1)} %get-tuple-element.45), channel_id=1, source_target_pairs={{0,24},{4,28},{8,16},{12,20},{16,8},{20,12},{24,0},{28,4},{1,25},{... | collective-permute-start | bytes 663560 | tf_op jit(solution)/shard_map/ppermute | solution.py:567
  117.9 12.1 %collective-permute-start.9 = (bf16[864,128]{1,0:T(8,128)(2,1)S(1)}, bf16[864,128]{1,0:T(8,128)(2,1)}, u32[]{:S(2)}, u32[]{:S(2)}) collective-permute-start(bf16[864,128]{1,0:T(8,128)(2,1)S(1)} %multiply_convert_fusion.refs_0_), channel_id=1, source_target_pairs={{0,8},{4,12},{8,0},{12,4},{16,24},{20,28},{24,16},{28,20},{1,9},{5... | collective-permute-start | bytes 663560 | tf_op jit(solution)/shard_map/ppermute | solution.py:567
  118.5 12.0 %collective-permute-start.10 = (bf16[864,128]{1,0:T(8,128)(2,1)S(1)}, bf16[864,128]{1,0:T(8,128)(2,1)}, u32[]{:S(2)}, u32[]{:S(2)}) collective-permute-start(bf16[864,128]{1,0:T(8,128)(2,1)S(1)} %multiply_convert_fusion.refs_0_), channel_id=1, source_target_pairs={{0,16},{4,20},{8,24},{12,28},{16,0},{20,4},{24,8},{28,12},{1,17},{... | collective-permute-start | bytes 663560 | tf_op jit(solution)/shard_map/ppermute | solution.py:567
  119.9 10.7 %collective-permute-start.11 = (bf16[864,128]{1,0:T(8,128)(2,1)S(1)}, bf16[864,128]{1,0:T(8,128)(2,1)}, u32[]{:S(2)}, u32[]{:S(2)}) collective-permute-start(bf16[864,128]{1,0:T(8,128)(2,1)S(1)} %multiply_convert_fusion.refs_0_), channel_id=1, source_target_pairs={{0,24},{4,28},{8,16},{12,20},{16,8},{20,12},{24,0},{28,4},{1,25},{... | collective-permute-start | bytes 663560 | tf_op jit(solution)/shard_map/ppermute | solution.py:567
  121.5 8.6 %collective-permute-start.36 = (bf16[216,256]{1,0:T(8,128)(2,1)S(1)}, bf16[216,256]{1,0:T(8,128)(2,1)S(1)}, u32[]{:S(2)}, u32[]{:S(2)}) collective-permute-start(bf16[216,256]{1,0:T(8,128)(2,1)S(1)} %get-tuple-element.61), channel_id=1, source_target_pairs={{0,2},{1,3},{2,0},{3,1},{4,6},{5,7},{6,4},{7,5},{8,10},{9,11},{10,... | collective-permute-start | bytes 331784 | tf_op jit(solution)/shard_map/ppermute | solution.py:621
  125.3 6.6 %collective-permute-start.37 = (bf16[216,256]{1,0:T(8,128)(2,1)S(1)}, bf16[216,256]{1,0:T(8,128)(2,1)S(1)}, u32[]{:S(2)}, u32[]{:S(2)}) collective-permute-start(bf16[216,256]{1,0:T(8,128)(2,1)S(1)} %get-tuple-element.62), channel_id=1, source_target_pairs={{0,3},{1,2},{2,1},{3,0},{4,7},{5,6},{6,5},{7,4},{8,11},{9,10},{10,... | collective-permute-start | bytes 331784 | tf_op jit(solution)/shard_map/ppermute | solution.py:621
  141.9 17.1 %collective-permute-start.16 = (bf16[432,256]{1,0:T(8,128)(2,1)S(1)}, bf16[432,256]{1,0:T(8,128)(2,1)S(1)}, u32[]{:S(2)}, u32[]{:S(2)}) collective-permute-start(bf16[432,256]{1,0:T(8,128)(2,1)S(1)} %get-tuple-element.47), channel_id=1, source_target_pairs={{0,1},{1,0},{2,3},{3,2},{4,5},{5,4},{6,7},{7,6},{8,9},{9,8},{10,11... | collective-permute-start | bytes 663560 | tf_op jit(solution)/shard_map/ppermute | solution.py:621
  142.9 18.7 %collective-permute-start.17 = (bf16[432,256]{1,0:T(8,128)(2,1)S(1)}, bf16[432,256]{1,0:T(8,128)(2,1)S(1)}, u32[]{:S(2)}, u32[]{:S(2)}) collective-permute-start(bf16[432,256]{1,0:T(8,128)(2,1)S(1)} %get-tuple-element.48), channel_id=1, source_target_pairs={{0,2},{1,3},{2,0},{3,1},{4,6},{5,7},{6,4},{7,5},{8,10},{9,11},{10,... | collective-permute-start | bytes 663560 | tf_op jit(solution)/shard_map/ppermute | solution.py:621
  144.4 17.3 %collective-permute-start.18 = (bf16[432,256]{1,0:T(8,128)(2,1)S(1)}, bf16[432,256]{1,0:T(8,128)(2,1)S(1)}, u32[]{:S(2)}, u32[]{:S(2)}) collective-permute-start(bf16[432,256]{1,0:T(8,128)(2,1)S(1)} %get-tuple-element.49), channel_id=1, source_target_pairs={{0,3},{1,2},{2,1},{3,0},{4,7},{5,6},{6,5},{7,4},{8,11},{9,10},{10,... | collective-permute-start | bytes 663560 | tf_op jit(solution)/shard_map/ppermute | solution.py:621
  (37 other events, 240.1 us)

commit v2 on v1

--- a/solution.py
+++ b/solution.py
@@ -581,8 +581,8 @@
                 shards,
                 sources,
                 slots,
-                kernel_tangent,
-                kernel,
+                pltpu.with_memory_space_constraint(kernel_tangent, pltpu.HBM),
+                pltpu.with_memory_space_constraint(kernel, pltpu.HBM),
                 len(chunks[c]),
                 before,
                 n == len(stages) - 1,
@@ -627,8 +627,9 @@
     mine = [exchange(*sums[c]) for c in range(2)]
     w = [weighted(mine[c], factors[c]) for c in range(2)]
     cots, whole = [], []
+    kernel_hbm = pltpu.with_memory_space_constraint(kernel, pltpu.HBM)
     for c, place in enumerate([places_of(groups) for groups in chunks]):
-        own_part, *parts, rows = cotangent_part(meta, w[c], chunks[c], kernel, place, depth)
+        own_part, *parts, rows = cotangent_part(meta, w[c], chunks[c], kernel_hbm, place, depth)
         cots.append(spread(own_part, parts))
         whole.append(rows)
     scale = float(1.0 / (float(pixels) ** 0.5))

time: 164 us -> 162 us (0.988)
  Pallas kernels: 59.4 us -> 66.2 us
  local copies, waits for them, and re-layouts: 14 us -> 7.94 us
  waiting for transfers between devices: 46.1 us -> 44.4 us
    unnamed x60 -> x58, local copies, waits for them, and re-layouts: 13.3 us -> 7.24 us
    pallas_call x5, Pallas kernels: 27.9 us -> 32.5 us  [tangent(): pl.pallas_call(functools.partial(tangent_kernel, groups, sources, slots,...]
    pallas_call x2, Pallas kernels: 13.5 us -> 15.9 us  [cotangent_part(): pl.pallas_call(functools.partial(cotangent_kernel, groups, places, parts)...]
  transfers between devices with their start and end apart: 39 -> 39, of which waited for: 15 -> 13; matrix products, arithmetic and copies ran while one was open for 1% -> 1% of each run, Pallas kernels for 31% -> 35%
where the time goes in v2:
time: 162 us; the launch traced here: 161 us
  Pallas kernels  66.2 us (41%)
  waiting for transfers between devices  44.4 us (27%)
  starting transfers between devices  39 us (24%)
  local copies, waits for them, and re-layouts  7.94 us (5%)
  other arithmetic  2.29 us (1%)
    pallas_call x5, Pallas kernels, tangent(): pl.pallas_call(functools.partial(tangent_kernel, groups, sources, slots,...  32.5 us
    ppermute x10, waiting for transfers between devices, gathered(): now[link] = lax.ppermute(last[1 - link], 'filt', pairs)  23.3 us
    pallas_call x2, Pallas kernels, cotangent_part(): pl.pallas_call(functools.partial(cotangent_kernel, groups, places, parts)...  15.9 us
    ppermute x22, starting transfers between devices, swap(): return lax.ppermute(x, 'chan', [(i, i ^ bit) for i in range(across)])  15.8 us
    ppermute x22, waiting for transfers between devices, swap(): return lax.ppermute(x, 'chan', [(i, i ^ bit) for i in range(across)])  12.6 us
    pallas_call x1, Pallas kernels, product_of(): pl.pallas_call(functools.partial(product_kernel, own, counts, [len(chunk)...  11.2 us
    ppermute x10, starting transfers between devices, gathered(): now[link] = lax.ppermute(last[1 - link], 'filt', pairs)  10.9 us
    ppermute x6, waiting for transfers between devices, spread(): part = lax.ppermute(part, 'filt', [(i, i ^ m + 1) for i in range(depth)])  8.56 us
  transfers between devices with their start and end apart: 39, of which 13 were waited for; matrix products, arithmetic and copies ran while one was open for 1% of the time, Pallas kernels for 35%

profile of v2, /device:TPU:0, one launch (start us, length us, event | category | flops | bytes accessed | tf_op | source)
XLA Modules:
  0.0 161.0 jit_solution(16709234527287102490)
XLA Ops:
  3.7 3.1 %collective-permute-start = (bf16[1728,128]{1,0:T(8,128)(2,1)S(1)}, bf16[1728,128]{1,0:T(8,128)(2,1)S(1)}, u32[]{:S(2)}, u32[]{:S(2)}) collective-permute-start(bf16[1728,128]{1,0:T(8,128)(2,1)S(1)} %get-tuple-element.37.refs_0_), channel_id=1, source_target_pairs={{0,1},{1,0},{2,3},{3,2},{4,5},{5,4},{6,7},{7,6},{8,9},{9,8},{10,11... | collective-permute-start | bytes 1327112 | tf_op jit(solution)/shard_map/ppermute | solution.py:561
  7.5 10.3 %collective-permute-done.refs_1_ = bf16[1728,128]{1,0:T(8,128)(2,1)S(1)} collective-permute-done((bf16[1728,128]{1,0:T(8,128)(2,1)S(1)}, bf16[1728,128]{1,0:T(8,128)(2,1)S(1)}, u32[]{:S(2)}, u32[]{:S(2)}) %collective-permute-start) | collective-permute-done | bytes 442400 | tf_op jit(solution)/shard_map/ppermute | solution.py:561
  22.4 4.2 %all-to-all-start = ((bf16[8,672,128]{2,1,0:T(8,128)(2,1)}), bf16[8,672,128]{2,1,0:T(8,128)(2,1)S(1)}, u32[]{:S(2)}, u32[]{:S(2)}) async-start(bf16[8,672,128]{2,1,0:T(8,128)(2,1)} %pack.1), calls=%async_computation | async-start | bytes 2752512 | tf_op jit(solution)/shard_map/all_to_all | solution.py:548
  29.2 7.0 %tangent.8 = (f32[864,512]{1,0:T(8,128)S(1)}, bf16[128,864]{1,0:T(8,128)(2,1)}) custom-call(s32[7]{0:T(128)S(1)} %fusion.meta, bf16[864,128]{1,0:T(8,128)(2,1)} %get-tuple-element.51.refs_0_, bf16[864,128]{1,0:T(8,128)(2,1)} %collective-permute-done.21.refs_1_, bf16[9,256,512]{2,1,0:T(8,128)(2,1)} %refs_4_.1, bf16[9,256,512]{2,1,0:T(8,128)(2,1)} %refs_8_.3), custom_call_target="tpu_custom_call" | custom-call | flops 2038431744 | bytes 4718592 | tf_op jit(solution)/shard_map/tangent/pallas_call | solution.py:289
  40.2 9.0 %tangent.5 = (f32[1728,512]{1,0:T(8,128)S(1)}, bf16[128,1728]{1,0:T(8,128)(2,1)}) custom-call(s32[7]{0:T(128)S(1)} %fusion.meta, bf16[1728,128]{1,0:T(8,128)(2,1)S(1)} %get-tuple-element.37.refs_0_, bf16[1728,128]{1,0:T(8,128)(2,1)S(1)} %collective-permute-done.refs_1_, bf16[9,256,512]{2,1,0:T(8,128)(2,1)} %refs_4_.1, bf16[9,256,512]{2,1,0:T(8,128)(2,1)} %refs_8_.3), custom_call_target="tpu_custom_call" | custom-call | flops 4076863488 | bytes 4718592 | tf_op jit(solution)/shard_map/tangent/pallas_call | solution.py:289
  49.2 13.0 %collective-permute-done.23.refs_3_ = bf16[864,128]{1,0:T(8,128)(2,1)S(1)} collective-permute-done((bf16[864,128]{1,0:T(8,128)(2,1)S(1)}, bf16[864,128]{1,0:T(8,128)(2,1)S(1)}, u32[]{:S(2)}, u32[]{:S(2)}) %collective-permute-start.23) | collective-permute-done | bytes 221216 | tf_op jit(solution)/shard_map/ppermute | solution.py:561
  62.1 6.0 %tangent.9 = (bf16[432,512]{1,0:T(8,128)(2,1)S(1)}, f32[432,512]{1,0:T(8,128)S(1)}, bf16[128,864]{1,0:T(8,128)(2,1)}) custom-call(s32[7]{0:T(128)S(1)} %fusion.meta, bf16[864,128]{1,0:T(8,128)(2,1)S(1)} %collective-permute-done.19.refs_0_, bf16[864,128]{1,0:T(8,128)(2,1)S(1)} %collective-permute-done.20.refs_1_, ...), custom_call_target="tpu_custom_call" | custom-call | flops 2038431744 | bytes 4718592 | tf_op jit(solution)/shard_map/tangent/pallas_call | solution.py:289
  68.3 4.7 %tangent.6 = (f32[1728,512]{1,0:T(8,128)S(1)}, bf16[64,1728]{1,0:T(8,128)(2,1)}) custom-call(s32[7]{0:T(128)S(1)} %fusion.meta, bf16[1728,128]{1,0:T(8,128)(2,1)S(1)} %collective-permute-done.3.refs_0_, bf16[1728,128]{1,0:T(8,128)(2,1)S(1)} %collective-permute-done.4.refs_1_, bf16[9,256,512]{2,1,0:T(8,128)(2,1)} %refs_4_.1, bf16[9,256,512]{2,1,0:T(8,128)(2,1)} %refs_8_.3, ...), custom_call_target="tpu_custom_call" | custom-call | flops 2038431744 | bytes 4718592 | tf_op jit(solution)/shard_map/tangent/pallas_call | solution.py:289
  73.0 5.8 %tangent.7 = (bf16[864,512]{1,0:T(8,128)(2,1)}, f32[864,512]{1,0:T(8,128)S(1)}, bf16[64,1728]{1,0:T(8,128)(2,1)}) custom-call(s32[7]{0:T(128)S(1)} %fusion.meta, bf16[1728,128]{1,0:T(8,128)(2,1)S(1)} %copy-done.1, bf16[1728,128]{1,0:T(8,128)(2,1)S(1)} %collective-permute-done.2.refs_1_, bf16[9,256,512]{2,1,0:T(8,128)(2,1)} %refs_4_.1, ...), custom_call_target="tpu_custom_call" | custom-call | flops 2038431744 | bytes 4718592 | tf_op jit(solution)/shard_map/tangent/pallas_call | solution.py:289
  80.7 2.0 %collective-permute-start.25 = (bf16[432,128]{1,0:T(8,128)(2,1)}, bf16[432,128]{1,0:T(8,128)(2,1)}, u32[]{:S(2)}, u32[]{:S(2)}) collective-permute-start(bf16[432,128]{1,0:T(8,128)(2,1)} %get-tuple-element.56), channel_id=1, source_target_pairs={{0,8},{4,12},{8,0},{12,4},{16,24},{20,28},{24,16},{28,20},{1,9},{5... | collective-permute-start | bytes 331784 | tf_op jit(solution)/shard_map/ppermute | solution.py:567
  82.7 1.5 collective-permute-start.26
  85.1 1.4 collective-permute-done.25
  86.5 3.7 %collective-permute-done.26 = bf16[432,128]{1,0:T(8,128)(2,1)} collective-permute-done((bf16[432,128]{1,0:T(8,128)(2,1)}, bf16[432,128]{1,0:T(8,128)(2,1)}, u32[]{:S(2)}, u32[]{:S(2)}) %collective-permute-start.26) | collective-permute-done | bytes 110624 | tf_op jit(solution)/shard_map/ppermute | solution.py:567
  93.3 1.5 collective-permute-start.30
  94.8 2.2 %collective-permute-done.28.refs_1_ = bf16[432,128]{1,0:T(8,128)(2,1)S(1)} collective-permute-done((bf16[432,128]{1,0:T(8,128)(2,1)S(1)}, bf16[432,128]{1,0:T(8,128)(2,1)S(1)}, u32[]{:S(2)}, u32[]{:S(2)}) %collective-permute-start.28) | collective-permute-done | bytes 110624 | tf_op jit(solution)/shard_map/ppermute | solution.py:567
  99.0 2.1 %split.2 = (f32[864,128]{1,0:T(8,128)S(1)}, bf16[864,128]{1,0:T(8,128)(2,1)S(1)}, bf16[864,128]{1,0:T(8,128)(2,1)S(1)}, bf16[864,128]{1,0:T(8,128)(2,1)S(1)}) custom-call(s32[7]{0:T(128)S(1)} %fusion.meta, f32[864,512]{1,0:T(8,128)S(1)} %get-tuple-element.40.keep_ref, bf16[864,512]{1,0:T(8,128)(2,1)} %collective-permute-done.5.got_ref), custom_call_target="tpu_custom_call" | custom-call | flops 442368 | bytes 3538944 | tf_op jit(solution)/shard_map/split/pallas_call | solution.py:333
  101.1 1.5 collective-permute-start.6
  103.9 1.4 collective-permute-start.8
  105.3 6.6 %cotangent.3 = (f32[216,256]{1,0:T(8,128)S(1)}, bf16[216,256]{1,0:T(8,128)(2,1)S(1)}, bf16[216,256]{1,0:T(8,128)(2,1)S(1)}, bf16[216,256]{1,0:T(8,128)(2,1)S(1)}, bf16[864,512]{1,0:T(8,128)(2,1)}) custom-call(s32[7]{0:T(128)S(1)} %fusion.meta, bf16[432,128]{1,0:T(8,128)(2,1)} %copy-done.16, bf16[432,128]{1,0:T(8,128)(2,1)} %copy-done.24, ...), custom_call_target="tpu_custom_call" | custom-call | flops 2038431744 | bytes 2359296 | tf_op jit(solution)/shard_map/cotangent/pallas_call | solution.py:401
  111.9 3.0 %collective-permute-done.7 = bf16[864,128]{1,0:T(8,128)(2,1)S(1)} collective-permute-done((bf16[864,128]{1,0:T(8,128)(2,1)S(1)}, bf16[864,128]{1,0:T(8,128)(2,1)S(1)}, u32[]{:S(2)}, u32[]{:S(2)}) %collective-permute-start.7) | collective-permute-done | bytes 221216 | tf_op jit(solution)/shard_map/ppermute | solution.py:567
  115.7 1.4 collective-permute-start.10
  117.1 1.5 collective-permute-start.11
  118.6 2.1 %collective-permute-start.36 = (bf16[216,256]{1,0:T(8,128)(2,1)S(1)}, bf16[216,256]{1,0:T(8,128)(2,1)S(1)}, u32[]{:S(2)}, u32[]{:S(2)}) collective-permute-start(bf16[216,256]{1,0:T(8,128)(2,1)S(1)} %get-tuple-element.61), channel_id=1, source_target_pairs={{0,2},{1,3},{2,0},{3,1},{4,6},{5,7},{6,4},{7,5},{8,10},{9,11},{10,... | collective-permute-start | bytes 331784 | tf_op jit(solution)/shard_map/ppermute | solution.py:621
  120.8 1.8 %collective-permute-done.35 = bf16[216,256]{1,0:T(8,128)(2,1)S(1)} collective-permute-done((bf16[216,256]{1,0:T(8,128)(2,1)S(1)}, bf16[216,256]{1,0:T(8,128)(2,1)S(1)}, u32[]{:S(2)}, u32[]{:S(2)}) %collective-permute-start.35) | collective-permute-done | bytes 110624 | tf_op jit(solution)/shard_map/ppermute | solution.py:621
  122.6 1.5 collective-permute-start.37
  124.1 3.2 %collective-permute-done.36 = bf16[216,256]{1,0:T(8,128)(2,1)S(1)} collective-permute-done((bf16[216,256]{1,0:T(8,128)(2,1)S(1)}, bf16[216,256]{1,0:T(8,128)(2,1)S(1)}, u32[]{:S(2)}, u32[]{:S(2)}) %collective-permute-start.36) | collective-permute-done | bytes 110624 | tf_op jit(solution)/shard_map/ppermute | solution.py:621
  130.9 9.3 %cotangent.2 = (f32[432,256]{1,0:T(8,128)S(1)}, bf16[432,256]{1,0:T(8,128)(2,1)S(1)}, bf16[432,256]{1,0:T(8,128)(2,1)S(1)}, bf16[432,256]{1,0:T(8,128)(2,1)S(1)}, bf16[1728,512]{1,0:T(8,128)(2,1)}) custom-call(s32[7]{0:T(128)S(1)} %fusion.meta, bf16[864,128]{1,0:T(8,128)(2,1)} %copy-done.15, bf16[864,128]{1,0:T(8,128)(2,1)} %copy-done.17, ...), custom_call_target="tpu_custom_call" | custom-call | flops 4076863488 | bytes 2359296 | tf_op jit(solution)/shard_map/cotangent/pallas_call | solution.py:401
  141.3 1.4 collective-permute-start.17
  142.7 2.0 %collective-permute-start.18 = (bf16[432,256]{1,0:T(8,128)(2,1)S(1)}, bf16[432,256]{1,0:T(8,128)(2,1)S(1)}, u32[]{:S(2)}, u32[]{:S(2)}) collective-permute-start(bf16[432,256]{1,0:T(8,128)(2,1)S(1)} %get-tuple-element.49), channel_id=1, source_target_pairs={{0,3},{1,2},{2,1},{3,0},{4,7},{5,6},{6,5},{7,4},{8,11},{9,10},{10,... | collective-permute-start | bytes 663560 | tf_op jit(solution)/shard_map/ppermute | solution.py:621
  144.7 1.5 copy-done.13
  146.2 11.2 %product.1 = f32[9,256,512]{2,1,0:T(8,128)} custom-call(s32[7]{0:T(128)S(1)} %fusion.meta, bf16[1728,512]{1,0:T(8,128)(2,1)S(1)} %copy-done.13, bf16[128,1728]{1,0:T(8,128)(2,1)S(1)} %copy-done.14, bf16[64,1728]{1,0:T(8,128)(2,1)S(1)} %copy-done.8, bf16[64,1728]{1,0:T(8,128)(2,1)S(1)} %copy-done.9, bf16[864,512]{1,0:T(8,128)(2,1)S(1)} %copy-done.11, ...), custom_call_target="tpu_custom_call" | custom-call | flops 6115295232 | bytes 4718592 | tf_op jit(solution)/shard_map/product/pallas_call | solution.py:470
  157.4 2.6 %collective-permute-done.17 = bf16[432,256]{1,0:T(8,128)(2,1)S(1)} collective-permute-done((bf16[432,256]{1,0:T(8,128)(2,1)S(1)}, bf16[432,256]{1,0:T(8,128)(2,1)S(1)}, u32[]{:S(2)}, u32[]{:S(2)}) %collective-permute-start.17) | collective-permute-done | bytes 221216 | tf_op jit(solution)/shard_map/ppermute | solution.py:621
  (123 shorter events, 30.6 us)
Async XLA Ops:
  3.7 14.1 %collective-permute-start = (bf16[1728,128]{1,0:T(8,128)(2,1)S(1)}, bf16[1728,128]{1,0:T(8,128)(2,1)S(1)}, u32[]{:S(2)}, u32[]{:S(2)}) collective-permute-start(bf16[1728,128]{1,0:T(8,128)(2,1)S(1)} %get-tuple-element.37.refs_0_), channel_id=1, source_target_pairs={{0,1},{1,0},{2,3},{3,2},{4,5},{5,4},{6,7},{7,6},{8,9},{9,8},{10,11... | collective-permute-start | bytes 1327112 | tf_op jit(solution)/shard_map/ppermute | solution.py:561
  6.8 19.8 %collective-permute-start.21 = (bf16[864,128]{1,0:T(8,128)(2,1)}, bf16[864,128]{1,0:T(8,128)(2,1)}, u32[]{:S(2)}, u32[]{:S(2)}) collective-permute-start(bf16[864,128]{1,0:T(8,128)(2,1)} %get-tuple-element.51.refs_0_), channel_id=1, source_target_pairs={{0,1},{1,0},{2,3},{3,2},{4,5},{5,4},{6,7},{7,6},{8,9},{9,8},{10,11... | collective-permute-start | bytes 663560 | tf_op jit(solution)/shard_map/ppermute | solution.py:561
  6.8 29.4 %collective-permute-start.3 = (bf16[1728,128]{1,0:T(8,128)(2,1)S(1)}, bf16[1728,128]{1,0:T(8,128)(2,1)S(1)}, u32[]{:S(2)}, u32[]{:S(2)}) collective-permute-start(bf16[1728,128]{1,0:T(8,128)(2,1)S(1)} %get-tuple-element.37.refs_0_), channel_id=1, source_target_pairs={{1,2},{2,1},{5,6},{6,5},{9,10},{10,9},{13,14},{14,13},{17,18},{18,... | collective-permute-start | bytes 1327112 | tf_op jit(solution)/shard_map/ppermute | solution.py:561
  17.8 21.0 %collective-permute-start.1 = (bf16[1728,128]{1,0:T(8,128)(2,1)S(1)}, bf16[1728,128]{1,0:T(8,128)(2,1)S(1)}, u32[]{:S(2)}, u32[]{:S(2)}) collective-permute-start(bf16[1728,128]{1,0:T(8,128)(2,1)S(1)} %collective-permute-done.refs_1_), channel_id=1, source_target_pairs={{1,2},{2,1},{5,6},{6,5},{9,10},{10,9},{13,14},{14,13},{17,18},{18,... | collective-permute-start | bytes 1327112 | tf_op jit(solution)/shard_map/ppermute | solution.py:561
  18.5 9.5 %collective-permute-start.19 = (bf16[864,128]{1,0:T(8,128)(2,1)}, bf16[864,128]{1,0:T(8,128)(2,1)S(1)}, u32[]{:S(2)}, u32[]{:S(2)}) collective-permute-start(bf16[864,128]{1,0:T(8,128)(2,1)} %get-tuple-element.51.refs_0_), channel_id=1, source_target_pairs={{1,2},{2,1},{5,6},{6,5},{9,10},{10,9},{13,14},{14,13},{17,18},{18,... | collective-permute-start | bytes 663560 | tf_op jit(solution)/shard_map/ppermute | solution.py:561
  22.4 61.8 %all-to-all-start = ((bf16[8,672,128]{2,1,0:T(8,128)(2,1)}), bf16[8,672,128]{2,1,0:T(8,128)(2,1)S(1)}, u32[]{:S(2)}, u32[]{:S(2)}) async-start(bf16[8,672,128]{2,1,0:T(8,128)(2,1)} %pack.1), calls=%async_computation | async-start | bytes 2752512 | tf_op jit(solution)/shard_map/all_to_all | solution.py:548
  26.6 11.0 %collective-permute-start.22 = (bf16[864,128]{1,0:T(8,128)(2,1)}, bf16[864,128]{1,0:T(8,128)(2,1)S(1)}, u32[]{:S(2)}, u32[]{:S(2)}) collective-permute-start(bf16[864,128]{1,0:T(8,128)(2,1)} %collective-permute-done.21.refs_1_), channel_id=1, source_target_pairs={{1,2},{2,1},{5,6},{6,5},{9,10},{10,9},{13,14},{14,13},{17,18},{18,... | collective-permute-start | bytes 663560 | tf_op jit(solution)/shard_map/ppermute | solution.py:561
  27.9 21.2 %collective-permute-start.20 = (bf16[864,128]{1,0:T(8,128)(2,1)S(1)}, bf16[864,128]{1,0:T(8,128)(2,1)S(1)}, u32[]{:S(2)}, u32[]{:S(2)}) collective-permute-start(bf16[864,128]{1,0:T(8,128)(2,1)S(1)} %collective-permute-done.19.refs_0_), channel_id=1, source_target_pairs={{1,0},{2,3},{5,4},{6,7},{9,8},{10,11},{13,12},{14,15},{17,16},{18,... | collective-permute-start | bytes 663560 | tf_op jit(solution)/shard_map/ppermute | solution.py:561
  36.2 32.0 %collective-permute-start.4 = (bf16[1728,128]{1,0:T(8,128)(2,1)S(1)}, bf16[1728,128]{1,0:T(8,128)(2,1)S(1)}, u32[]{:S(2)}, u32[]{:S(2)}) collective-permute-start(bf16[1728,128]{1,0:T(8,128)(2,1)S(1)} %collective-permute-done.3.refs_0_), channel_id=1, source_target_pairs={{1,0},{2,3},{5,4},{6,7},{9,8},{10,11},{13,12},{14,15},{17,16},{18,... | collective-permute-start | bytes 1327112 | tf_op jit(solution)/shard_map/ppermute | solution.py:561
  37.5 24.6 %collective-permute-start.23 = (bf16[864,128]{1,0:T(8,128)(2,1)S(1)}, bf16[864,128]{1,0:T(8,128)(2,1)S(1)}, u32[]{:S(2)}, u32[]{:S(2)}) collective-permute-start(bf16[864,128]{1,0:T(8,128)(2,1)S(1)} %collective-permute-done.22.refs_2_), channel_id=1, source_target_pairs={{1,0},{2,3},{5,4},{6,7},{9,8},{10,11},{13,12},{14,15},{17,16},{18,... | collective-permute-start | bytes 663560 | tf_op jit(solution)/shard_map/ppermute | solution.py:561
  38.9 34.1 %collective-permute-start.2 = (bf16[1728,128]{1,0:T(8,128)(2,1)S(1)}, bf16[1728,128]{1,0:T(8,128)(2,1)S(1)}, u32[]{:S(2)}, u32[]{:S(2)}) collective-permute-start(bf16[1728,128]{1,0:T(8,128)(2,1)S(1)} %collective-permute-done.1.refs_0_), channel_id=1, source_target_pairs={{1,0},{2,3},{5,4},{6,7},{9,8},{10,11},{13,12},{14,15},{17,16},{18,... | collective-permute-start | bytes 1327112 | tf_op jit(solution)/shard_map/ppermute | solution.py:561
  68.2 11.1 %collective-permute-start.24 = (bf16[432,512]{1,0:T(8,128)(2,1)S(1)}, bf16[432,512]{1,0:T(8,128)(2,1)S(1)}, u32[]{:S(2)}, u32[]{:S(2)}) collective-permute-start(bf16[432,512]{1,0:T(8,128)(2,1)S(1)} %get-tuple-element.54), channel_id=1, source_target_pairs={{0,4},{4,0},{8,12},{12,8},{16,20},{20,16},{24,28},{28,24},{1,5},{5... | collective-permute-start | bytes 1327112 | tf_op jit(solution)/shard_map/ppermute | solution.py:567
  78.8 20.2 %collective-permute-start.5 = (bf16[864,512]{1,0:T(8,128)(2,1)}, bf16[864,512]{1,0:T(8,128)(2,1)}, u32[]{:S(2)}, u32[]{:S(2)}) collective-permute-start(bf16[864,512]{1,0:T(8,128)(2,1)} %get-tuple-element.41), channel_id=1, source_target_pairs={{0,4},{4,0},{8,12},{12,8},{16,20},{20,16},{24,28},{28,24},{1,5},{5... | collective-permute-start | bytes 2654216 | tf_op jit(solution)/shard_map/ppermute | solution.py:567
  80.7 5.8 %collective-permute-start.25 = (bf16[432,128]{1,0:T(8,128)(2,1)}, bf16[432,128]{1,0:T(8,128)(2,1)}, u32[]{:S(2)}, u32[]{:S(2)}) collective-permute-start(bf16[432,128]{1,0:T(8,128)(2,1)} %get-tuple-element.56), channel_id=1, source_target_pairs={{0,8},{4,12},{8,0},{12,4},{16,24},{20,28},{24,16},{28,20},{1,9},{5... | collective-permute-start | bytes 331784 | tf_op jit(solution)/shard_map/ppermute | solution.py:567
  82.7 7.4 %collective-permute-start.26 = (bf16[432,128]{1,0:T(8,128)(2,1)}, bf16[432,128]{1,0:T(8,128)(2,1)}, u32[]{:S(2)}, u32[]{:S(2)}) collective-permute-start(bf16[432,128]{1,0:T(8,128)(2,1)} %get-tuple-element.57), channel_id=1, source_target_pairs={{0,16},{4,20},{8,24},{12,28},{16,0},{20,4},{24,8},{28,12},{1,17},{... | collective-permute-start | bytes 331784 | tf_op jit(solution)/shard_map/ppermute | solution.py:567
  84.2 6.0 %collective-permute-start.27 = (bf16[432,128]{1,0:T(8,128)(2,1)S(1)}, bf16[432,128]{1,0:T(8,128)(2,1)}, u32[]{:S(2)}, u32[]{:S(2)}) collective-permute-start(bf16[432,128]{1,0:T(8,128)(2,1)S(1)} %get-tuple-element.58), channel_id=1, source_target_pairs={{0,24},{4,28},{8,16},{12,20},{16,8},{20,12},{24,0},{28,4},{1,25},{... | collective-permute-start | bytes 331784 | tf_op jit(solution)/shard_map/ppermute | solution.py:567
  91.3 5.7 %collective-permute-start.28 = (bf16[432,128]{1,0:T(8,128)(2,1)S(1)}, bf16[432,128]{1,0:T(8,128)(2,1)S(1)}, u32[]{:S(2)}, u32[]{:S(2)}) collective-permute-start(bf16[432,128]{1,0:T(8,128)(2,1)S(1)} %multiply_convert_fusion.1.refs_0_), channel_id=1, source_target_pairs={{0,8},{4,12},{8,0},{12,4},{16,24},{20,28},{24,16},{28,20},{1,9},{5... | collective-permute-start | bytes 331784 | tf_op jit(solution)/shard_map/ppermute | solution.py:567
  94.8 7.8 %collective-permute-start.31 = (bf16[432,128]{1,0:T(8,128)(2,1)S(1)}, bf16[432,128]{1,0:T(8,128)(2,1)S(1)}, u32[]{:S(2)}, u32[]{:S(2)}) collective-permute-start(bf16[432,128]{1,0:T(8,128)(2,1)S(1)} %multiply_convert_fusion.1.refs_0_), channel_id=1, source_target_pairs={{0,4},{4,0},{8,12},{12,8},{16,20},{20,16},{24,28},{28,24},{1,5},{5... | collective-permute-start | bytes 331784 | tf_op jit(solution)/shard_map/ppermute | solution.py:567
  97.0 6.2 %collective-permute-start.32 = (bf16[432,128]{1,0:T(8,128)(2,1)S(1)}, bf16[432,128]{1,0:T(8,128)(2,1)S(1)}, u32[]{:S(2)}, u32[]{:S(2)}) collective-permute-start(bf16[432,128]{1,0:T(8,128)(2,1)S(1)} %collective-permute-done.28.refs_1_), channel_id=1, source_target_pairs={{0,4},{4,0},{8,12},{12,8},{16,20},{20,16},{24,28},{28,24},{1,5},{5... | collective-permute-start | bytes 331784 | tf_op jit(solution)/shard_map/ppermute | solution.py:567
  97.7 7.6 %collective-permute-start.33 = (bf16[432,128]{1,0:T(8,128)(2,1)S(1)}, bf16[432,128]{1,0:T(8,128)(2,1)}, u32[]{:S(2)}, u32[]{:S(2)}) collective-permute-start(bf16[432,128]{1,0:T(8,128)(2,1)S(1)} %collective-permute-done.29.refs_2_), channel_id=1, source_target_pairs={{0,4},{4,0},{8,12},{12,8},{16,20},{20,16},{24,28},{28,24},{1,5},{5... | collective-permute-start | bytes 331784 | tf_op jit(solution)/shard_map/ppermute | solution.py:567
  99.0 6.3 %collective-permute-start.34 = (bf16[432,128]{1,0:T(8,128)(2,1)S(1)}, bf16[432,128]{1,0:T(8,128)(2,1)}, u32[]{:S(2)}, u32[]{:S(2)}) collective-permute-start(bf16[432,128]{1,0:T(8,128)(2,1)S(1)} %collective-permute-done.30.refs_3_), channel_id=1, source_target_pairs={{0,4},{4,0},{8,12},{12,8},{16,20},{20,16},{24,28},{28,24},{1,5},{5... | collective-permute-start | bytes 331784 | tf_op jit(solution)/shard_map/ppermute | solution.py:567
  101.1 10.8 %collective-permute-start.6 = (bf16[864,128]{1,0:T(8,128)(2,1)S(1)}, bf16[864,128]{1,0:T(8,128)(2,1)S(1)}, u32[]{:S(2)}, u32[]{:S(2)}) collective-permute-start(bf16[864,128]{1,0:T(8,128)(2,1)S(1)} %get-tuple-element.43), channel_id=1, source_target_pairs={{0,8},{4,12},{8,0},{12,4},{16,24},{20,28},{24,16},{28,20},{1,9},{5... | collective-permute-start | bytes 663560 | tf_op jit(solution)/shard_map/ppermute | solution.py:567
  102.6 12.3 %collective-permute-start.7 = (bf16[864,128]{1,0:T(8,128)(2,1)S(1)}, bf16[864,128]{1,0:T(8,128)(2,1)S(1)}, u32[]{:S(2)}, u32[]{:S(2)}) collective-permute-start(bf16[864,128]{1,0:T(8,128)(2,1)S(1)} %get-tuple-element.44), channel_id=1, source_target_pairs={{0,16},{4,20},{8,24},{12,28},{16,0},{20,4},{24,8},{28,12},{1,17},{... | collective-permute-start | bytes 663560 | tf_op jit(solution)/shard_map/ppermute | solution.py:567
  103.9 11.0 %collective-permute-start.8 = (bf16[864,128]{1,0:T(8,128)(2,1)S(1)}, bf16[864,128]{1,0:T(8,128)(2,1)S(1)}, u32[]{:S(2)}, u32[]{:S(2)}) collective-permute-start(bf16[864,128]{1,0:T(8,128)(2,1)S(1)} %get-tuple-element.45), channel_id=1, source_target_pairs={{0,24},{4,28},{8,16},{12,20},{16,8},{20,12},{24,0},{28,4},{1,25},{... | collective-permute-start | bytes 663560 | tf_op jit(solution)/shard_map/ppermute | solution.py:567
  115.1 12.3 %collective-permute-start.9 = (bf16[864,128]{1,0:T(8,128)(2,1)S(1)}, bf16[864,128]{1,0:T(8,128)(2,1)S(1)}, u32[]{:S(2)}, u32[]{:S(2)}) collective-permute-start(bf16[864,128]{1,0:T(8,128)(2,1)S(1)} %multiply_convert_fusion.refs_0_), channel_id=1, source_target_pairs={{0,8},{4,12},{8,0},{12,4},{16,24},{20,28},{24,16},{28,20},{1,9},{5... | collective-permute-start | bytes 663560 | tf_op jit(solution)/shard_map/ppermute | solution.py:567
  115.7 12.1 %collective-permute-start.10 = (bf16[864,128]{1,0:T(8,128)(2,1)S(1)}, bf16[864,128]{1,0:T(8,128)(2,1)S(1)}, u32[]{:S(2)}, u32[]{:S(2)}) collective-permute-start(bf16[864,128]{1,0:T(8,128)(2,1)S(1)} %multiply_convert_fusion.refs_0_), channel_id=1, source_target_pairs={{0,16},{4,20},{8,24},{12,28},{16,0},{20,4},{24,8},{28,12},{1,17},{... | collective-permute-start | bytes 663560 | tf_op jit(solution)/shard_map/ppermute | solution.py:567
  117.1 10.8 %collective-permute-start.11 = (bf16[864,128]{1,0:T(8,128)(2,1)S(1)}, bf16[864,128]{1,0:T(8,128)(2,1)S(1)}, u32[]{:S(2)}, u32[]{:S(2)}) collective-permute-start(bf16[864,128]{1,0:T(8,128)(2,1)S(1)} %multiply_convert_fusion.refs_0_), channel_id=1, source_target_pairs={{0,24},{4,28},{8,16},{12,20},{16,8},{20,12},{24,0},{28,4},{1,25},{... | collective-permute-start | bytes 663560 | tf_op jit(solution)/shard_map/ppermute | solution.py:567
  118.6 8.7 %collective-permute-start.36 = (bf16[216,256]{1,0:T(8,128)(2,1)S(1)}, bf16[216,256]{1,0:T(8,128)(2,1)S(1)}, u32[]{:S(2)}, u32[]{:S(2)}) collective-permute-start(bf16[216,256]{1,0:T(8,128)(2,1)S(1)} %get-tuple-element.61), channel_id=1, source_target_pairs={{0,2},{1,3},{2,0},{3,1},{4,6},{5,7},{6,4},{7,5},{8,10},{9,11},{10,... | collective-permute-start | bytes 331784 | tf_op jit(solution)/shard_map/ppermute | solution.py:621
  122.6 6.6 %collective-permute-start.37 = (bf16[216,256]{1,0:T(8,128)(2,1)S(1)}, bf16[216,256]{1,0:T(8,128)(2,1)S(1)}, u32[]{:S(2)}, u32[]{:S(2)}) collective-permute-start(bf16[216,256]{1,0:T(8,128)(2,1)S(1)} %get-tuple-element.62), channel_id=1, source_target_pairs={{0,3},{1,2},{2,1},{3,0},{4,7},{5,6},{6,5},{7,4},{8,11},{9,10},{10,... | collective-permute-start | bytes 331784 | tf_op jit(solution)/shard_map/ppermute | solution.py:621
  140.2 17.1 %collective-permute-start.16 = (bf16[432,256]{1,0:T(8,128)(2,1)S(1)}, bf16[432,256]{1,0:T(8,128)(2,1)S(1)}, u32[]{:S(2)}, u32[]{:S(2)}) collective-permute-start(bf16[432,256]{1,0:T(8,128)(2,1)S(1)} %get-tuple-element.47), channel_id=1, source_target_pairs={{0,1},{1,0},{2,3},{3,2},{4,5},{5,4},{6,7},{7,6},{8,9},{9,8},{10,11... | collective-permute-start | bytes 663560 | tf_op jit(solution)/shard_map/ppermute | solution.py:621
  141.3 18.7 %collective-permute-start.17 = (bf16[432,256]{1,0:T(8,128)(2,1)S(1)}, bf16[432,256]{1,0:T(8,128)(2,1)S(1)}, u32[]{:S(2)}, u32[]{:S(2)}) collective-permute-start(bf16[432,256]{1,0:T(8,128)(2,1)S(1)} %get-tuple-element.48), channel_id=1, source_target_pairs={{0,2},{1,3},{2,0},{3,1},{4,6},{5,7},{6,4},{7,5},{8,10},{9,11},{10,... | collective-permute-start | bytes 663560 | tf_op jit(solution)/shard_map/ppermute | solution.py:621
  142.7 17.3 %collective-permute-start.18 = (bf16[432,256]{1,0:T(8,128)(2,1)S(1)}, bf16[432,256]{1,0:T(8,128)(2,1)S(1)}, u32[]{:S(2)}, u32[]{:S(2)}) collective-permute-start(bf16[432,256]{1,0:T(8,128)(2,1)S(1)} %get-tuple-element.49), channel_id=1, source_target_pairs={{0,3},{1,2},{2,1},{3,0},{4,7},{5,6},{6,5},{7,4},{8,11},{9,10},{10,... | collective-permute-start | bytes 663560 | tf_op jit(solution)/shard_map/ppermute | solution.py:621
  (36 other events, 223.4 us)

commit v3 on v2

--- a/solution.py
+++ b/solution.py
@@ -395,7 +395,7 @@
                 out[:, cols] = flat[pl.ds(at, share), :].astype(out.dtype)
 
 
-def cotangent_part(meta, w_parts, groups, kernel, places, parts):
+def cotangent_part(meta, w_parts, groups, kernel, places, parts, rows_space):
     channels, filters = kernel.shape[1:]
     rows = 2 * w_parts[0].shape[0]
     return pl.pallas_call(
@@ -406,7 +406,7 @@
             in_specs=[pl.BlockSpec(memory_space=pl.ANY)] * len(w_parts)
             + [pl.BlockSpec((3, channels, filters), lambda t, m: (t, 0, 0))],
             out_specs=[pl.BlockSpec((rows // parts, channels), lambda t, m: (0, 0))] * parts
-            + [pl.BlockSpec(memory_space=pltpu.HBM)],
+            + [pl.BlockSpec(memory_space=rows_space)],
             scratch_shapes=[
                 pltpu.VMEM((rows, filters), jnp.bfloat16),
                 views_shape(len(groups), filters),
@@ -419,7 +419,7 @@
             jax.ShapeDtypeStruct((rows // parts, channels), jnp.bfloat16 if m else jnp.float32)
             for m in range(parts)
         ]
-        + [pltpu.HBM((rows, filters), jnp.bfloat16)],
+        + [rows_space((rows, filters), jnp.bfloat16)],
         cost_estimate=pl.CostEstimate(
             flops=18 * rows * channels * filters,
             bytes_accessed=18 * channels * filters,
@@ -542,7 +542,13 @@
         jnp.asarray(table, jnp.int32), z * across + me, 0, keepdims=False
     )
 
-    mixed = sort_call(mix_kernel, chunks, [activations.T, act_tangent.T], pixels, 2 * own)
+    mixed = sort_call(
+        mix_kernel,
+        chunks,
+        [pltpu.with_memory_space_constraint(x.T, pltpu.HBM) for x in (activations, act_tangent)],
+        pixels,
+        2 * own,
+    )
 
     packed = pack(slope, curvature)
     packed = lax.all_to_all(packed, "chan", 0, 0, tiled=True)
@@ -598,13 +604,15 @@
             mine = mine + swap(part, 2 * (m + 1)).astype(jnp.float32)
         return mine
 
-    def weighted(mine, factor):
+    def weighted(mine, factor, c):
         rows = mine.shape[0]
         factor = lax.dynamic_slice_in_dim(factor, half * rows, rows, axis=0)
         w = weigh(factor[:, :LANES], factor[:, LANES:], mine)
         parts = [w] + [swap(w, 2 * m) for m in range(1, chips)]
         parts += [swap(part, 1) for part in parts]
-        return [pltpu.with_memory_space_constraint(part, pltpu.HBM) for part in parts]
+        if c == 0:
+            parts = [pltpu.with_memory_space_constraint(part, pltpu.HBM) for part in parts]
+        return parts
 
     def places_of(groups):
         strip_rows = GROUP // EIGHT
@@ -625,11 +633,11 @@
     got = [gathered(x) for x in mixed]
     sums, xts = zip(*[tangents(c) for c in range(2)])
     mine = [exchange(*sums[c]) for c in range(2)]
-    w = [weighted(mine[c], factors[c]) for c in range(2)]
+    w = [weighted(mine[c], factors[c], c) for c in range(2)]
     cots, whole = [], []
     kernel_hbm = pltpu.with_memory_space_constraint(kernel, pltpu.HBM)
     for c, place in enumerate([places_of(groups) for groups in chunks]):
-        own_part, *parts, rows = cotangent_part(meta, w[c], chunks[c], kernel_hbm, place, depth)
+        own_part, *parts, rows = cotangent_part(meta, w[c], chunks[c], kernel_hbm, place, depth, (pltpu.HBM, pltpu.VMEM)[c])
         cots.append(spread(own_part, parts))
         whole.append(rows)
     scale = float(1.0 / (float(pixels) ** 0.5))

time: 162 us -> 165 us (1.019)
  local copies, waits for them, and re-layouts: 7.94 us -> 10.2 us
  waiting for transfers between devices: 44.4 us -> 42.4 us
    ppermute x22, waiting for transfers between devices: 12.6 us -> 9.85 us  [swap(): return lax.ppermute(x, 'chan', [(i, i ^ bit) for i in range(across)])]
    unnamed x58 -> x56, local copies, waits for them, and re-layouts: 7.24 us -> 9.45 us
  transfers between devices with their start and end apart: 39 -> 39, of which waited for: 13 -> 13; matrix products, arithmetic and copies ran while one was open for 1% -> 1% of each run, Pallas kernels for 35% -> 34%
where the time goes in v3:
time: 165 us; the launch traced here: 163 us
  Pallas kernels  67.4 us (41%)
  waiting for transfers between devices  42.4 us (26%)
  starting transfers between devices  39 us (24%)
  local copies, waits for them, and re-layouts  10.2 us (6%)
  other arithmetic  3.25 us (2%)
    pallas_call x5, Pallas kernels, tangent(): pl.pallas_call(functools.partial(tangent_kernel, groups, sources, slots,...  32.5 us
    ppermute x10, waiting for transfers between devices, gathered(): now[link] = lax.ppermute(last[1 - link], 'filt', pairs)  23.3 us
    pallas_call x2, Pallas kernels, cotangent_part(): pl.pallas_call(functools.partial(cotangent_kernel, groups, places, parts)...  15.9 us
    ppermute x22, starting transfers between devices, swap(): return lax.ppermute(x, 'chan', [(i, i ^ bit) for i in range(across)])  15.8 us
    pallas_call x1, Pallas kernels, product_of(): pl.pallas_call(functools.partial(product_kernel, own, counts, [len(chunk)...  11.2 us
    ppermute x10, starting transfers between devices, gathered(): now[link] = lax.ppermute(last[1 - link], 'filt', pairs)  10.9 us
    ppermute x22, waiting for transfers between devices, swap(): return lax.ppermute(x, 'chan', [(i, i ^ bit) for i in range(across)])  9.85 us
    unnamed x56, local copies, waits for them, and re-layouts  9.45 us
  transfers between devices with their start and end apart: 39, of which 13 were waited for; matrix products, arithmetic and copies ran while one was open for 1% of the time, Pallas kernels for 34%

profile of v3, /device:TPU:0, one launch (start us, length us, event | category | flops | bytes accessed | tf_op | source)
XLA Modules:
  0.0 163.2 jit_solution(1933632222209134433)
XLA Ops:
  0.6 2.2 %shard_map.87 = (bf16[1728,128]{1,0:T(8,128)(2,1)S(1)}, bf16[864,128]{1,0:T(8,128)(2,1)}) custom-call(bf16[64,2592]{1,0:T(8,128)(2,1)} %bitcast.4, bf16[64,2592]{1,0:T(8,128)(2,1)} %bitcast.5), custom_call_target="tpu_custom_call" | custom-call | tf_op jit(solution)/shard_map/pallas_call | solution.py:122
  2.9 3.1 %collective-permute-start = (bf16[1728,128]{1,0:T(8,128)(2,1)S(1)}, bf16[1728,128]{1,0:T(8,128)(2,1)S(1)}, u32[]{:S(2)}, u32[]{:S(2)}) collective-permute-start(bf16[1728,128]{1,0:T(8,128)(2,1)S(1)} %get-tuple-element.37.refs_0_), channel_id=1, source_target_pairs={{0,1},{1,0},{2,3},{3,2},{4,5},{5,4},{6,7},{7,6},{8,9},{9,8},{10,11... | collective-permute-start | bytes 1327112 | tf_op jit(solution)/shard_map/ppermute | solution.py:567
  6.6 10.3 %collective-permute-done.refs_1_ = bf16[1728,128]{1,0:T(8,128)(2,1)S(1)} collective-permute-done((bf16[1728,128]{1,0:T(8,128)(2,1)S(1)}, bf16[1728,128]{1,0:T(8,128)(2,1)S(1)}, u32[]{:S(2)}, u32[]{:S(2)}) %collective-permute-start) | collective-permute-done | bytes 442400 | tf_op jit(solution)/shard_map/ppermute | solution.py:567
  21.5 4.2 %all-to-all-start = ((bf16[8,672,128]{2,1,0:T(8,128)(2,1)}), bf16[8,672,128]{2,1,0:T(8,128)(2,1)S(1)}, u32[]{:S(2)}, u32[]{:S(2)}) async-start(bf16[8,672,128]{2,1,0:T(8,128)(2,1)} %pack.1), calls=%async_computation | async-start | bytes 2752512 | tf_op jit(solution)/shard_map/all_to_all | solution.py:554
  28.4 7.0 %tangent.8 = (f32[864,512]{1,0:T(8,128)S(1)}, bf16[128,864]{1,0:T(8,128)(2,1)}) custom-call(s32[7]{0:T(128)S(1)} %fusion.meta, bf16[864,128]{1,0:T(8,128)(2,1)} %get-tuple-element.51.refs_0_, bf16[864,128]{1,0:T(8,128)(2,1)} %collective-permute-done.21.refs_1_, bf16[9,256,512]{2,1,0:T(8,128)(2,1)} %refs_4_.1, bf16[9,256,512]{2,1,0:T(8,128)(2,1)} %refs_8_.3), custom_call_target="tpu_custom_call" | custom-call | flops 2038431744 | bytes 4718592 | tf_op jit(solution)/shard_map/tangent/pallas_call | solution.py:289
  39.3 9.0 %tangent.5 = (f32[1728,512]{1,0:T(8,128)S(1)}, bf16[128,1728]{1,0:T(8,128)(2,1)}) custom-call(s32[7]{0:T(128)S(1)} %fusion.meta, bf16[1728,128]{1,0:T(8,128)(2,1)S(1)} %get-tuple-element.37.refs_0_, bf16[1728,128]{1,0:T(8,128)(2,1)S(1)} %collective-permute-done.refs_1_, bf16[9,256,512]{2,1,0:T(8,128)(2,1)} %refs_4_.1, bf16[9,256,512]{2,1,0:T(8,128)(2,1)} %refs_8_.3), custom_call_target="tpu_custom_call" | custom-call | flops 4076863488 | bytes 4718592 | tf_op jit(solution)/shard_map/tangent/pallas_call | solution.py:289
  48.3 13.0 %collective-permute-done.23.refs_3_ = bf16[864,128]{1,0:T(8,128)(2,1)S(1)} collective-permute-done((bf16[864,128]{1,0:T(8,128)(2,1)S(1)}, bf16[864,128]{1,0:T(8,128)(2,1)S(1)}, u32[]{:S(2)}, u32[]{:S(2)}) %collective-permute-start.23) | collective-permute-done | bytes 221216 | tf_op jit(solution)/shard_map/ppermute | solution.py:567
  61.3 6.0 %tangent.9 = (bf16[432,512]{1,0:T(8,128)(2,1)S(1)}, f32[432,512]{1,0:T(8,128)S(1)}, bf16[128,864]{1,0:T(8,128)(2,1)}) custom-call(s32[7]{0:T(128)S(1)} %fusion.meta, bf16[864,128]{1,0:T(8,128)(2,1)S(1)} %collective-permute-done.19.refs_0_, bf16[864,128]{1,0:T(8,128)(2,1)S(1)} %collective-permute-done.20.refs_1_, ...), custom_call_target="tpu_custom_call" | custom-call | flops 2038431744 | bytes 4718592 | tf_op jit(solution)/shard_map/tangent/pallas_call | solution.py:289
  67.4 4.7 %tangent.6 = (f32[1728,512]{1,0:T(8,128)S(1)}, bf16[64,1728]{1,0:T(8,128)(2,1)}) custom-call(s32[7]{0:T(128)S(1)} %fusion.meta, bf16[1728,128]{1,0:T(8,128)(2,1)S(1)} %collective-permute-done.3.refs_0_, bf16[1728,128]{1,0:T(8,128)(2,1)S(1)} %collective-permute-done.4.refs_1_, bf16[9,256,512]{2,1,0:T(8,128)(2,1)} %refs_4_.1, bf16[9,256,512]{2,1,0:T(8,128)(2,1)} %refs_8_.3, ...), custom_call_target="tpu_custom_call" | custom-call | flops 2038431744 | bytes 4718592 | tf_op jit(solution)/shard_map/tangent/pallas_call | solution.py:289
  72.1 5.8 %tangent.7 = (bf16[864,512]{1,0:T(8,128)(2,1)}, f32[864,512]{1,0:T(8,128)S(1)}, bf16[64,1728]{1,0:T(8,128)(2,1)}) custom-call(s32[7]{0:T(128)S(1)} %fusion.meta, bf16[1728,128]{1,0:T(8,128)(2,1)S(1)} %copy-done.1, bf16[1728,128]{1,0:T(8,128)(2,1)S(1)} %collective-permute-done.2.refs_1_, bf16[9,256,512]{2,1,0:T(8,128)(2,1)} %refs_4_.1, ...), custom_call_target="tpu_custom_call" | custom-call | flops 2038431744 | bytes 4718592 | tf_op jit(solution)/shard_map/tangent/pallas_call | solution.py:289
  78.5 1.4 split.3
  79.9 2.0 %collective-permute-start.25 = (bf16[432,128]{1,0:T(8,128)(2,1)}, bf16[432,128]{1,0:T(8,128)(2,1)}, u32[]{:S(2)}, u32[]{:S(2)}) collective-permute-start(bf16[432,128]{1,0:T(8,128)(2,1)} %get-tuple-element.56), channel_id=1, source_target_pairs={{0,8},{4,12},{8,0},{12,4},{16,24},{20,28},{24,16},{28,20},{1,9},{5... | collective-permute-start | bytes 331784 | tf_op jit(solution)/shard_map/ppermute | solution.py:573
  81.9 1.5 collective-permute-start.26
  84.2 1.4 collective-permute-done.25
  85.6 3.7 %collective-permute-done.26 = bf16[432,128]{1,0:T(8,128)(2,1)} collective-permute-done((bf16[432,128]{1,0:T(8,128)(2,1)}, bf16[432,128]{1,0:T(8,128)(2,1)}, u32[]{:S(2)}, u32[]{:S(2)}) %collective-permute-start.26) | collective-permute-done | bytes 110624 | tf_op jit(solution)/shard_map/ppermute | solution.py:573
  92.5 1.5 collective-permute-start.30
  94.0 2.2 %collective-permute-done.28.refs_1_ = bf16[432,128]{1,0:T(8,128)(2,1)S(1)} collective-permute-done((bf16[432,128]{1,0:T(8,128)(2,1)S(1)}, bf16[432,128]{1,0:T(8,128)(2,1)S(1)}, u32[]{:S(2)}, u32[]{:S(2)}) %collective-permute-start.28) | collective-permute-done | bytes 110624 | tf_op jit(solution)/shard_map/ppermute | solution.py:573
  98.1 2.1 %split.2 = (f32[864,128]{1,0:T(8,128)S(1)}, bf16[864,128]{1,0:T(8,128)(2,1)S(1)}, bf16[864,128]{1,0:T(8,128)(2,1)S(1)}, bf16[864,128]{1,0:T(8,128)(2,1)S(1)}) custom-call(s32[7]{0:T(128)S(1)} %fusion.meta, f32[864,512]{1,0:T(8,128)S(1)} %get-tuple-element.40.keep_ref, bf16[864,512]{1,0:T(8,128)(2,1)} %collective-permute-done.5.got_ref), custom_call_target="tpu_custom_call" | custom-call | flops 442368 | bytes 3538944 | tf_op jit(solution)/shard_map/split/pallas_call | solution.py:333
  100.2 1.5 collective-permute-start.6
  103.6 1.4 collective-permute-start.8
  108.7 6.6 %cotangent.3 = (f32[216,256]{1,0:T(8,128)S(1)}, bf16[216,256]{1,0:T(8,128)(2,1)S(1)}, bf16[216,256]{1,0:T(8,128)(2,1)S(1)}, bf16[216,256]{1,0:T(8,128)(2,1)S(1)}, bf16[864,512]{1,0:T(8,128)(2,1)S(1)}) custom-call(s32[7]{0:T(128)S(1)} %fusion.meta, bf16[432,128]{1,0:T(8,128)(2,1)S(1)} %multiply_convert_fusion.1.refs_0_, ...), custom_call_target="tpu_custom_call" | custom-call | flops 2038431744 | bytes 2359296 | tf_op jit(solution)/shard_map/cotangent/pallas_call | solution.py:401
  116.5 1.5 collective-permute-start.9
  118.6 1.4 collective-permute-start.11
  120.1 2.1 %collective-permute-start.36 = (bf16[216,256]{1,0:T(8,128)(2,1)S(1)}, bf16[216,256]{1,0:T(8,128)(2,1)S(1)}, u32[]{:S(2)}, u32[]{:S(2)}) collective-permute-start(bf16[216,256]{1,0:T(8,128)(2,1)S(1)} %get-tuple-element.61), channel_id=1, source_target_pairs={{0,2},{1,3},{2,0},{3,1},{4,6},{5,7},{6,4},{7,5},{8,10},{9,11},{10,... | collective-permute-start | bytes 331784 | tf_op jit(solution)/shard_map/ppermute | solution.py:629
  122.2 2.4 %collective-permute-done.35 = bf16[216,256]{1,0:T(8,128)(2,1)S(1)} collective-permute-done((bf16[216,256]{1,0:T(8,128)(2,1)S(1)}, bf16[216,256]{1,0:T(8,128)(2,1)S(1)}, u32[]{:S(2)}, u32[]{:S(2)}) %collective-permute-start.35) | collective-permute-done | bytes 110624 | tf_op jit(solution)/shard_map/ppermute | solution.py:629
  124.6 1.6 collective-permute-start.37
  126.1 3.4 %collective-permute-done.36 = bf16[216,256]{1,0:T(8,128)(2,1)S(1)} collective-permute-done((bf16[216,256]{1,0:T(8,128)(2,1)S(1)}, bf16[216,256]{1,0:T(8,128)(2,1)S(1)}, u32[]{:S(2)}, u32[]{:S(2)}) %collective-permute-start.36) | collective-permute-done | bytes 110624 | tf_op jit(solution)/shard_map/ppermute | solution.py:629
  133.0 9.3 %cotangent.2 = (f32[432,256]{1,0:T(8,128)S(1)}, bf16[432,256]{1,0:T(8,128)(2,1)S(1)}, bf16[432,256]{1,0:T(8,128)(2,1)S(1)}, bf16[432,256]{1,0:T(8,128)(2,1)S(1)}, bf16[1728,512]{1,0:T(8,128)(2,1)}) custom-call(s32[7]{0:T(128)S(1)} %fusion.meta, bf16[864,128]{1,0:T(8,128)(2,1)} %copy-done.20, bf16[864,128]{1,0:T(8,128)(2,1)} %copy-done.21, ...), custom_call_target="tpu_custom_call" | custom-call | flops 4076863488 | bytes 2359296 | tf_op jit(solution)/shard_map/cotangent/pallas_call | solution.py:401
  144.6 2.3 %collective-permute-start.18 = (bf16[432,256]{1,0:T(8,128)(2,1)S(1)}, bf16[432,256]{1,0:T(8,128)(2,1)S(1)}, u32[]{:S(2)}, u32[]{:S(2)}) collective-permute-start(bf16[432,256]{1,0:T(8,128)(2,1)S(1)} %get-tuple-element.49), channel_id=1, source_target_pairs={{0,3},{1,2},{2,1},{3,0},{4,7},{5,6},{6,5},{7,4},{8,11},{9,10},{10,... | collective-permute-start | bytes 663560 | tf_op jit(solution)/shard_map/ppermute | solution.py:629
  146.9 1.5 copy-done.18
  148.3 11.2 %product.1 = f32[9,256,512]{2,1,0:T(8,128)} custom-call(s32[7]{0:T(128)S(1)} %fusion.meta, bf16[1728,512]{1,0:T(8,128)(2,1)S(1)} %copy-done.18, bf16[128,1728]{1,0:T(8,128)(2,1)S(1)} %copy-done.19, bf16[64,1728]{1,0:T(8,128)(2,1)S(1)} %copy-done.6, bf16[64,1728]{1,0:T(8,128)(2,1)S(1)} %copy-done.7, bf16[864,512]{1,0:T(8,128)(2,1)S(1)} %get-tuple-element.67.refs_4_, ...), custom_call_target="tpu_custom_call" | custom-call | flops 6115295232 | bytes 4718592 | tf_op jit(solution)/shard_map/product/pallas_call | solution.py:470
  159.5 2.7 %collective-permute-done.17 = bf16[432,256]{1,0:T(8,128)(2,1)S(1)} collective-permute-done((bf16[432,256]{1,0:T(8,128)(2,1)S(1)}, bf16[432,256]{1,0:T(8,128)(2,1)S(1)}, u32[]{:S(2)}, u32[]{:S(2)}) %collective-permute-start.17) | collective-permute-done | bytes 221216 | tf_op jit(solution)/shard_map/ppermute | solution.py:629
  (121 shorter events, 32.3 us)
Async XLA Ops:
  2.9 14.1 %collective-permute-start = (bf16[1728,128]{1,0:T(8,128)(2,1)S(1)}, bf16[1728,128]{1,0:T(8,128)(2,1)S(1)}, u32[]{:S(2)}, u32[]{:S(2)}) collective-permute-start(bf16[1728,128]{1,0:T(8,128)(2,1)S(1)} %get-tuple-element.37.refs_0_), channel_id=1, source_target_pairs={{0,1},{1,0},{2,3},{3,2},{4,5},{5,4},{6,7},{7,6},{8,9},{9,8},{10,11... | collective-permute-start | bytes 1327112 | tf_op jit(solution)/shard_map/ppermute | solution.py:567
  5.9 19.8 %collective-permute-start.21 = (bf16[864,128]{1,0:T(8,128)(2,1)}, bf16[864,128]{1,0:T(8,128)(2,1)}, u32[]{:S(2)}, u32[]{:S(2)}) collective-permute-start(bf16[864,128]{1,0:T(8,128)(2,1)} %get-tuple-element.51.refs_0_), channel_id=1, source_target_pairs={{0,1},{1,0},{2,3},{3,2},{4,5},{5,4},{6,7},{7,6},{8,9},{9,8},{10,11... | collective-permute-start | bytes 663560 | tf_op jit(solution)/shard_map/ppermute | solution.py:567
  5.9 29.4 %collective-permute-start.3 = (bf16[1728,128]{1,0:T(8,128)(2,1)S(1)}, bf16[1728,128]{1,0:T(8,128)(2,1)S(1)}, u32[]{:S(2)}, u32[]{:S(2)}) collective-permute-start(bf16[1728,128]{1,0:T(8,128)(2,1)S(1)} %get-tuple-element.37.refs_0_), channel_id=1, source_target_pairs={{1,2},{2,1},{5,6},{6,5},{9,10},{10,9},{13,14},{14,13},{17,18},{18,... | collective-permute-start | bytes 1327112 | tf_op jit(solution)/shard_map/ppermute | solution.py:567
  16.9 21.0 %collective-permute-start.1 = (bf16[1728,128]{1,0:T(8,128)(2,1)S(1)}, bf16[1728,128]{1,0:T(8,128)(2,1)S(1)}, u32[]{:S(2)}, u32[]{:S(2)}) collective-permute-start(bf16[1728,128]{1,0:T(8,128)(2,1)S(1)} %collective-permute-done.refs_1_), channel_id=1, source_target_pairs={{1,2},{2,1},{5,6},{6,5},{9,10},{10,9},{13,14},{14,13},{17,18},{18,... | collective-permute-start | bytes 1327112 | tf_op jit(solution)/shard_map/ppermute | solution.py:567
  17.6 9.5 %collective-permute-start.19 = (bf16[864,128]{1,0:T(8,128)(2,1)}, bf16[864,128]{1,0:T(8,128)(2,1)S(1)}, u32[]{:S(2)}, u32[]{:S(2)}) collective-permute-start(bf16[864,128]{1,0:T(8,128)(2,1)} %get-tuple-element.51.refs_0_), channel_id=1, source_target_pairs={{1,2},{2,1},{5,6},{6,5},{9,10},{10,9},{13,14},{14,13},{17,18},{18,... | collective-permute-start | bytes 663560 | tf_op jit(solution)/shard_map/ppermute | solution.py:567
  21.5 61.8 %all-to-all-start = ((bf16[8,672,128]{2,1,0:T(8,128)(2,1)}), bf16[8,672,128]{2,1,0:T(8,128)(2,1)S(1)}, u32[]{:S(2)}, u32[]{:S(2)}) async-start(bf16[8,672,128]{2,1,0:T(8,128)(2,1)} %pack.1), calls=%async_computation | async-start | bytes 2752512 | tf_op jit(solution)/shard_map/all_to_all | solution.py:554
  25.7 11.0 %collective-permute-start.22 = (bf16[864,128]{1,0:T(8,128)(2,1)}, bf16[864,128]{1,0:T(8,128)(2,1)S(1)}, u32[]{:S(2)}, u32[]{:S(2)}) collective-permute-start(bf16[864,128]{1,0:T(8,128)(2,1)} %collective-permute-done.21.refs_1_), channel_id=1, source_target_pairs={{1,2},{2,1},{5,6},{6,5},{9,10},{10,9},{13,14},{14,13},{17,18},{18,... | collective-permute-start | bytes 663560 | tf_op jit(solution)/shard_map/ppermute | solution.py:567
  27.1 21.2 %collective-permute-start.20 = (bf16[864,128]{1,0:T(8,128)(2,1)S(1)}, bf16[864,128]{1,0:T(8,128)(2,1)S(1)}, u32[]{:S(2)}, u32[]{:S(2)}) collective-permute-start(bf16[864,128]{1,0:T(8,128)(2,1)S(1)} %collective-permute-done.19.refs_0_), channel_id=1, source_target_pairs={{1,0},{2,3},{5,4},{6,7},{9,8},{10,11},{13,12},{14,15},{17,16},{18,... | collective-permute-start | bytes 663560 | tf_op jit(solution)/shard_map/ppermute | solution.py:567
  35.4 32.0 %collective-permute-start.4 = (bf16[1728,128]{1,0:T(8,128)(2,1)S(1)}, bf16[1728,128]{1,0:T(8,128)(2,1)S(1)}, u32[]{:S(2)}, u32[]{:S(2)}) collective-permute-start(bf16[1728,128]{1,0:T(8,128)(2,1)S(1)} %collective-permute-done.3.refs_0_), channel_id=1, source_target_pairs={{1,0},{2,3},{5,4},{6,7},{9,8},{10,11},{13,12},{14,15},{17,16},{18,... | collective-permute-start | bytes 1327112 | tf_op jit(solution)/shard_map/ppermute | solution.py:567
  36.7 24.6 %collective-permute-start.23 = (bf16[864,128]{1,0:T(8,128)(2,1)S(1)}, bf16[864,128]{1,0:T(8,128)(2,1)S(1)}, u32[]{:S(2)}, u32[]{:S(2)}) collective-permute-start(bf16[864,128]{1,0:T(8,128)(2,1)S(1)} %collective-permute-done.22.refs_2_), channel_id=1, source_target_pairs={{1,0},{2,3},{5,4},{6,7},{9,8},{10,11},{13,12},{14,15},{17,16},{18,... | collective-permute-start | bytes 663560 | tf_op jit(solution)/shard_map/ppermute | solution.py:567
  38.0 34.1 %collective-permute-start.2 = (bf16[1728,128]{1,0:T(8,128)(2,1)S(1)}, bf16[1728,128]{1,0:T(8,128)(2,1)S(1)}, u32[]{:S(2)}, u32[]{:S(2)}) collective-permute-start(bf16[1728,128]{1,0:T(8,128)(2,1)S(1)} %collective-permute-done.1.refs_0_), channel_id=1, source_target_pairs={{1,0},{2,3},{5,4},{6,7},{9,8},{10,11},{13,12},{14,15},{17,16},{18,... | collective-permute-start | bytes 1327112 | tf_op jit(solution)/shard_map/ppermute | solution.py:567
  67.3 11.2 %collective-permute-start.24 = (bf16[432,512]{1,0:T(8,128)(2,1)S(1)}, bf16[432,512]{1,0:T(8,128)(2,1)S(1)}, u32[]{:S(2)}, u32[]{:S(2)}) collective-permute-start(bf16[432,512]{1,0:T(8,128)(2,1)S(1)} %get-tuple-element.54), channel_id=1, source_target_pairs={{0,4},{4,0},{8,12},{12,8},{16,20},{20,16},{24,28},{28,24},{1,5},{5... | collective-permute-start | bytes 1327112 | tf_op jit(solution)/shard_map/ppermute | solution.py:573
  78.0 20.2 %collective-permute-start.5 = (bf16[864,512]{1,0:T(8,128)(2,1)}, bf16[864,512]{1,0:T(8,128)(2,1)}, u32[]{:S(2)}, u32[]{:S(2)}) collective-permute-start(bf16[864,512]{1,0:T(8,128)(2,1)} %get-tuple-element.41), channel_id=1, source_target_pairs={{0,4},{4,0},{8,12},{12,8},{16,20},{20,16},{24,28},{28,24},{1,5},{5... | collective-permute-start | bytes 2654216 | tf_op jit(solution)/shard_map/ppermute | solution.py:573
  79.9 5.8 %collective-permute-start.25 = (bf16[432,128]{1,0:T(8,128)(2,1)}, bf16[432,128]{1,0:T(8,128)(2,1)}, u32[]{:S(2)}, u32[]{:S(2)}) collective-permute-start(bf16[432,128]{1,0:T(8,128)(2,1)} %get-tuple-element.56), channel_id=1, source_target_pairs={{0,8},{4,12},{8,0},{12,4},{16,24},{20,28},{24,16},{28,20},{1,9},{5... | collective-permute-start | bytes 331784 | tf_op jit(solution)/shard_map/ppermute | solution.py:573
  81.9 7.4 %collective-permute-start.26 = (bf16[432,128]{1,0:T(8,128)(2,1)}, bf16[432,128]{1,0:T(8,128)(2,1)}, u32[]{:S(2)}, u32[]{:S(2)}) collective-permute-start(bf16[432,128]{1,0:T(8,128)(2,1)} %get-tuple-element.57), channel_id=1, source_target_pairs={{0,16},{4,20},{8,24},{12,28},{16,0},{20,4},{24,8},{28,12},{1,17},{... | collective-permute-start | bytes 331784 | tf_op jit(solution)/shard_map/ppermute | solution.py:573
  83.3 6.0 %collective-permute-start.27 = (bf16[432,128]{1,0:T(8,128)(2,1)S(1)}, bf16[432,128]{1,0:T(8,128)(2,1)}, u32[]{:S(2)}, u32[]{:S(2)}) collective-permute-start(bf16[432,128]{1,0:T(8,128)(2,1)S(1)} %get-tuple-element.58), channel_id=1, source_target_pairs={{0,24},{4,28},{8,16},{12,20},{16,8},{20,12},{24,0},{28,4},{1,25},{... | collective-permute-start | bytes 331784 | tf_op jit(solution)/shard_map/ppermute | solution.py:573
  94.0 7.8 %collective-permute-start.31 = (bf16[432,128]{1,0:T(8,128)(2,1)S(1)}, bf16[432,128]{1,0:T(8,128)(2,1)S(1)}, u32[]{:S(2)}, u32[]{:S(2)}) collective-permute-start(bf16[432,128]{1,0:T(8,128)(2,1)S(1)} %multiply_convert_fusion.1.refs_0_), channel_id=1, source_target_pairs={{0,4},{4,0},{8,12},{12,8},{16,20},{20,16},{24,28},{28,24},{1,5},{5... | collective-permute-start | bytes 331784 | tf_op jit(solution)/shard_map/ppermute | solution.py:573
  96.2 6.8 %collective-permute-start.32 = (bf16[432,128]{1,0:T(8,128)(2,1)S(1)}, bf16[432,128]{1,0:T(8,128)(2,1)S(1)}, u32[]{:S(2)}, u32[]{:S(2)}) collective-permute-start(bf16[432,128]{1,0:T(8,128)(2,1)S(1)} %collective-permute-done.28.refs_1_), channel_id=1, source_target_pairs={{0,4},{4,0},{8,12},{12,8},{16,20},{20,16},{24,28},{28,24},{1,5},{5... | collective-permute-start | bytes 331784 | tf_op jit(solution)/shard_map/ppermute | solution.py:573
  96.8 8.2 %collective-permute-start.33 = (bf16[432,128]{1,0:T(8,128)(2,1)S(1)}, bf16[432,128]{1,0:T(8,128)(2,1)}, u32[]{:S(2)}, u32[]{:S(2)}) collective-permute-start(bf16[432,128]{1,0:T(8,128)(2,1)S(1)} %collective-permute-done.29.refs_2_), channel_id=1, source_target_pairs={{0,4},{4,0},{8,12},{12,8},{16,20},{20,16},{24,28},{28,24},{1,5},{5... | collective-permute-start | bytes 331784 | tf_op jit(solution)/shard_map/ppermute | solution.py:573
  98.1 6.9 %collective-permute-start.34 = (bf16[432,128]{1,0:T(8,128)(2,1)S(1)}, bf16[432,128]{1,0:T(8,128)(2,1)}, u32[]{:S(2)}, u32[]{:S(2)}) collective-permute-start(bf16[432,128]{1,0:T(8,128)(2,1)S(1)} %collective-permute-done.30.refs_3_), channel_id=1, source_target_pairs={{0,4},{4,0},{8,12},{12,8},{16,20},{20,16},{24,28},{28,24},{1,5},{5... | collective-permute-start | bytes 331784 | tf_op jit(solution)/shard_map/ppermute | solution.py:573
  100.2 15.1 %collective-permute-start.6 = (bf16[864,128]{1,0:T(8,128)(2,1)S(1)}, bf16[864,128]{1,0:T(8,128)(2,1)S(1)}, u32[]{:S(2)}, u32[]{:S(2)}) collective-permute-start(bf16[864,128]{1,0:T(8,128)(2,1)S(1)} %get-tuple-element.43), channel_id=1, source_target_pairs={{0,8},{4,12},{8,0},{12,4},{16,24},{20,28},{24,16},{28,20},{1,9},{5... | collective-permute-start | bytes 663560 | tf_op jit(solution)/shard_map/ppermute | solution.py:573
  102.4 13.0 %collective-permute-start.7 = (bf16[864,128]{1,0:T(8,128)(2,1)S(1)}, bf16[864,128]{1,0:T(8,128)(2,1)S(1)}, u32[]{:S(2)}, u32[]{:S(2)}) collective-permute-start(bf16[864,128]{1,0:T(8,128)(2,1)S(1)} %get-tuple-element.44), channel_id=1, source_target_pairs={{0,16},{4,20},{8,24},{12,28},{16,0},{20,4},{24,8},{28,12},{1,17},{... | collective-permute-start | bytes 663560 | tf_op jit(solution)/shard_map/ppermute | solution.py:573
  103.6 11.8 %collective-permute-start.8 = (bf16[864,128]{1,0:T(8,128)(2,1)S(1)}, bf16[864,128]{1,0:T(8,128)(2,1)}, u32[]{:S(2)}, u32[]{:S(2)}) collective-permute-start(bf16[864,128]{1,0:T(8,128)(2,1)S(1)} %get-tuple-element.45), channel_id=1, source_target_pairs={{0,24},{4,28},{8,16},{12,20},{16,8},{20,12},{24,0},{28,4},{1,25},{... | collective-permute-start | bytes 663560 | tf_op jit(solution)/shard_map/ppermute | solution.py:573
  116.5 13.0 %collective-permute-start.9 = (bf16[864,128]{1,0:T(8,128)(2,1)S(1)}, bf16[864,128]{1,0:T(8,128)(2,1)S(1)}, u32[]{:S(2)}, u32[]{:S(2)}) collective-permute-start(bf16[864,128]{1,0:T(8,128)(2,1)S(1)} %multiply_convert_fusion.refs_0_), channel_id=1, source_target_pairs={{0,8},{4,12},{8,0},{12,4},{16,24},{20,28},{24,16},{28,20},{1,9},{5... | collective-permute-start | bytes 663560 | tf_op jit(solution)/shard_map/ppermute | solution.py:573
  118.1 12.0 %collective-permute-start.10 = (bf16[864,128]{1,0:T(8,128)(2,1)S(1)}, bf16[864,128]{1,0:T(8,128)(2,1)S(1)}, u32[]{:S(2)}, u32[]{:S(2)}) collective-permute-start(bf16[864,128]{1,0:T(8,128)(2,1)S(1)} %multiply_convert_fusion.refs_0_), channel_id=1, source_target_pairs={{0,16},{4,20},{8,24},{12,28},{16,0},{20,4},{24,8},{28,12},{1,17},{... | collective-permute-start | bytes 663560 | tf_op jit(solution)/shard_map/ppermute | solution.py:573
  118.6 5.9 %collective-permute-start.35 = (bf16[216,256]{1,0:T(8,128)(2,1)S(1)}, bf16[216,256]{1,0:T(8,128)(2,1)S(1)}, u32[]{:S(2)}, u32[]{:S(2)}) collective-permute-start(bf16[216,256]{1,0:T(8,128)(2,1)S(1)} %get-tuple-element.60), channel_id=1, source_target_pairs={{0,1},{1,0},{2,3},{3,2},{4,5},{5,4},{6,7},{7,6},{8,9},{9,8},{10,11... | collective-permute-start | bytes 331784 | tf_op jit(solution)/shard_map/ppermute | solution.py:629
  118.6 11.5 %collective-permute-start.11 = (bf16[864,128]{1,0:T(8,128)(2,1)S(1)}, bf16[864,128]{1,0:T(8,128)(2,1)S(1)}, u32[]{:S(2)}, u32[]{:S(2)}) collective-permute-start(bf16[864,128]{1,0:T(8,128)(2,1)S(1)} %multiply_convert_fusion.refs_0_), channel_id=1, source_target_pairs={{0,24},{4,28},{8,16},{12,20},{16,8},{20,12},{24,0},{28,4},{1,25},{... | collective-permute-start | bytes 663560 | tf_op jit(solution)/shard_map/ppermute | solution.py:573
  120.1 9.5 %collective-permute-start.36 = (bf16[216,256]{1,0:T(8,128)(2,1)S(1)}, bf16[216,256]{1,0:T(8,128)(2,1)S(1)}, u32[]{:S(2)}, u32[]{:S(2)}) collective-permute-start(bf16[216,256]{1,0:T(8,128)(2,1)S(1)} %get-tuple-element.61), channel_id=1, source_target_pairs={{0,2},{1,3},{2,0},{3,1},{4,6},{5,7},{6,4},{7,5},{8,10},{9,11},{10,... | collective-permute-start | bytes 331784 | tf_op jit(solution)/shard_map/ppermute | solution.py:629
  124.6 6.6 %collective-permute-start.37 = (bf16[216,256]{1,0:T(8,128)(2,1)S(1)}, bf16[216,256]{1,0:T(8,128)(2,1)S(1)}, u32[]{:S(2)}, u32[]{:S(2)}) collective-permute-start(bf16[216,256]{1,0:T(8,128)(2,1)S(1)} %get-tuple-element.62), channel_id=1, source_target_pairs={{0,3},{1,2},{2,1},{3,0},{4,7},{5,6},{6,5},{7,4},{8,11},{9,10},{10,... | collective-permute-start | bytes 331784 | tf_op jit(solution)/shard_map/ppermute | solution.py:629
  142.4 17.1 %collective-permute-start.16 = (bf16[432,256]{1,0:T(8,128)(2,1)S(1)}, bf16[432,256]{1,0:T(8,128)(2,1)S(1)}, u32[]{:S(2)}, u32[]{:S(2)}) collective-permute-start(bf16[432,256]{1,0:T(8,128)(2,1)S(1)} %get-tuple-element.47), channel_id=1, source_target_pairs={{0,1},{1,0},{2,3},{3,2},{4,5},{5,4},{6,7},{7,6},{8,9},{9,8},{10,11... | collective-permute-start | bytes 663560 | tf_op jit(solution)/shard_map/ppermute | solution.py:629
  143.6 18.7 %collective-permute-start.17 = (bf16[432,256]{1,0:T(8,128)(2,1)S(1)}, bf16[432,256]{1,0:T(8,128)(2,1)S(1)}, u32[]{:S(2)}, u32[]{:S(2)}) collective-permute-start(bf16[432,256]{1,0:T(8,128)(2,1)S(1)} %get-tuple-element.48), channel_id=1, source_target_pairs={{0,2},{1,3},{2,0},{3,1},{4,6},{5,7},{6,4},{7,5},{8,10},{9,11},{10,... | collective-permute-start | bytes 663560 | tf_op jit(solution)/shard_map/ppermute | solution.py:629
  144.6 17.7 %collective-permute-start.18 = (bf16[432,256]{1,0:T(8,128)(2,1)S(1)}, bf16[432,256]{1,0:T(8,128)(2,1)S(1)}, u32[]{:S(2)}, u32[]{:S(2)}) collective-permute-start(bf16[432,256]{1,0:T(8,128)(2,1)S(1)} %get-tuple-element.49), channel_id=1, source_target_pairs={{0,3},{1,2},{2,1},{3,0},{4,7},{5,6},{6,5},{7,4},{8,11},{9,10},{10,... | collective-permute-start | bytes 663560 | tf_op jit(solution)/shard_map/ppermute | solution.py:629
  (35 other events, 188.5 us)

commit v4 on v3

--- a/solution.py
+++ b/solution.py
@@ -17,6 +17,7 @@
 EIGHT = PAIR * STRIPS
 PIECE = WW * EIGHT
 GROUP = DEEP * PIECE
+SPARE = 64
 
 INNER = 1
 PARAMS = pltpu.CompilerParams(vmem_limit_bytes=28 << 20)
@@ -100,7 +101,7 @@
 def sort_kernel(chunks, x_ref, *refs):
     outs, (flat, sorted_) = refs[: len(chunks)], refs[len(chunks) :]
     blocks, each = x_ref.shape[0], x_ref.shape[1] // 2
-    rows = flat.shape[0] // blocks
+    rows = (flat.shape[0] - SPARE) // blocks
     for kind in range(2):
         for n in range(blocks):
             block = x_ref[n, kind * each : (kind + 1) * each, :].astype(jnp.float32)
@@ -113,7 +114,7 @@
     both = jnp.concatenate(
         [a_ref[...].astype(jnp.float32), t_ref[...].astype(jnp.float32)], axis=0
     )
-    flat[...] = both.T
+    flat[pl.ds(0, both.shape[1]), :] = both.T
     sort_into(chunks, flat, sorted_, outs, pl.ds(0, LANES))
 
 
@@ -123,8 +124,8 @@
         functools.partial(kernel, chunks),
         out_shape=[jax.ShapeDtypeStruct((r, width), given[0].dtype) for r in rows],
         scratch_shapes=[
-            pltpu.VMEM((pixels, LANES), jnp.float32),
-            pltpu.VMEM((max(rows), LANES), jnp.float32),
+            pltpu.VMEM((pixels + SPARE, LANES), jnp.float32),
+            pltpu.VMEM((max(rows) + SPARE, LANES), jnp.float32),
         ],
         compiler_params=PARAMS,
     )(*given)
@@ -379,7 +380,7 @@
     )
     for n in range(acc.shape[0]):
         column = value[:, n * LANES : (n + 1) * LANES]
-        acc[n] = jnp.where(step == 0, column, acc[n] + column)
+        acc[n, : x.shape[0]] = jnp.where(step == 0, column, acc[n, : x.shape[0]] + column)
 
     @pl.when(step == 2)
     def _():
@@ -388,7 +389,7 @@
             for g, strip, deep, _, row in pieces_of(groups):
                 target = places[g, strip] + deep * WW
                 flat[pl.ds(target, WW), :] = acc[n, pl.ds(row, WW, stride=EIGHT), :]
-            share = flat.shape[0] // parts
+            share = x.shape[0] // parts
             for m, out in enumerate(outs):
                 at = pl.multiple_of((meta[PLACE] ^ m) * share, share)
                 cols = pl.ds(n * LANES, LANES)
@@ -411,8 +412,8 @@
                 pltpu.VMEM((rows, filters), jnp.bfloat16),
                 views_shape(len(groups), filters),
                 pltpu.SemaphoreType.DMA((len(w_parts) + 1,)),
-                pltpu.VMEM((channels // LANES, rows, LANES), jnp.float32),
-                pltpu.VMEM((rows, LANES), jnp.float32),
+                pltpu.VMEM((channels // LANES, rows + SPARE, LANES), jnp.float32),
+                pltpu.VMEM((rows + SPARE, LANES), jnp.float32),
             ],
         ),
         out_shape=[

time: 165 us -> 165 us (level)
  no operation moved by 1% of the time
where the time goes in v4:
time: 165 us; the launch traced here: 163 us
  Pallas kernels  67.4 us (41%)
  waiting for transfers between devices  42.4 us (26%)
  starting transfers between devices  39 us (24%)
  local copies, waits for them, and re-layouts  10.2 us (6%)
  other arithmetic  3.25 us (2%)
    pallas_call x5, Pallas kernels, tangent(): pl.pallas_call(functools.partial(tangent_kernel, groups, sources, slots,...  32.5 us
    ppermute x10, waiting for transfers between devices, gathered(): now[link] = lax.ppermute(last[1 - link], 'filt', pairs)  23.3 us
    pallas_call x2, Pallas kernels, cotangent_part(): pl.pallas_call(functools.partial(cotangent_kernel, groups, places, parts)...  15.9 us
    ppermute x22, starting transfers between devices, swap(): return lax.ppermute(x, 'chan', [(i, i ^ bit) for i in range(across)])  15.8 us
    pallas_call x1, Pallas kernels, product_of(): pl.pallas_call(functools.partial(product_kernel, own, counts, [len(chunk)...  11.2 us
    ppermute x10, starting transfers between devices, gathered(): now[link] = lax.ppermute(last[1 - link], 'filt', pairs)  10.9 us
    ppermute x22, waiting for transfers between devices, swap(): return lax.ppermute(x, 'chan', [(i, i ^ bit) for i in range(across)])  9.85 us
    unnamed x56, local copies, waits for them, and re-layouts  9.45 us
  transfers between devices with their start and end apart: 39, of which 13 were waited for; matrix products, arithmetic and copies ran while one was open for 1% of the time, Pallas kernels for 34%

profile of v4, /device:TPU:0, one launch (start us, length us, event | category | flops | bytes accessed | tf_op | source)
XLA Modules:
  0.0 163.2 jit_solution(9286355840498078719)
XLA Ops:
  0.6 2.2 %shard_map.87 = (bf16[1728,128]{1,0:T(8,128)(2,1)S(1)}, bf16[864,128]{1,0:T(8,128)(2,1)}) custom-call(bf16[64,2592]{1,0:T(8,128)(2,1)} %bitcast.4, bf16[64,2592]{1,0:T(8,128)(2,1)} %bitcast.5), custom_call_target="tpu_custom_call" | custom-call | tf_op jit(solution)/shard_map/pallas_call | solution.py:123
  2.9 3.1 %collective-permute-start = (bf16[1728,128]{1,0:T(8,128)(2,1)S(1)}, bf16[1728,128]{1,0:T(8,128)(2,1)S(1)}, u32[]{:S(2)}, u32[]{:S(2)}) collective-permute-start(bf16[1728,128]{1,0:T(8,128)(2,1)S(1)} %get-tuple-element.37.refs_0_), channel_id=1, source_target_pairs={{0,1},{1,0},{2,3},{3,2},{4,5},{5,4},{6,7},{7,6},{8,9},{9,8},{10,11... | collective-permute-start | bytes 1327112 | tf_op jit(solution)/shard_map/ppermute | solution.py:568
  6.6 10.3 %collective-permute-done.refs_1_ = bf16[1728,128]{1,0:T(8,128)(2,1)S(1)} collective-permute-done((bf16[1728,128]{1,0:T(8,128)(2,1)S(1)}, bf16[1728,128]{1,0:T(8,128)(2,1)S(1)}, u32[]{:S(2)}, u32[]{:S(2)}) %collective-permute-start) | collective-permute-done | bytes 442400 | tf_op jit(solution)/shard_map/ppermute | solution.py:568
  21.5 4.2 %all-to-all-start = ((bf16[8,672,128]{2,1,0:T(8,128)(2,1)}), bf16[8,672,128]{2,1,0:T(8,128)(2,1)S(1)}, u32[]{:S(2)}, u32[]{:S(2)}) async-start(bf16[8,672,128]{2,1,0:T(8,128)(2,1)} %pack.1), calls=%async_computation | async-start | bytes 2752512 | tf_op jit(solution)/shard_map/all_to_all | solution.py:555
  28.4 7.0 %tangent.8 = (f32[864,512]{1,0:T(8,128)S(1)}, bf16[128,864]{1,0:T(8,128)(2,1)}) custom-call(s32[7]{0:T(128)S(1)} %fusion.meta, bf16[864,128]{1,0:T(8,128)(2,1)} %get-tuple-element.51.refs_0_, bf16[864,128]{1,0:T(8,128)(2,1)} %collective-permute-done.21.refs_1_, bf16[9,256,512]{2,1,0:T(8,128)(2,1)} %refs_4_.1, bf16[9,256,512]{2,1,0:T(8,128)(2,1)} %refs_8_.3), custom_call_target="tpu_custom_call" | custom-call | flops 2038431744 | bytes 4718592 | tf_op jit(solution)/shard_map/tangent/pallas_call | solution.py:290
  39.3 9.0 %tangent.5 = (f32[1728,512]{1,0:T(8,128)S(1)}, bf16[128,1728]{1,0:T(8,128)(2,1)}) custom-call(s32[7]{0:T(128)S(1)} %fusion.meta, bf16[1728,128]{1,0:T(8,128)(2,1)S(1)} %get-tuple-element.37.refs_0_, bf16[1728,128]{1,0:T(8,128)(2,1)S(1)} %collective-permute-done.refs_1_, bf16[9,256,512]{2,1,0:T(8,128)(2,1)} %refs_4_.1, bf16[9,256,512]{2,1,0:T(8,128)(2,1)} %refs_8_.3), custom_call_target="tpu_custom_call" | custom-call | flops 4076863488 | bytes 4718592 | tf_op jit(solution)/shard_map/tangent/pallas_call | solution.py:290
  48.3 13.0 %collective-permute-done.23.refs_3_ = bf16[864,128]{1,0:T(8,128)(2,1)S(1)} collective-permute-done((bf16[864,128]{1,0:T(8,128)(2,1)S(1)}, bf16[864,128]{1,0:T(8,128)(2,1)S(1)}, u32[]{:S(2)}, u32[]{:S(2)}) %collective-permute-start.23) | collective-permute-done | bytes 221216 | tf_op jit(solution)/shard_map/ppermute | solution.py:568
  61.3 6.0 %tangent.9 = (bf16[432,512]{1,0:T(8,128)(2,1)S(1)}, f32[432,512]{1,0:T(8,128)S(1)}, bf16[128,864]{1,0:T(8,128)(2,1)}) custom-call(s32[7]{0:T(128)S(1)} %fusion.meta, bf16[864,128]{1,0:T(8,128)(2,1)S(1)} %collective-permute-done.19.refs_0_, bf16[864,128]{1,0:T(8,128)(2,1)S(1)} %collective-permute-done.20.refs_1_, ...), custom_call_target="tpu_custom_call" | custom-call | flops 2038431744 | bytes 4718592 | tf_op jit(solution)/shard_map/tangent/pallas_call | solution.py:290
  67.4 4.7 %tangent.6 = (f32[1728,512]{1,0:T(8,128)S(1)}, bf16[64,1728]{1,0:T(8,128)(2,1)}) custom-call(s32[7]{0:T(128)S(1)} %fusion.meta, bf16[1728,128]{1,0:T(8,128)(2,1)S(1)} %collective-permute-done.3.refs_0_, bf16[1728,128]{1,0:T(8,128)(2,1)S(1)} %collective-permute-done.4.refs_1_, bf16[9,256,512]{2,1,0:T(8,128)(2,1)} %refs_4_.1, bf16[9,256,512]{2,1,0:T(8,128)(2,1)} %refs_8_.3, ...), custom_call_target="tpu_custom_call" | custom-call | flops 2038431744 | bytes 4718592 | tf_op jit(solution)/shard_map/tangent/pallas_call | solution.py:290
  72.1 5.8 %tangent.7 = (bf16[864,512]{1,0:T(8,128)(2,1)}, f32[864,512]{1,0:T(8,128)S(1)}, bf16[64,1728]{1,0:T(8,128)(2,1)}) custom-call(s32[7]{0:T(128)S(1)} %fusion.meta, bf16[1728,128]{1,0:T(8,128)(2,1)S(1)} %copy-done.1, bf16[1728,128]{1,0:T(8,128)(2,1)S(1)} %collective-permute-done.2.refs_1_, bf16[9,256,512]{2,1,0:T(8,128)(2,1)} %refs_4_.1, ...), custom_call_target="tpu_custom_call" | custom-call | flops 2038431744 | bytes 4718592 | tf_op jit(solution)/shard_map/tangent/pallas_call | solution.py:290
  78.5 1.4 split.3
  79.9 2.0 %collective-permute-start.25 = (bf16[432,128]{1,0:T(8,128)(2,1)}, bf16[432,128]{1,0:T(8,128)(2,1)}, u32[]{:S(2)}, u32[]{:S(2)}) collective-permute-start(bf16[432,128]{1,0:T(8,128)(2,1)} %get-tuple-element.56), channel_id=1, source_target_pairs={{0,8},{4,12},{8,0},{12,4},{16,24},{20,28},{24,16},{28,20},{1,9},{5... | collective-permute-start | bytes 331784 | tf_op jit(solution)/shard_map/ppermute | solution.py:574
  81.9 1.5 collective-permute-start.26
  84.2 1.4 collective-permute-done.25
  85.6 3.7 %collective-permute-done.26 = bf16[432,128]{1,0:T(8,128)(2,1)} collective-permute-done((bf16[432,128]{1,0:T(8,128)(2,1)}, bf16[432,128]{1,0:T(8,128)(2,1)}, u32[]{:S(2)}, u32[]{:S(2)}) %collective-permute-start.26) | collective-permute-done | bytes 110624 | tf_op jit(solution)/shard_map/ppermute | solution.py:574
  92.5 1.5 collective-permute-start.30
  94.0 2.2 %collective-permute-done.28.refs_1_ = bf16[432,128]{1,0:T(8,128)(2,1)S(1)} collective-permute-done((bf16[432,128]{1,0:T(8,128)(2,1)S(1)}, bf16[432,128]{1,0:T(8,128)(2,1)S(1)}, u32[]{:S(2)}, u32[]{:S(2)}) %collective-permute-start.28) | collective-permute-done | bytes 110624 | tf_op jit(solution)/shard_map/ppermute | solution.py:574
  98.1 2.1 %split.2 = (f32[864,128]{1,0:T(8,128)S(1)}, bf16[864,128]{1,0:T(8,128)(2,1)S(1)}, bf16[864,128]{1,0:T(8,128)(2,1)S(1)}, bf16[864,128]{1,0:T(8,128)(2,1)S(1)}) custom-call(s32[7]{0:T(128)S(1)} %fusion.meta, f32[864,512]{1,0:T(8,128)S(1)} %get-tuple-element.40.keep_ref, bf16[864,512]{1,0:T(8,128)(2,1)} %collective-permute-done.5.got_ref), custom_call_target="tpu_custom_call" | custom-call | flops 442368 | bytes 3538944 | tf_op jit(solution)/shard_map/split/pallas_call | solution.py:334
  100.2 1.5 collective-permute-start.6
  103.6 1.4 collective-permute-start.8
  108.7 6.6 %cotangent.3 = (f32[216,256]{1,0:T(8,128)S(1)}, bf16[216,256]{1,0:T(8,128)(2,1)S(1)}, bf16[216,256]{1,0:T(8,128)(2,1)S(1)}, bf16[216,256]{1,0:T(8,128)(2,1)S(1)}, bf16[864,512]{1,0:T(8,128)(2,1)S(1)}) custom-call(s32[7]{0:T(128)S(1)} %fusion.meta, bf16[432,128]{1,0:T(8,128)(2,1)S(1)} %multiply_convert_fusion.1.refs_0_, ...), custom_call_target="tpu_custom_call" | custom-call | flops 2038431744 | bytes 2359296 | tf_op jit(solution)/shard_map/cotangent/pallas_call | solution.py:402
  116.5 1.5 collective-permute-start.9
  118.6 1.4 collective-permute-start.11
  120.1 2.1 %collective-permute-start.36 = (bf16[216,256]{1,0:T(8,128)(2,1)S(1)}, bf16[216,256]{1,0:T(8,128)(2,1)S(1)}, u32[]{:S(2)}, u32[]{:S(2)}) collective-permute-start(bf16[216,256]{1,0:T(8,128)(2,1)S(1)} %get-tuple-element.61), channel_id=1, source_target_pairs={{0,2},{1,3},{2,0},{3,1},{4,6},{5,7},{6,4},{7,5},{8,10},{9,11},{10,... | collective-permute-start | bytes 331784 | tf_op jit(solution)/shard_map/ppermute | solution.py:630
  122.2 2.4 %collective-permute-done.35 = bf16[216,256]{1,0:T(8,128)(2,1)S(1)} collective-permute-done((bf16[216,256]{1,0:T(8,128)(2,1)S(1)}, bf16[216,256]{1,0:T(8,128)(2,1)S(1)}, u32[]{:S(2)}, u32[]{:S(2)}) %collective-permute-start.35) | collective-permute-done | bytes 110624 | tf_op jit(solution)/shard_map/ppermute | solution.py:630
  124.6 1.6 collective-permute-start.37
  126.1 3.4 %collective-permute-done.36 = bf16[216,256]{1,0:T(8,128)(2,1)S(1)} collective-permute-done((bf16[216,256]{1,0:T(8,128)(2,1)S(1)}, bf16[216,256]{1,0:T(8,128)(2,1)S(1)}, u32[]{:S(2)}, u32[]{:S(2)}) %collective-permute-start.36) | collective-permute-done | bytes 110624 | tf_op jit(solution)/shard_map/ppermute | solution.py:630
  133.0 9.3 %cotangent.2 = (f32[432,256]{1,0:T(8,128)S(1)}, bf16[432,256]{1,0:T(8,128)(2,1)S(1)}, bf16[432,256]{1,0:T(8,128)(2,1)S(1)}, bf16[432,256]{1,0:T(8,128)(2,1)S(1)}, bf16[1728,512]{1,0:T(8,128)(2,1)}) custom-call(s32[7]{0:T(128)S(1)} %fusion.meta, bf16[864,128]{1,0:T(8,128)(2,1)} %copy-done.20, bf16[864,128]{1,0:T(8,128)(2,1)} %copy-done.21, ...), custom_call_target="tpu_custom_call" | custom-call | flops 4076863488 | bytes 2359296 | tf_op jit(solution)/shard_map/cotangent/pallas_call | solution.py:402
  144.6 2.3 %collective-permute-start.18 = (bf16[432,256]{1,0:T(8,128)(2,1)S(1)}, bf16[432,256]{1,0:T(8,128)(2,1)S(1)}, u32[]{:S(2)}, u32[]{:S(2)}) collective-permute-start(bf16[432,256]{1,0:T(8,128)(2,1)S(1)} %get-tuple-element.49), channel_id=1, source_target_pairs={{0,3},{1,2},{2,1},{3,0},{4,7},{5,6},{6,5},{7,4},{8,11},{9,10},{10,... | collective-permute-start | bytes 663560 | tf_op jit(solution)/shard_map/ppermute | solution.py:630
  146.9 1.5 copy-done.18
  148.3 11.2 %product.1 = f32[9,256,512]{2,1,0:T(8,128)} custom-call(s32[7]{0:T(128)S(1)} %fusion.meta, bf16[1728,512]{1,0:T(8,128)(2,1)S(1)} %copy-done.18, bf16[128,1728]{1,0:T(8,128)(2,1)S(1)} %copy-done.19, bf16[64,1728]{1,0:T(8,128)(2,1)S(1)} %copy-done.6, bf16[64,1728]{1,0:T(8,128)(2,1)S(1)} %copy-done.7, bf16[864,512]{1,0:T(8,128)(2,1)S(1)} %get-tuple-element.67.refs_4_, ...), custom_call_target="tpu_custom_call" | custom-call | flops 6115295232 | bytes 4718592 | tf_op jit(solution)/shard_map/product/pallas_call | solution.py:471
  159.5 2.7 %collective-permute-done.17 = bf16[432,256]{1,0:T(8,128)(2,1)S(1)} collective-permute-done((bf16[432,256]{1,0:T(8,128)(2,1)S(1)}, bf16[432,256]{1,0:T(8,128)(2,1)S(1)}, u32[]{:S(2)}, u32[]{:S(2)}) %collective-permute-start.17) | collective-permute-done | bytes 221216 | tf_op jit(solution)/shard_map/ppermute | solution.py:630
  (121 shorter events, 32.3 us)
Async XLA Ops:
  2.9 14.1 %collective-permute-start = (bf16[1728,128]{1,0:T(8,128)(2,1)S(1)}, bf16[1728,128]{1,0:T(8,128)(2,1)S(1)}, u32[]{:S(2)}, u32[]{:S(2)}) collective-permute-start(bf16[1728,128]{1,0:T(8,128)(2,1)S(1)} %get-tuple-element.37.refs_0_), channel_id=1, source_target_pairs={{0,1},{1,0},{2,3},{3,2},{4,5},{5,4},{6,7},{7,6},{8,9},{9,8},{10,11... | collective-permute-start | bytes 1327112 | tf_op jit(solution)/shard_map/ppermute | solution.py:568
  5.9 19.8 %collective-permute-start.21 = (bf16[864,128]{1,0:T(8,128)(2,1)}, bf16[864,128]{1,0:T(8,128)(2,1)}, u32[]{:S(2)}, u32[]{:S(2)}) collective-permute-start(bf16[864,128]{1,0:T(8,128)(2,1)} %get-tuple-element.51.refs_0_), channel_id=1, source_target_pairs={{0,1},{1,0},{2,3},{3,2},{4,5},{5,4},{6,7},{7,6},{8,9},{9,8},{10,11... | collective-permute-start | bytes 663560 | tf_op jit(solution)/shard_map/ppermute | solution.py:568
  5.9 29.4 %collective-permute-start.3 = (bf16[1728,128]{1,0:T(8,128)(2,1)S(1)}, bf16[1728,128]{1,0:T(8,128)(2,1)S(1)}, u32[]{:S(2)}, u32[]{:S(2)}) collective-permute-start(bf16[1728,128]{1,0:T(8,128)(2,1)S(1)} %get-tuple-element.37.refs_0_), channel_id=1, source_target_pairs={{1,2},{2,1},{5,6},{6,5},{9,10},{10,9},{13,14},{14,13},{17,18},{18,... | collective-permute-start | bytes 1327112 | tf_op jit(solution)/shard_map/ppermute | solution.py:568
  16.9 21.0 %collective-permute-start.1 = (bf16[1728,128]{1,0:T(8,128)(2,1)S(1)}, bf16[1728,128]{1,0:T(8,128)(2,1)S(1)}, u32[]{:S(2)}, u32[]{:S(2)}) collective-permute-start(bf16[1728,128]{1,0:T(8,128)(2,1)S(1)} %collective-permute-done.refs_1_), channel_id=1, source_target_pairs={{1,2},{2,1},{5,6},{6,5},{9,10},{10,9},{13,14},{14,13},{17,18},{18,... | collective-permute-start | bytes 1327112 | tf_op jit(solution)/shard_map/ppermute | solution.py:568
  17.6 9.5 %collective-permute-start.19 = (bf16[864,128]{1,0:T(8,128)(2,1)}, bf16[864,128]{1,0:T(8,128)(2,1)S(1)}, u32[]{:S(2)}, u32[]{:S(2)}) collective-permute-start(bf16[864,128]{1,0:T(8,128)(2,1)} %get-tuple-element.51.refs_0_), channel_id=1, source_target_pairs={{1,2},{2,1},{5,6},{6,5},{9,10},{10,9},{13,14},{14,13},{17,18},{18,... | collective-permute-start | bytes 663560 | tf_op jit(solution)/shard_map/ppermute | solution.py:568
  21.5 61.8 %all-to-all-start = ((bf16[8,672,128]{2,1,0:T(8,128)(2,1)}), bf16[8,672,128]{2,1,0:T(8,128)(2,1)S(1)}, u32[]{:S(2)}, u32[]{:S(2)}) async-start(bf16[8,672,128]{2,1,0:T(8,128)(2,1)} %pack.1), calls=%async_computation | async-start | bytes 2752512 | tf_op jit(solution)/shard_map/all_to_all | solution.py:555
  25.7 11.0 %collective-permute-start.22 = (bf16[864,128]{1,0:T(8,128)(2,1)}, bf16[864,128]{1,0:T(8,128)(2,1)S(1)}, u32[]{:S(2)}, u32[]{:S(2)}) collective-permute-start(bf16[864,128]{1,0:T(8,128)(2,1)} %collective-permute-done.21.refs_1_), channel_id=1, source_target_pairs={{1,2},{2,1},{5,6},{6,5},{9,10},{10,9},{13,14},{14,13},{17,18},{18,... | collective-permute-start | bytes 663560 | tf_op jit(solution)/shard_map/ppermute | solution.py:568
  27.1 21.2 %collective-permute-start.20 = (bf16[864,128]{1,0:T(8,128)(2,1)S(1)}, bf16[864,128]{1,0:T(8,128)(2,1)S(1)}, u32[]{:S(2)}, u32[]{:S(2)}) collective-permute-start(bf16[864,128]{1,0:T(8,128)(2,1)S(1)} %collective-permute-done.19.refs_0_), channel_id=1, source_target_pairs={{1,0},{2,3},{5,4},{6,7},{9,8},{10,11},{13,12},{14,15},{17,16},{18,... | collective-permute-start | bytes 663560 | tf_op jit(solution)/shard_map/ppermute | solution.py:568
  35.4 32.0 %collective-permute-start.4 = (bf16[1728,128]{1,0:T(8,128)(2,1)S(1)}, bf16[1728,128]{1,0:T(8,128)(2,1)S(1)}, u32[]{:S(2)}, u32[]{:S(2)}) collective-permute-start(bf16[1728,128]{1,0:T(8,128)(2,1)S(1)} %collective-permute-done.3.refs_0_), channel_id=1, source_target_pairs={{1,0},{2,3},{5,4},{6,7},{9,8},{10,11},{13,12},{14,15},{17,16},{18,... | collective-permute-start | bytes 1327112 | tf_op jit(solution)/shard_map/ppermute | solution.py:568
  36.7 24.6 %collective-permute-start.23 = (bf16[864,128]{1,0:T(8,128)(2,1)S(1)}, bf16[864,128]{1,0:T(8,128)(2,1)S(1)}, u32[]{:S(2)}, u32[]{:S(2)}) collective-permute-start(bf16[864,128]{1,0:T(8,128)(2,1)S(1)} %collective-permute-done.22.refs_2_), channel_id=1, source_target_pairs={{1,0},{2,3},{5,4},{6,7},{9,8},{10,11},{13,12},{14,15},{17,16},{18,... | collective-permute-start | bytes 663560 | tf_op jit(solution)/shard_map/ppermute | solution.py:568
  38.0 34.1 %collective-permute-start.2 = (bf16[1728,128]{1,0:T(8,128)(2,1)S(1)}, bf16[1728,128]{1,0:T(8,128)(2,1)S(1)}, u32[]{:S(2)}, u32[]{:S(2)}) collective-permute-start(bf16[1728,128]{1,0:T(8,128)(2,1)S(1)} %collective-permute-done.1.refs_0_), channel_id=1, source_target_pairs={{1,0},{2,3},{5,4},{6,7},{9,8},{10,11},{13,12},{14,15},{17,16},{18,... | collective-permute-start | bytes 1327112 | tf_op jit(solution)/shard_map/ppermute | solution.py:568
  67.3 11.2 %collective-permute-start.24 = (bf16[432,512]{1,0:T(8,128)(2,1)S(1)}, bf16[432,512]{1,0:T(8,128)(2,1)S(1)}, u32[]{:S(2)}, u32[]{:S(2)}) collective-permute-start(bf16[432,512]{1,0:T(8,128)(2,1)S(1)} %get-tuple-element.54), channel_id=1, source_target_pairs={{0,4},{4,0},{8,12},{12,8},{16,20},{20,16},{24,28},{28,24},{1,5},{5... | collective-permute-start | bytes 1327112 | tf_op jit(solution)/shard_map/ppermute | solution.py:574
  78.0 20.2 %collective-permute-start.5 = (bf16[864,512]{1,0:T(8,128)(2,1)}, bf16[864,512]{1,0:T(8,128)(2,1)}, u32[]{:S(2)}, u32[]{:S(2)}) collective-permute-start(bf16[864,512]{1,0:T(8,128)(2,1)} %get-tuple-element.41), channel_id=1, source_target_pairs={{0,4},{4,0},{8,12},{12,8},{16,20},{20,16},{24,28},{28,24},{1,5},{5... | collective-permute-start | bytes 2654216 | tf_op jit(solution)/shard_map/ppermute | solution.py:574
  79.9 5.8 %collective-permute-start.25 = (bf16[432,128]{1,0:T(8,128)(2,1)}, bf16[432,128]{1,0:T(8,128)(2,1)}, u32[]{:S(2)}, u32[]{:S(2)}) collective-permute-start(bf16[432,128]{1,0:T(8,128)(2,1)} %get-tuple-element.56), channel_id=1, source_target_pairs={{0,8},{4,12},{8,0},{12,4},{16,24},{20,28},{24,16},{28,20},{1,9},{5... | collective-permute-start | bytes 331784 | tf_op jit(solution)/shard_map/ppermute | solution.py:574
  81.9 7.4 %collective-permute-start.26 = (bf16[432,128]{1,0:T(8,128)(2,1)}, bf16[432,128]{1,0:T(8,128)(2,1)}, u32[]{:S(2)}, u32[]{:S(2)}) collective-permute-start(bf16[432,128]{1,0:T(8,128)(2,1)} %get-tuple-element.57), channel_id=1, source_target_pairs={{0,16},{4,20},{8,24},{12,28},{16,0},{20,4},{24,8},{28,12},{1,17},{... | collective-permute-start | bytes 331784 | tf_op jit(solution)/shard_map/ppermute | solution.py:574
  83.3 6.0 %collective-permute-start.27 = (bf16[432,128]{1,0:T(8,128)(2,1)S(1)}, bf16[432,128]{1,0:T(8,128)(2,1)}, u32[]{:S(2)}, u32[]{:S(2)}) collective-permute-start(bf16[432,128]{1,0:T(8,128)(2,1)S(1)} %get-tuple-element.58), channel_id=1, source_target_pairs={{0,24},{4,28},{8,16},{12,20},{16,8},{20,12},{24,0},{28,4},{1,25},{... | collective-permute-start | bytes 331784 | tf_op jit(solution)/shard_map/ppermute | solution.py:574
  94.0 7.8 %collective-permute-start.31 = (bf16[432,128]{1,0:T(8,128)(2,1)S(1)}, bf16[432,128]{1,0:T(8,128)(2,1)S(1)}, u32[]{:S(2)}, u32[]{:S(2)}) collective-permute-start(bf16[432,128]{1,0:T(8,128)(2,1)S(1)} %multiply_convert_fusion.1.refs_0_), channel_id=1, source_target_pairs={{0,4},{4,0},{8,12},{12,8},{16,20},{20,16},{24,28},{28,24},{1,5},{5... | collective-permute-start | bytes 331784 | tf_op jit(solution)/shard_map/ppermute | solution.py:574
  96.2 6.8 %collective-permute-start.32 = (bf16[432,128]{1,0:T(8,128)(2,1)S(1)}, bf16[432,128]{1,0:T(8,128)(2,1)S(1)}, u32[]{:S(2)}, u32[]{:S(2)}) collective-permute-start(bf16[432,128]{1,0:T(8,128)(2,1)S(1)} %collective-permute-done.28.refs_1_), channel_id=1, source_target_pairs={{0,4},{4,0},{8,12},{12,8},{16,20},{20,16},{24,28},{28,24},{1,5},{5... | collective-permute-start | bytes 331784 | tf_op jit(solution)/shard_map/ppermute | solution.py:574
  96.8 8.2 %collective-permute-start.33 = (bf16[432,128]{1,0:T(8,128)(2,1)S(1)}, bf16[432,128]{1,0:T(8,128)(2,1)}, u32[]{:S(2)}, u32[]{:S(2)}) collective-permute-start(bf16[432,128]{1,0:T(8,128)(2,1)S(1)} %collective-permute-done.29.refs_2_), channel_id=1, source_target_pairs={{0,4},{4,0},{8,12},{12,8},{16,20},{20,16},{24,28},{28,24},{1,5},{5... | collective-permute-start | bytes 331784 | tf_op jit(solution)/shard_map/ppermute | solution.py:574
  98.1 6.9 %collective-permute-start.34 = (bf16[432,128]{1,0:T(8,128)(2,1)S(1)}, bf16[432,128]{1,0:T(8,128)(2,1)}, u32[]{:S(2)}, u32[]{:S(2)}) collective-permute-start(bf16[432,128]{1,0:T(8,128)(2,1)S(1)} %collective-permute-done.30.refs_3_), channel_id=1, source_target_pairs={{0,4},{4,0},{8,12},{12,8},{16,20},{20,16},{24,28},{28,24},{1,5},{5... | collective-permute-start | bytes 331784 | tf_op jit(solution)/shard_map/ppermute | solution.py:574
  100.2 15.1 %collective-permute-start.6 = (bf16[864,128]{1,0:T(8,128)(2,1)S(1)}, bf16[864,128]{1,0:T(8,128)(2,1)S(1)}, u32[]{:S(2)}, u32[]{:S(2)}) collective-permute-start(bf16[864,128]{1,0:T(8,128)(2,1)S(1)} %get-tuple-element.43), channel_id=1, source_target_pairs={{0,8},{4,12},{8,0},{12,4},{16,24},{20,28},{24,16},{28,20},{1,9},{5... | collective-permute-start | bytes 663560 | tf_op jit(solution)/shard_map/ppermute | solution.py:574
  102.4 13.0 %collective-permute-start.7 = (bf16[864,128]{1,0:T(8,128)(2,1)S(1)}, bf16[864,128]{1,0:T(8,128)(2,1)S(1)}, u32[]{:S(2)}, u32[]{:S(2)}) collective-permute-start(bf16[864,128]{1,0:T(8,128)(2,1)S(1)} %get-tuple-element.44), channel_id=1, source_target_pairs={{0,16},{4,20},{8,24},{12,28},{16,0},{20,4},{24,8},{28,12},{1,17},{... | collective-permute-start | bytes 663560 | tf_op jit(solution)/shard_map/ppermute | solution.py:574
  103.6 11.8 %collective-permute-start.8 = (bf16[864,128]{1,0:T(8,128)(2,1)S(1)}, bf16[864,128]{1,0:T(8,128)(2,1)}, u32[]{:S(2)}, u32[]{:S(2)}) collective-permute-start(bf16[864,128]{1,0:T(8,128)(2,1)S(1)} %get-tuple-element.45), channel_id=1, source_target_pairs={{0,24},{4,28},{8,16},{12,20},{16,8},{20,12},{24,0},{28,4},{1,25},{... | collective-permute-start | bytes 663560 | tf_op jit(solution)/shard_map/ppermute | solution.py:574
  116.5 13.0 %collective-permute-start.9 = (bf16[864,128]{1,0:T(8,128)(2,1)S(1)}, bf16[864,128]{1,0:T(8,128)(2,1)S(1)}, u32[]{:S(2)}, u32[]{:S(2)}) collective-permute-start(bf16[864,128]{1,0:T(8,128)(2,1)S(1)} %multiply_convert_fusion.refs_0_), channel_id=1, source_target_pairs={{0,8},{4,12},{8,0},{12,4},{16,24},{20,28},{24,16},{28,20},{1,9},{5... | collective-permute-start | bytes 663560 | tf_op jit(solution)/shard_map/ppermute | solution.py:574
  118.1 12.0 %collective-permute-start.10 = (bf16[864,128]{1,0:T(8,128)(2,1)S(1)}, bf16[864,128]{1,0:T(8,128)(2,1)S(1)}, u32[]{:S(2)}, u32[]{:S(2)}) collective-permute-start(bf16[864,128]{1,0:T(8,128)(2,1)S(1)} %multiply_convert_fusion.refs_0_), channel_id=1, source_target_pairs={{0,16},{4,20},{8,24},{12,28},{16,0},{20,4},{24,8},{28,12},{1,17},{... | collective-permute-start | bytes 663560 | tf_op jit(solution)/shard_map/ppermute | solution.py:574
  118.6 5.9 %collective-permute-start.35 = (bf16[216,256]{1,0:T(8,128)(2,1)S(1)}, bf16[216,256]{1,0:T(8,128)(2,1)S(1)}, u32[]{:S(2)}, u32[]{:S(2)}) collective-permute-start(bf16[216,256]{1,0:T(8,128)(2,1)S(1)} %get-tuple-element.60), channel_id=1, source_target_pairs={{0,1},{1,0},{2,3},{3,2},{4,5},{5,4},{6,7},{7,6},{8,9},{9,8},{10,11... | collective-permute-start | bytes 331784 | tf_op jit(solution)/shard_map/ppermute | solution.py:630
  118.6 11.5 %collective-permute-start.11 = (bf16[864,128]{1,0:T(8,128)(2,1)S(1)}, bf16[864,128]{1,0:T(8,128)(2,1)S(1)}, u32[]{:S(2)}, u32[]{:S(2)}) collective-permute-start(bf16[864,128]{1,0:T(8,128)(2,1)S(1)} %multiply_convert_fusion.refs_0_), channel_id=1, source_target_pairs={{0,24},{4,28},{8,16},{12,20},{16,8},{20,12},{24,0},{28,4},{1,25},{... | collective-permute-start | bytes 663560 | tf_op jit(solution)/shard_map/ppermute | solution.py:574
  120.1 9.5 %collective-permute-start.36 = (bf16[216,256]{1,0:T(8,128)(2,1)S(1)}, bf16[216,256]{1,0:T(8,128)(2,1)S(1)}, u32[]{:S(2)}, u32[]{:S(2)}) collective-permute-start(bf16[216,256]{1,0:T(8,128)(2,1)S(1)} %get-tuple-element.61), channel_id=1, source_target_pairs={{0,2},{1,3},{2,0},{3,1},{4,6},{5,7},{6,4},{7,5},{8,10},{9,11},{10,... | collective-permute-start | bytes 331784 | tf_op jit(solution)/shard_map/ppermute | solution.py:630
  124.6 6.6 %collective-permute-start.37 = (bf16[216,256]{1,0:T(8,128)(2,1)S(1)}, bf16[216,256]{1,0:T(8,128)(2,1)S(1)}, u32[]{:S(2)}, u32[]{:S(2)}) collective-permute-start(bf16[216,256]{1,0:T(8,128)(2,1)S(1)} %get-tuple-element.62), channel_id=1, source_target_pairs={{0,3},{1,2},{2,1},{3,0},{4,7},{5,6},{6,5},{7,4},{8,11},{9,10},{10,... | collective-permute-start | bytes 331784 | tf_op jit(solution)/shard_map/ppermute | solution.py:630
  142.4 17.1 %collective-permute-start.16 = (bf16[432,256]{1,0:T(8,128)(2,1)S(1)}, bf16[432,256]{1,0:T(8,128)(2,1)S(1)}, u32[]{:S(2)}, u32[]{:S(2)}) collective-permute-start(bf16[432,256]{1,0:T(8,128)(2,1)S(1)} %get-tuple-element.47), channel_id=1, source_target_pairs={{0,1},{1,0},{2,3},{3,2},{4,5},{5,4},{6,7},{7,6},{8,9},{9,8},{10,11... | collective-permute-start | bytes 663560 | tf_op jit(solution)/shard_map/ppermute | solution.py:630
  143.6 18.7 %collective-permute-start.17 = (bf16[432,256]{1,0:T(8,128)(2,1)S(1)}, bf16[432,256]{1,0:T(8,128)(2,1)S(1)}, u32[]{:S(2)}, u32[]{:S(2)}) collective-permute-start(bf16[432,256]{1,0:T(8,128)(2,1)S(1)} %get-tuple-element.48), channel_id=1, source_target_pairs={{0,2},{1,3},{2,0},{3,1},{4,6},{5,7},{6,4},{7,5},{8,10},{9,11},{10,... | collective-permute-start | bytes 663560 | tf_op jit(solution)/shard_map/ppermute | solution.py:630
  144.6 17.7 %collective-permute-start.18 = (bf16[432,256]{1,0:T(8,128)(2,1)S(1)}, bf16[432,256]{1,0:T(8,128)(2,1)S(1)}, u32[]{:S(2)}, u32[]{:S(2)}) collective-permute-start(bf16[432,256]{1,0:T(8,128)(2,1)S(1)} %get-tuple-element.49), channel_id=1, source_target_pairs={{0,3},{1,2},{2,1},{3,0},{4,7},{5,6},{6,5},{7,4},{8,11},{9,10},{10,... | collective-permute-start | bytes 663560 | tf_op jit(solution)/shard_map/ppermute | solution.py:630
  (35 other events, 188.5 us)
